TPU v7x, 512 devices: a whole 4x4x16 slice. The times are simulated.
512 devices in a mesh: ctx: 32 (over y, x, core), tp: 16 (over z).
Axes of the slice: x: 4, y: 4, z: 16, core: 2. Of those that a mesh axis runs over, the one named last changes fastest.
Arguments:
- hidden: bfloat16 [16384, 4096], P('ctx', 'tp'), may hold values from -6 to 6
- norm_gain: float32 [4096], replicated, may hold values from 0.1 to 16
- query_weight: bfloat16 [4096, 4096], P('ctx', 'tp'), may hold values from -0.09375 to 0.09375
- key_weight: bfloat16 [1024, 4096], P(None, 'tp'), may hold values from -0.1875 to 0.1875
- value_weight: bfloat16 [1024, 4096], P(None, 'tp'), may hold values from -0.1875 to 0.1875
- out_weight: bfloat16 [4096, 4096], P('tp'), may hold values from -0.09375 to 0.09375
- encodings: bfloat16 [512, 128, 1024], P('ctx', 'tp'), may hold values from -70 to 70
- row_place: int32 [512], replicated, may hold values from 0 to 511, as said below
- neighbour_ids: int32 [256, 2], replicated, may hold values from 0 to 511, as said below
- neighbour_counts: int32 [256], replicated, may hold values from 1 to 2
Outputs:
- mixed: bfloat16 [16384, 4096], P(('ctx', 'tp'))
Inputs may be any that keep to these rules, and one draw needn't show every extreme that they name: `row_place`: a permutation of 0 to 511. `neighbour_ids`: the 16 neighbour slots of the spans of one ctx index name neighbours stored on exactly 16 ctx indices, one slot for each of them; a neighbour may serve several slots.
All inputs are finite; a program needn't handle non-finite values.
Results may differ from a plain program's by a relative error of at most 0.039.
The roundings to bfloat16 on the way count: a program that leaves them out, or rounds other values in their place, can miss the bound.
Values may be sent and summed in bfloat16 or wider, within the bound.
A program may use at most 128 MiB of HBM per device.

v0:
```python
import jax
import jax.numpy as jnp
from jax import lax
from jax.sharding import PartitionSpec as P

HS = 128
CH = 64
KNB = 2
LENGTH = 8192


epsilon = 1e-05
masked_score = -1e30


def shifted(block, axis, distance):
    devices = range(lax.axis_size(axis))
    route = [(i - distance, i) for i in devices if i - distance in devices]
    return lax.ppermute(block, axis, route)


def project_rows(rows, weight):
    flat = rows.reshape(-1, rows.shape[-1])
    return jnp.dot(flat, weight, preferred_element_type=jnp.float32).astype(jnp.bfloat16)


def local(
    hidden,
    norm_gain,
    query_weight,
    key_weight,
    value_weight,
    out_weight,
    encodings,
    row_place,
    neighbour_ids,
    neighbour_counts,
):
    ctx_count = lax.axis_size("ctx")
    ctx_index = lax.axis_index("ctx")
    tok_dev = hidden.shape[0]
    rows_dev = encodings.shape[0]
    slice_tokens = encodings.shape[1]
    enc_width = encodings.shape[2]
    span_dev = tok_dev // CH
    head_width = query_weight.shape[1]
    head_count = head_width // HS
    slot_cap = -(-rows_dev // ctx_count)
    whole = lax.all_gather(hidden, "tp", axis=1, tiled=True)
    values_wide = whole.astype(jnp.float32)
    mean_square = jnp.mean(values_wide * values_wide, axis=1, keepdims=True)
    normed = (values_wide * lax.rsqrt(mean_square + epsilon) * norm_gain[None, :]).astype(
        jnp.bfloat16
    )
    query_sum = jnp.dot(
        normed,
        lax.all_gather(query_weight, "ctx", axis=0, tiled=True),
        preferred_element_type=jnp.float32,
    )
    queries = (query_sum * HS ** (-0.5)).astype(jnp.bfloat16)
    storage = row_place[neighbour_ids.reshape(-1)].reshape(ctx_count, rows_dev)
    sources = storage // rows_dev
    local_rows = storage % rows_dev
    from_here = sources == ctx_index
    rank_position = jnp.cumsum(from_here.astype(jnp.int32), axis=1) - 1
    picked_rows = from_here & (rank_position == 0)
    pick_list = [jnp.sum(jnp.where(picked_rows, local_rows, 0), axis=1)]
    fill_list = [jnp.any(picked_rows, axis=1)]
    pick_index = jnp.stack(pick_list, axis=1)
    fill_mask = jnp.stack(fill_list, axis=1)
    outgoing = encodings[pick_index] * fill_mask[:, :, None, None].astype(jnp.bfloat16)
    incoming = lax.all_to_all(outgoing, "ctx", split_axis=0, concat_axis=0, tiled=True)
    own_sources = lax.dynamic_index_in_dim(sources, ctx_index, 0, keepdims=False)
    slot_order = jnp.arange(rows_dev)
    earlier = (own_sources[:, None] == own_sources[None, :]) & (
        slot_order[None, :] < slot_order[:, None]
    )
    own_rank = jnp.sum(earlier.astype(jnp.int32), axis=1)
    flat_index = own_sources * slot_cap + own_rank
    picked = incoming.reshape(ctx_count * slot_cap, slice_tokens, enc_width)[flat_index]
    row_total = picked.shape[0]
    full_rows = lax.all_gather(picked, "tp", axis=1, tiled=True)
    keys = project_rows(full_rows, key_weight).reshape(row_total, -1, head_width)
    values = project_rows(full_rows, value_weight).reshape(row_total, -1, head_width)
    neighbour_len = keys.shape[1]
    prior_keys, prior_values = shifted(
        (keys[row_total - KNB :], values[row_total - KNB :]), "ctx", 1
    )
    key_stack = jnp.concatenate([prior_keys, keys], axis=0)
    value_stack = jnp.concatenate([prior_values, values], axis=0)
    key_blocks = key_stack.reshape(span_dev + 1, KNB * neighbour_len, head_count, HS)
    value_blocks = value_stack.reshape(span_dev + 1, KNB * neighbour_len, head_count, HS)
    first_span = ctx_index * span_dev
    local_counts = lax.dynamic_slice_in_dim(neighbour_counts, first_span, span_dev)
    prior_count = lax.dynamic_slice_in_dim(neighbour_counts, jnp.maximum(first_span - 1, 0), 1)
    block_counts = jnp.concatenate([prior_count, local_counts], axis=0)
    padded = jnp.concatenate(
        [
            jnp.zeros((1, head_width), jnp.bfloat16),
            queries,
            jnp.zeros((CH - 1, head_width), jnp.bfloat16),
        ],
        axis=0,
    )
    query_blocks = padded.reshape(span_dev + 1, CH, head_count, HS)
    scores = jnp.einsum(
        "wqhd,wkhd->whqk", query_blocks, key_blocks, preferred_element_type=jnp.float32
    )
    slot_of_key = jnp.arange(KNB * neighbour_len) // neighbour_len
    live = slot_of_key[None, :] < block_counts[:, None]
    scores = jnp.where(live[:, None, None, :], scores, masked_score)
    peak = jnp.max(scores, axis=3, keepdims=True)
    expos = jnp.exp(scores - peak)
    total = jnp.sum(expos, axis=3)
    weights = expos.astype(jnp.bfloat16)
    blended = jnp.einsum(
        "whqk,wkhd->wqhd", weights, value_blocks, preferred_element_type=jnp.float32
    )
    blended = blended / jnp.swapaxes(total, 1, 2)[:, :, :, None]
    blended = blended.reshape((span_dev + 1) * CH, head_width)[1 : tok_dev + 1]
    position = ctx_index * tok_dev + jnp.arange(tok_dev)
    valid = position % LENGTH >= CH - 1
    attended = jnp.where(valid[:, None], blended, jnp.zeros_like(blended)).astype(jnp.bfloat16)
    return lax.psum_scatter(
        jnp.dot(attended, out_weight, preferred_element_type=jnp.float32).astype(jnp.bfloat16),
        "tp",
        scatter_dimension=0,
        tiled=True,
    )


def solution(mesh):
    return jax.shard_map(
        local,
        mesh=mesh,
        in_specs=(
            P("ctx", "tp"),
            P(),
            P("ctx", "tp"),
            P(None, "tp"),
            P(None, "tp"),
            P("tp", None),
            P("ctx", "tp", None),
            P(),
            P(),
            P(),
        ),
        out_specs=P(("ctx", "tp"), None),
        check_vma=False,
    )
```

profile of v0, /device:TPU:24, one launch (start us, length us, event | category | flops | bytes accessed | tf_op | source)
XLA Modules:
  0.0 356.5 jit_solution(18267812057511833881)
XLA Ops:
  8.0 0.8 copy.22
  9.0 3.6 %gather_fusion = s32[512]{0:T(512)S(1)} fusion(s32[512]{0:T(512)} %param.17, s32[1024]{0:T(1024)S(1)} %pad_clamp_fusion.2), kind=kCustom, calls=%fused_computation | custom fusion | bytes 6144 | tf_op jit(solution)/shard_map/gather | solution.py:61
  13.8 0.9 bitcast_multiply_fusion
  14.7 9.3 %all-to-all-start = ((bf16[32,1,8,1024]{3,2,1,0:T(8,128)(2,1)}), bf16[32,1,8,1024]{3,2,1,0:T(8,128)(2,1)S(1)}, u32[]{:S(2)}, u32[]{:S(2)}) async-start(bf16[32,1,8,1024]{3,2,1,0:T(8,128)(2,1)} %bitcast_multiply_fusion), calls=%async_computation | async-start | bytes 1048576 | tf_op jit(solution)/shard_map/all_to_all | solution.py:72
  24.3 9.2 %all-to-all-done = bf16[32,1,8,1024]{3,2,1,0:T(8,128)(2,1)S(1)} async-done(((bf16[32,1,8,1024]{3,2,1,0:T(8,128)(2,1)}), bf16[32,1,8,1024]{3,2,1,0:T(8,128)(2,1)S(1)}, u32[]{:S(2)}, u32[]{:S(2)}) %all-to-all-start) | async-done | bytes 524320 | tf_op jit(solution)/shard_map/all_to_all | solution.py:72
  33.5 1.3 gather_fusion.2
  36.3 73.1 %all-gather.5.cloned.1.call-done = bf16[512,4096]{1,0:T(8,128)(2,1)} async-done(((bf16[512,256]{1,0:T(8,128)(2,1)}), bf16[512,4096]{1,0:T(8,128)(2,1)}) %all-gather.5.cloned.1.call-update) | async-done | bytes 4194320 | tf_op jit(solution)/shard_map/all_gather | solution.py:49
  109.4 3.1 fusion
  112.5 54.4 %all-gather.7.cloned.1.call-done = bf16[4096,256]{1,0:T(8,128)(2,1)} async-done(((bf16[128,256]{1,0:T(8,128)(2,1)}), bf16[4096,256]{1,0:T(8,128)(2,1)}) %all-gather.7.cloned.1.call-update) | async-done | bytes 2097168 | tf_op jit(solution)/shard_map/all_gather | solution.py:57
  166.9 4.2 %fusion.11 = bf16[512,256]{1,0:T(8,128)(2,1)S(1)} fusion(bf16[4096,256]{1,0:T(8,128)(2,1)} %all-gather.7.cloned.1.call-done, bf16[512,4096]{1,0:T(8,128)(2,1)} %all-gather.5.cloned.1.call-done, f32[4096]{0:T(1024)S(1)} %copy-done.7, f32[512]{0:T(512)S(1)} %add_rsqrt_fusion), kind=kOutput, calls=%fused_computation.18 | convolution fusion | flops 1082392576 | bytes 6572032 | tf_op jit(solution)/shard_map/dot_general | solution.py:55
  171.3 0.8 reshape.186
  172.1 75.6 %all-gather.9.cloned.1.call-done = bf16[16,128,1024]{2,1,0:T(8,128)(2,1)} async-done(((bf16[16,8,1024]{2,1,0:T(8,128)(2,1)}), bf16[16,128,1024]{2,1,0:T(8,128)(2,1)}) %all-gather.9.cloned.1.call-update) | async-done | bytes 4194320 | tf_op jit(solution)/shard_map/all_gather | solution.py:82
  247.7 3.6 %convolution_convert_fusion.1 = bf16[2048,256]{1,0:T(8,128)(2,1)S(1)} fusion(bf16[2048,1024]{1,0:T(8,128)(2,1)} %bitcast.49, bf16[1024,256]{1,0:T(8,128)(2,1)S(1)} %copy-done.5), kind=kOutput, calls=%fused_computation.12 | convolution fusion | flops 1074266112 | bytes 5767168 | tf_op jit(solution)/shard_map/dot_general | solution.py:24
  251.3 1.9 collective-permute-start.1
  253.3 1.3 convolution_convert_fusion.2
  254.6 3.7 %collective-permute-start = (bf16[2,128,256]{2,1,0:T(8,128)(2,1)S(1)}, bf16[2,128,256]{2,1,0:T(8,128)(2,1)S(1)}, u32[]{:S(2)}, u32[]{:S(2)}) collective-permute-start(bf16[2,128,256]{2,1,0:T(8,128)(2,1)S(1)} %bitcast.45), channel_id=1, source_target_pairs={{0,16},{16,32},{32,48},{48,64},{64,80},{80,96},{96,112},{112,128},... | collective-permute-start | bytes 393224 | tf_op jit(solution)/shard_map/ppermute | solution.py:19
  258.2 1.5 collective-permute-done.1
  259.7 1.1 pad_maximum_fusion
  260.8 2.8 reshape.188
  263.6 2.3 pad_maximum_fusion.1
  265.9 3.5 reshape.185
  269.5 1.7 fusion.40
  272.5 3.2 convolution_convert_fusion
  275.7 74.3 %reduce-scatter.2.cloned.1.call-done = bf16[32,4096]{1,0:T(8,128)(2,1)} async-done(((bf16[512,4096]{1,0:T(8,128)(2,1)}), bf16[32,4096]{1,0:T(8,128)(2,1)}) %reduce-scatter.2.cloned.1.call-update) | async-done | bytes 262160 | tf_op jit(solution)/shard_map/reduce_scatter | solution.py:124
  (60 shorter events, 6.0 us)
Async XLA Ops:
  6.5 265.9 %copy-start = (bf16[256,4096]{1,0:T(8,128)(2,1)S(1)}, bf16[256,4096]{1,0:T(8,128)(2,1)}, u32[]{:S(2)}) copy-start(bf16[256,4096]{1,0:T(8,128)(2,1)} %param.15) | copy-start | bytes 6291460
  6.5 6.6 %copy-start.3 = (bf16[16,8,1024]{2,1,0:T(8,128)(2,1)S(1)}, bf16[16,8,1024]{2,1,0:T(8,128)(2,1)}, u32[]{:S(2)}) copy-start(bf16[16,8,1024]{2,1,0:T(8,128)(2,1)} %param.16) | copy-start | bytes 786436
  6.5 102.8 %all-gather.5.cloned.1.call-start = ((), (), s32[]{:S(2)}) async-start(), calls=%async_computation.2 | async-start | bytes 4456448 | tf_op jit(solution)/shard_map/all_gather | solution.py:49
  7.3 159.7 %all-gather.7.cloned.1.call-start = ((), (), s32[]{:S(2)}) async-start(), calls=%async_computation.3 | async-start | bytes 2162688 | tf_op jit(solution)/shard_map/all_gather | solution.py:57
  12.6 22.2 %copy-start.8 = (s32[256]{0:T(256)S(1)}, s32[256]{0:T(256)}, u32[]{:S(2)}) copy-start(s32[256]{0:T(256)} %param.19) | copy-start | bytes 3076
  14.7 18.8 %all-to-all-start = ((bf16[32,1,8,1024]{3,2,1,0:T(8,128)(2,1)}), bf16[32,1,8,1024]{3,2,1,0:T(8,128)(2,1)S(1)}, u32[]{:S(2)}, u32[]{:S(2)}) async-start(bf16[32,1,8,1024]{3,2,1,0:T(8,128)(2,1)} %bitcast_multiply_fusion), calls=%async_computation | async-start | bytes 1048576 | tf_op jit(solution)/shard_map/all_to_all | solution.py:72
  24.0 223.7 %all-gather.9.cloned.1.call-start = ((), (), s32[]{:S(2)}) async-start(), calls=%async_computation.5 | async-start | bytes 4456448 | tf_op jit(solution)/shard_map/all_gather | solution.py:82
  34.8 315.2 %reduce-scatter.2.cloned.1.call-start = ((), (), s32[]{:S(2)}) async-start(), calls=%async_computation.4 | async-start | bytes 4456448 | tf_op jit(solution)/shard_map/reduce_scatter | solution.py:124
  36.3 130.6 %copy-start.7 = (f32[4096]{0:T(1024)S(1)}, f32[4096]{0:T(1024)}, u32[]{:S(2)}) copy-start(f32[4096]{0:T(1024)} %param.11) | copy-start | bytes 49156
  112.5 135.2 %copy-start.5 = (bf16[1024,256]{1,0:T(8,128)(2,1)S(1)}, bf16[1024,256]{1,0:T(8,128)(2,1)}, u32[]{:S(2)}) copy-start(bf16[1024,256]{1,0:T(8,128)(2,1)} %param.13) | copy-start | bytes 1572868
  247.7 5.6 %copy-start.4 = (bf16[16,128,1024]{2,1,0:T(8,128)(2,1)S(1)}, bf16[16,128,1024]{2,1,0:T(8,128)(2,1)}, u32[]{:S(2)}) copy-start(bf16[16,128,1024]{2,1,0:T(8,128)(2,1)} %all-gather.9.cloned.1.call-done) | copy-start | bytes 12582916
  247.7 5.6 %copy-start.6 = (bf16[1024,256]{1,0:T(8,128)(2,1)S(1)}, bf16[1024,256]{1,0:T(8,128)(2,1)}, u32[]{:S(2)}) copy-start(bf16[1024,256]{1,0:T(8,128)(2,1)} %param.14) | copy-start | bytes 1572868
  251.3 8.4 %collective-permute-start.1 = (bf16[2,128,256]{2,1,0:T(8,128)(2,1)S(1)}, bf16[2,128,256]{2,1,0:T(8,128)(2,1)S(1)}, u32[]{:S(2)}, u32[]{:S(2)}) collective-permute-start(bf16[2,128,256]{2,1,0:T(8,128)(2,1)S(1)} %bitcast.46), channel_id=1, source_target_pairs={{0,16},{16,32},{32,48},{48,64},{64,80},{80,96},{96,112},{112,128},... | collective-permute-start | bytes 393224 | tf_op jit(solution)/shard_map/ppermute | solution.py:19
  254.5 5.2 %copy-start.1 = (bf16[2048,256]{1,0:T(8,128)(2,1)}, bf16[2048,256]{1,0:T(8,128)(2,1)S(1)}, u32[]{:S(2)}) copy-start(bf16[2048,256]{1,0:T(8,128)(2,1)S(1)} %convolution_convert_fusion.2) | copy-start | bytes 3145732
  254.6 9.0 %collective-permute-start = (bf16[2,128,256]{2,1,0:T(8,128)(2,1)S(1)}, bf16[2,128,256]{2,1,0:T(8,128)(2,1)S(1)}, u32[]{:S(2)}, u32[]{:S(2)}) collective-permute-start(bf16[2,128,256]{2,1,0:T(8,128)(2,1)S(1)} %bitcast.45), channel_id=1, source_target_pairs={{0,16},{16,32},{32,48},{48,64},{64,80},{80,96},{96,112},{112,128},... | collective-permute-start | bytes 393224 | tf_op jit(solution)/shard_map/ppermute | solution.py:19
  269.5 2.1 copy-start.2
Sparse Core Ops, SparseCore 0:
  9.4 99.9 all-gather.4
  112.5 54.3 all-gather.6
  169.0 78.6 all-gather.8
  275.8 74.1 reduce-scatter.1
where the time goes:
time: 358 us; the launch traced here: 357 us
  waiting for transfers between devices  289 us (81%)
  starting transfers between devices  15 us (4%)
  local copies, waits for them, and re-layouts  14.7 us (4%)
  matrix products  14.4 us (4%)
  between operations  13.4 us (4%)
  other arithmetic  9.53 us (3%)
    all_gather x1, waiting for transfers between devices, local(): full_rows = lax.all_gather(picked, 'tp', axis=1, tiled=True)  75.6 us
    reduce_scatter x1, waiting for transfers between devices, local(): lax.psum_scatter(jnp.dot(attended, out_weight, preferred_element_type=jnp...  74.3 us
    all_gather x1, waiting for transfers between devices, local(): whole = lax.all_gather(hidden, 'tp', axis=1, tiled=True)  73.1 us
    all_gather x1, waiting for transfers between devices, local(): lax.all_gather(query_weight, 'ctx', axis=0, tiled=True)  54.4 us
    all_to_all x1, starting transfers between devices, local(): lax.all_to_all(outgoing, 'ctx', split_axis=0, concat_axis=0, tiled=True)  9.29 us
    all_to_all x1, waiting for transfers between devices, local(): lax.all_to_all(outgoing, 'ctx', split_axis=0, concat_axis=0, tiled=True)  9.19 us
  transfers between devices with their start and end apart: 7, of which 6 were waited for; matrix products, arithmetic and copies ran while one was open for 6% of the time, Pallas kernels for 0%

commit v1 on v0

--- a/solution.py
+++ b/solution.py
@@ -17,6 +17,22 @@
     devices = range(lax.axis_size(axis))
     route = [(i - distance, i) for i in devices if i - distance in devices]
     return lax.ppermute(block, axis, route)
+
+
+def ring_gather(block, axis, dim):
+    count = lax.axis_size(axis)
+    pieces = [block]
+    right = block
+    left = block
+    for step in range(count // 2):
+        right = lax.ppermute(
+            right, axis, [(i, (i + 1) % count) for i in range(count)]
+        )
+        pieces.append(right)
+        if step < count - 1 - count // 2:
+            left = lax.ppermute(left, axis, [(i, (i - 1) % count) for i in range(count)])
+            pieces.append(left)
+    return jnp.concatenate(pieces, axis=dim)
 
 
 def project_rows(rows, weight):
@@ -52,11 +68,14 @@
     normed = (values_wide * lax.rsqrt(mean_square + epsilon) * norm_gain[None, :]).astype(
         jnp.bfloat16
     )
-    query_sum = jnp.dot(
-        normed,
-        lax.all_gather(query_weight, "ctx", axis=0, tiled=True),
-        preferred_element_type=jnp.float32,
-    )
+    query_full = lax.all_to_all(
+        jnp.broadcast_to(query_weight[None], (ctx_count,) + query_weight.shape),
+        "ctx",
+        split_axis=0,
+        concat_axis=0,
+        tiled=True,
+    ).reshape(-1, query_weight.shape[1])
+    query_sum = jnp.dot(normed, query_full, preferred_element_type=jnp.float32)
     queries = (query_sum * HS ** (-0.5)).astype(jnp.bfloat16)
     storage = row_place[neighbour_ids.reshape(-1)].reshape(ctx_count, rows_dev)
     sources = storage // rows_dev
@@ -79,7 +98,7 @@
     flat_index = own_sources * slot_cap + own_rank
     picked = incoming.reshape(ctx_count * slot_cap, slice_tokens, enc_width)[flat_index]
     row_total = picked.shape[0]
-    full_rows = lax.all_gather(picked, "tp", axis=1, tiled=True)
+    full_rows = ring_gather(picked, "tp", 1)
     keys = project_rows(full_rows, key_weight).reshape(row_total, -1, head_width)
     values = project_rows(full_rows, value_weight).reshape(row_total, -1, head_width)
     neighbour_len = keys.shape[1]

time: 358 us -> 264 us (0.74)
  waiting for transfers between devices: 289 us -> 132 us
  starting transfers between devices: 15 us -> 78 us
    all_gather x2 -> x0, waiting for transfers between devices: 130 us -> none  [the longest x1 75.6 us: local(): full_rows = lax.all_gather(picked, 'tp', axis=1, tiled=True)]
    all_gather x1, waiting for transfers between devices: 73.1 us -> 0.02 us  [local(): whole = lax.all_gather(hidden, 'tp', axis=1, tiled=True)]
    ppermute x0 -> x15, starting transfers between devices: none -> 58.2 us  [the longest x7 41.8 us: ring_gather(): lax.ppermute(left, axis, [(i, (i - 1) % count) for i in range(count)])]
    ppermute x0 -> x15, waiting for transfers between devices: none -> 43.5 us  [the longest x7 28.8 us: ring_gather(): lax.ppermute(left, axis, [(i, (i - 1) % count) for i in range(count)])]
    all_to_all x0 -> x1, starting transfers between devices: none -> 6.05 us  [local(): lax.all_to_all(jnp.broadcast_to(query_weight[None], (ctx_count,) + query_...]
  transfers between devices with their start and end apart: 7 -> 21, of which waited for: 6 -> 13; matrix products, arithmetic and copies ran while one was open for 6% -> 9% of each run, Pallas kernels for 0% -> 0%
where the time goes in v1:
time: 264 us; the launch traced here: 262 us
  waiting for transfers between devices  132 us (50%)
  starting transfers between devices  78 us (30%)
  local copies, waits for them, and re-layouts  15.6 us (6%)
  between operations  14 us (5%)
  matrix products  13.3 us (5%)
  other arithmetic  9.33 us (4%)
    reduce_scatter x1, waiting for transfers between devices, local(): lax.psum_scatter(jnp.dot(attended, out_weight, preferred_element_type=jnp...  73.8 us
    ppermute x7, starting transfers between devices, ring_gather(): lax.ppermute(left, axis, [(i, (i - 1) % count) for i in range(count)])  41.8 us
    ppermute x7, waiting for transfers between devices, ring_gather(): lax.ppermute(left, axis, [(i, (i - 1) % count) for i in range(count)])  28.8 us
    ppermute x8, starting transfers between devices, ring_gather(): lax.ppermute(right, axis, [(i, (i + 1) % count) for i in range(count)])  16.4 us
    ppermute x8, waiting for transfers between devices, ring_gather(): lax.ppermute(right, axis, [(i, (i + 1) % count) for i in range(count)])  14.6 us
    all_to_all x1, starting transfers between devices, local(): lax.all_to_all(outgoing, 'ctx', split_axis=0, concat_axis=0, tiled=True)  9.42 us
    all_to_all x1, waiting for transfers between devices, local(): lax.all_to_all(outgoing, 'ctx', split_axis=0, concat_axis=0, tiled=True)  9.24 us
    all_to_all x1, starting transfers between devices, local(): lax.all_to_all(jnp.broadcast_to(query_weight[None], (ctx_count,) + query_...  6.05 us
  transfers between devices with their start and end apart: 21, of which 13 were waited for; matrix products, arithmetic and copies ran while one was open for 9% of the time, Pallas kernels for 0%

profile of v1, /device:TPU:24, one launch (start us, length us, event | category | flops | bytes accessed | tf_op | source)
XLA Modules:
  0.0 262.0 jit_solution(14955670351550521541)
XLA Ops:
  8.3 3.6 %gather_fusion = s32[512]{0:T(512)S(1)} fusion(s32[512]{0:T(512)} %param.17, s32[1024]{0:T(1024)S(1)} %pad_clamp_fusion.2), kind=kCustom, calls=%fused_computation | custom fusion | bytes 6144 | tf_op jit(solution)/shard_map/gather | solution.py:80
  14.9 9.4 %all-to-all-start = ((bf16[32,1,8,1024]{3,2,1,0:T(8,128)(2,1)}), bf16[32,1,8,1024]{3,2,1,0:T(8,128)(2,1)S(1)}, u32[]{:S(2)}, u32[]{:S(2)}) async-start(bf16[32,1,8,1024]{3,2,1,0:T(8,128)(2,1)} %bitcast_multiply_fusion), calls=%async_computation | async-start | bytes 1048576 | tf_op jit(solution)/shard_map/all_to_all | solution.py:91
  24.5 9.2 %all-to-all-done = bf16[32,1,8,1024]{3,2,1,0:T(8,128)(2,1)S(1)} async-done(((bf16[32,1,8,1024]{3,2,1,0:T(8,128)(2,1)}), bf16[32,1,8,1024]{3,2,1,0:T(8,128)(2,1)S(1)}, u32[]{:S(2)}, u32[]{:S(2)}) %all-to-all-start) | async-done | bytes 524320 | tf_op jit(solution)/shard_map/all_to_all | solution.py:91
  36.3 9.5 %collective-permute-start.1 = (bf16[16,8,1024]{2,1,0:T(8,128)(2,1)S(1)}, bf16[16,8,1024]{2,1,0:T(8,128)(2,1)S(1)}, u32[]{:S(2)}, u32[]{:S(2)}) collective-permute-start(bf16[16,8,1024]{2,1,0:T(8,128)(2,1)S(1)} %gather_fusion.2), channel_id=1, source_target_pairs={{0,15},{1,0},{2,1},{3,2},{4,3},{5,4},{6,5},{7,6},{8,7},{9,8},{10,9... | collective-permute-start | bytes 786440 | tf_op jit(solution)/shard_map/ppermute | solution.py:33
  45.7 8.9 %collective-permute-done = bf16[16,8,1024]{2,1,0:T(8,128)(2,1)S(1)} collective-permute-done((bf16[16,8,1024]{2,1,0:T(8,128)(2,1)S(1)}, bf16[16,8,1024]{2,1,0:T(8,128)(2,1)S(1)}, u32[]{:S(2)}, u32[]{:S(2)}) %collective-permute-start) | collective-permute-done | bytes 262176 | tf_op jit(solution)/shard_map/ppermute | solution.py:28
  58.1 6.0 %all-to-all-start.1 = ((bf16[32,128,256]{2,1,0:T(8,128)(2,1)}), bf16[32,128,256]{2,1,0:T(8,128)(2,1)}, u32[]{:S(2)}, u32[]{:S(2)}) async-start(bf16[32,128,256]{2,1,0:T(8,128)(2,1)} %broadcast_in_dim.30), calls=%async_computation.1 | async-start | bytes 4194304 | tf_op jit(solution)/shard_map/all_to_all | solution.py:71
  64.9 5.1 %collective-permute-start.3 = (bf16[16,8,1024]{2,1,0:T(8,128)(2,1)S(1)}, bf16[16,8,1024]{2,1,0:T(8,128)(2,1)S(1)}, u32[]{:S(2)}, u32[]{:S(2)}) collective-permute-start(bf16[16,8,1024]{2,1,0:T(8,128)(2,1)S(1)} %collective-permute-done.1), channel_id=1, source_target_pairs={{0,15},{1,0},{2,1},{3,2},{4,3},{5,4},{6,5},{7,6},{8,7},{9,8},{10,9... | collective-permute-start | bytes 786440 | tf_op jit(solution)/shard_map/ppermute | solution.py:33
  72.8 6.4 %collective-permute-done.3 = bf16[16,8,1024]{2,1,0:T(8,128)(2,1)S(1)} collective-permute-done((bf16[16,8,1024]{2,1,0:T(8,128)(2,1)S(1)}, bf16[16,8,1024]{2,1,0:T(8,128)(2,1)S(1)}, u32[]{:S(2)}, u32[]{:S(2)}) %collective-permute-start.3) | collective-permute-done | bytes 262176 | tf_op jit(solution)/shard_map/ppermute | solution.py:33
  79.1 5.6 %collective-permute-start.5 = (bf16[16,8,1024]{2,1,0:T(8,128)(2,1)S(1)}, bf16[16,8,1024]{2,1,0:T(8,128)(2,1)S(1)}, u32[]{:S(2)}, u32[]{:S(2)}) collective-permute-start(bf16[16,8,1024]{2,1,0:T(8,128)(2,1)S(1)} %collective-permute-done.3), channel_id=1, source_target_pairs={{0,15},{1,0},{2,1},{3,2},{4,3},{5,4},{6,5},{7,6},{8,7},{9,8},{10,9... | collective-permute-start | bytes 786440 | tf_op jit(solution)/shard_map/ppermute | solution.py:33
  87.0 8.3 %collective-permute-done.5 = bf16[16,8,1024]{2,1,0:T(8,128)(2,1)S(1)} collective-permute-done((bf16[16,8,1024]{2,1,0:T(8,128)(2,1)S(1)}, bf16[16,8,1024]{2,1,0:T(8,128)(2,1)S(1)}, u32[]{:S(2)}, u32[]{:S(2)}) %collective-permute-start.5) | collective-permute-done | bytes 262176 | tf_op jit(solution)/shard_map/ppermute | solution.py:33
  95.3 5.6 %collective-permute-start.7 = (bf16[16,8,1024]{2,1,0:T(8,128)(2,1)S(1)}, bf16[16,8,1024]{2,1,0:T(8,128)(2,1)S(1)}, u32[]{:S(2)}, u32[]{:S(2)}) collective-permute-start(bf16[16,8,1024]{2,1,0:T(8,128)(2,1)S(1)} %collective-permute-done.5), channel_id=1, source_target_pairs={{0,15},{1,0},{2,1},{3,2},{4,3},{5,4},{6,5},{7,6},{8,7},{9,8},{10,9... | collective-permute-start | bytes 786440 | tf_op jit(solution)/shard_map/ppermute | solution.py:33
  102.9 6.1 %collective-permute-done.7 = bf16[16,8,1024]{2,1,0:T(8,128)(2,1)S(1)} collective-permute-done((bf16[16,8,1024]{2,1,0:T(8,128)(2,1)S(1)}, bf16[16,8,1024]{2,1,0:T(8,128)(2,1)S(1)}, u32[]{:S(2)}, u32[]{:S(2)}) %collective-permute-start.7) | collective-permute-done | bytes 262176 | tf_op jit(solution)/shard_map/ppermute | solution.py:33
  109.0 4.9 %collective-permute-start.9 = (bf16[16,8,1024]{2,1,0:T(8,128)(2,1)S(1)}, bf16[16,8,1024]{2,1,0:T(8,128)(2,1)S(1)}, u32[]{:S(2)}, u32[]{:S(2)}) collective-permute-start(bf16[16,8,1024]{2,1,0:T(8,128)(2,1)S(1)} %collective-permute-done.7), channel_id=1, source_target_pairs={{0,15},{1,0},{2,1},{3,2},{4,3},{5,4},{6,5},{7,6},{8,7},{9,8},{10,9... | collective-permute-start | bytes 786440 | tf_op jit(solution)/shard_map/ppermute | solution.py:33
  114.0 2.9 %collective-permute-start.10 = (bf16[16,8,1024]{2,1,0:T(8,128)(2,1)S(1)}, bf16[16,8,1024]{2,1,0:T(8,128)(2,1)S(1)}, u32[]{:S(2)}, u32[]{:S(2)}) collective-permute-start(bf16[16,8,1024]{2,1,0:T(8,128)(2,1)S(1)} %collective-permute-done.8), channel_id=1, source_target_pairs={{0,1},{1,2},{2,3},{3,4},{4,5},{5,6},{6,7},{7,8},{8,9},{9,10},{10,1... | collective-permute-start | bytes 786440 | tf_op jit(solution)/shard_map/ppermute | solution.py:28
  117.0 4.3 %collective-permute-done.9 = bf16[16,8,1024]{2,1,0:T(8,128)(2,1)S(1)} collective-permute-done((bf16[16,8,1024]{2,1,0:T(8,128)(2,1)S(1)}, bf16[16,8,1024]{2,1,0:T(8,128)(2,1)S(1)}, u32[]{:S(2)}, u32[]{:S(2)}) %collective-permute-start.9) | collective-permute-done | bytes 262176 | tf_op jit(solution)/shard_map/ppermute | solution.py:33
  121.3 5.6 %collective-permute-start.11 = (bf16[16,8,1024]{2,1,0:T(8,128)(2,1)S(1)}, bf16[16,8,1024]{2,1,0:T(8,128)(2,1)S(1)}, u32[]{:S(2)}, u32[]{:S(2)}) collective-permute-start(bf16[16,8,1024]{2,1,0:T(8,128)(2,1)S(1)} %collective-permute-done.9), channel_id=1, source_target_pairs={{0,15},{1,0},{2,1},{3,2},{4,3},{5,4},{6,5},{7,6},{8,7},{9,8},{10,9... | collective-permute-start | bytes 786440 | tf_op jit(solution)/shard_map/ppermute | solution.py:33
  130.8 5.6 %collective-permute-start.13 = (bf16[16,8,1024]{2,1,0:T(8,128)(2,1)S(1)}, bf16[16,8,1024]{2,1,0:T(8,128)(2,1)S(1)}, u32[]{:S(2)}, u32[]{:S(2)}) collective-permute-start(bf16[16,8,1024]{2,1,0:T(8,128)(2,1)S(1)} %collective-permute-done.11), channel_id=1, source_target_pairs={{0,15},{1,0},{2,1},{3,2},{4,3},{5,4},{6,5},{7,6},{8,7},{9,8},{10,9... | collective-permute-start | bytes 786440 | tf_op jit(solution)/shard_map/ppermute | solution.py:33
  140.3 5.6 %collective-permute-done.14 = bf16[16,8,1024]{2,1,0:T(8,128)(2,1)S(1)} collective-permute-done((bf16[16,8,1024]{2,1,0:T(8,128)(2,1)S(1)}, bf16[16,8,1024]{2,1,0:T(8,128)(2,1)S(1)}, u32[]{:S(2)}, u32[]{:S(2)}) %collective-permute-start.14) | collective-permute-done | bytes 262176 | tf_op jit(solution)/shard_map/ppermute | solution.py:28
  152.8 2.8 %collective-permute-done.15 = bf16[2,128,256]{2,1,0:T(8,128)(2,1)S(1)} collective-permute-done((bf16[2,128,256]{2,1,0:T(8,128)(2,1)S(1)}, bf16[2,128,256]{2,1,0:T(8,128)(2,1)S(1)}, u32[]{:S(2)}, u32[]{:S(2)}) %collective-permute-start.15) | collective-permute-done | bytes 131104 | tf_op jit(solution)/shard_map/ppermute | solution.py:19
  161.3 2.8 %reshape.193 = bf16[9,256,2,128]{3,2,1,0:T(2,128)(2,1)S(1)} reshape(bf16[18,128,256]{2,1,0:T(8,128)(2,1)} %pad_maximum_fusion) | data formatting | bytes 2359296 | tf_op jit(solution)/shard_map/reshape | solution.py:110
  164.1 3.1 %fusion = f32[512]{0:T(512)S(1)} fusion(bf16[512,4096]{1,0:T(8,128)(2,1)} %all-gather.2.cloned.1.call-done), kind=kLoop, calls=%fused_computation.5 | loop fusion | flops 6290944 | bytes 4196352 | tf_op jit(solution)/shard_map/reduce_sum | solution.py:67
  167.2 4.2 %fusion.11 = bf16[512,256]{1,0:T(8,128)(2,1)S(1)} fusion(bf16[4096,256]{1,0:T(8,128)(2,1)} %bitcast.12, bf16[512,4096]{1,0:T(8,128)(2,1)} %all-gather.2.cloned.1.call-done, f32[4096]{0:T(1024)S(1)} %copy-done.5, f32[512]{0:T(512)S(1)} %add_rsqrt_fusion), kind=kOutput, calls=%fused_computation.18 | convolution fusion | flops 1082392576 | bytes 6572032 | tf_op jit(solution)/shard_map/dot_general | solution.py:78
  178.2 3.3 %convolution_convert_fusion = bf16[512,4096]{1,0:T(8,128)(2,1)} fusion(bf16[256,4096]{1,0:T(8,128)(2,1)S(1)} %copy-done, bf16[576,256]{1,0:T(8,128)(2,1)S(1)} %bitcast.45, pred[512]{0:T(512)(128)(4,1)S(1)} %fusion.32), kind=kOutput, calls=%fused_computation.8 | convolution fusion | flops 1075970048 | bytes 6554112 | tf_op jit(solution)/shard_map/dot_general | solution.py:144
  181.4 73.8 %reduce-scatter.2.cloned.1.call-done = bf16[32,4096]{1,0:T(8,128)(2,1)} async-done(((bf16[512,4096]{1,0:T(8,128)(2,1)}), bf16[32,4096]{1,0:T(8,128)(2,1)}) %reduce-scatter.2.cloned.1.call-update) | async-done | bytes 262160 | tf_op jit(solution)/shard_map/reduce_scatter | solution.py:143
  (99 shorter events, 45.6 us)
Async XLA Ops:
  6.5 171.6 %copy-start = (bf16[256,4096]{1,0:T(8,128)(2,1)S(1)}, bf16[256,4096]{1,0:T(8,128)(2,1)}, u32[]{:S(2)}) copy-start(bf16[256,4096]{1,0:T(8,128)(2,1)} %param.15) | copy-start | bytes 6291460
  6.5 50.0 %copy-start.2 = (bf16[128,256]{1,0:T(8,128)(2,1)S(1)}, bf16[128,256]{1,0:T(8,128)(2,1)}, u32[]{:S(2)}) copy-start(bf16[128,256]{1,0:T(8,128)(2,1)} %param.12) | copy-start | bytes 196612
  6.5 157.5 %all-gather.2.cloned.1.call-start = ((), (), s32[]{:S(2)}) async-start(), calls=%async_computation.3 | async-start | bytes 4456448 | tf_op jit(solution)/shard_map/all_gather | solution.py:65
  14.9 18.9 %all-to-all-start = ((bf16[32,1,8,1024]{3,2,1,0:T(8,128)(2,1)}), bf16[32,1,8,1024]{3,2,1,0:T(8,128)(2,1)S(1)}, u32[]{:S(2)}, u32[]{:S(2)}) async-start(bf16[32,1,8,1024]{3,2,1,0:T(8,128)(2,1)} %bitcast_multiply_fusion), calls=%async_computation | async-start | bytes 1048576 | tf_op jit(solution)/shard_map/all_to_all | solution.py:91
  34.3 20.3 %collective-permute-start = (bf16[16,8,1024]{2,1,0:T(8,128)(2,1)S(1)}, bf16[16,8,1024]{2,1,0:T(8,128)(2,1)S(1)}, u32[]{:S(2)}, u32[]{:S(2)}) collective-permute-start(bf16[16,8,1024]{2,1,0:T(8,128)(2,1)S(1)} %gather_fusion.2), channel_id=1, source_target_pairs={{0,1},{1,2},{2,3},{3,4},{4,5},{5,6},{6,7},{7,8},{8,9},{9,10},{10,1... | collective-permute-start | bytes 786440 | tf_op jit(solution)/shard_map/ppermute | solution.py:28
  36.3 28.6 %collective-permute-start.1 = (bf16[16,8,1024]{2,1,0:T(8,128)(2,1)S(1)}, bf16[16,8,1024]{2,1,0:T(8,128)(2,1)S(1)}, u32[]{:S(2)}, u32[]{:S(2)}) collective-permute-start(bf16[16,8,1024]{2,1,0:T(8,128)(2,1)S(1)} %gather_fusion.2), channel_id=1, source_target_pairs={{0,15},{1,0},{2,1},{3,2},{4,3},{5,4},{6,5},{7,6},{8,7},{9,8},{10,9... | collective-permute-start | bytes 786440 | tf_op jit(solution)/shard_map/ppermute | solution.py:33
  54.6 16.2 %collective-permute-start.2 = (bf16[16,8,1024]{2,1,0:T(8,128)(2,1)S(1)}, bf16[16,8,1024]{2,1,0:T(8,128)(2,1)S(1)}, u32[]{:S(2)}, u32[]{:S(2)}) collective-permute-start(bf16[16,8,1024]{2,1,0:T(8,128)(2,1)S(1)} %collective-permute-done), channel_id=1, source_target_pairs={{0,1},{1,2},{2,3},{3,4},{4,5},{5,6},{6,7},{7,8},{8,9},{9,10},{10,1... | collective-permute-start | bytes 786440 | tf_op jit(solution)/shard_map/ppermute | solution.py:28
  58.1 109.0 %all-to-all-start.1 = ((bf16[32,128,256]{2,1,0:T(8,128)(2,1)}), bf16[32,128,256]{2,1,0:T(8,128)(2,1)}, u32[]{:S(2)}, u32[]{:S(2)}) async-start(bf16[32,128,256]{2,1,0:T(8,128)(2,1)} %broadcast_in_dim.30), calls=%async_computation.1 | async-start | bytes 4194304 | tf_op jit(solution)/shard_map/all_to_all | solution.py:71
  64.2 191.0 %reduce-scatter.2.cloned.1.call-start = ((), (), s32[]{:S(2)}) async-start(), calls=%async_computation.4 | async-start | bytes 4456448 | tf_op jit(solution)/shard_map/reduce_scatter | solution.py:143
  64.9 14.2 %collective-permute-start.3 = (bf16[16,8,1024]{2,1,0:T(8,128)(2,1)S(1)}, bf16[16,8,1024]{2,1,0:T(8,128)(2,1)S(1)}, u32[]{:S(2)}, u32[]{:S(2)}) collective-permute-start(bf16[16,8,1024]{2,1,0:T(8,128)(2,1)S(1)} %collective-permute-done.1), channel_id=1, source_target_pairs={{0,15},{1,0},{2,1},{3,2},{4,3},{5,4},{6,5},{7,6},{8,7},{9,8},{10,9... | collective-permute-start | bytes 786440 | tf_op jit(solution)/shard_map/ppermute | solution.py:33
  70.8 14.1 %collective-permute-start.4 = (bf16[16,8,1024]{2,1,0:T(8,128)(2,1)S(1)}, bf16[16,8,1024]{2,1,0:T(8,128)(2,1)S(1)}, u32[]{:S(2)}, u32[]{:S(2)}) collective-permute-start(bf16[16,8,1024]{2,1,0:T(8,128)(2,1)S(1)} %collective-permute-done.2), channel_id=1, source_target_pairs={{0,1},{1,2},{2,3},{3,4},{4,5},{5,6},{6,7},{7,8},{8,9},{9,10},{10,1... | collective-permute-start | bytes 786440 | tf_op jit(solution)/shard_map/ppermute | solution.py:28
  79.1 16.2 %collective-permute-start.5 = (bf16[16,8,1024]{2,1,0:T(8,128)(2,1)S(1)}, bf16[16,8,1024]{2,1,0:T(8,128)(2,1)S(1)}, u32[]{:S(2)}, u32[]{:S(2)}) collective-permute-start(bf16[16,8,1024]{2,1,0:T(8,128)(2,1)S(1)} %collective-permute-done.3), channel_id=1, source_target_pairs={{0,15},{1,0},{2,1},{3,2},{4,3},{5,4},{6,5},{7,6},{8,7},{9,8},{10,9... | collective-permute-start | bytes 786440 | tf_op jit(solution)/shard_map/ppermute | solution.py:33
  84.8 61.1 %copy-start.3 = (bf16[1024,256]{1,0:T(8,128)(2,1)S(1)}, bf16[1024,256]{1,0:T(8,128)(2,1)}, u32[]{:S(2)}) copy-start(bf16[1024,256]{1,0:T(8,128)(2,1)} %param.14) | copy-start | bytes 1572868
  84.9 16.1 %collective-permute-start.6 = (bf16[16,8,1024]{2,1,0:T(8,128)(2,1)S(1)}, bf16[16,8,1024]{2,1,0:T(8,128)(2,1)S(1)}, u32[]{:S(2)}, u32[]{:S(2)}) collective-permute-start(bf16[16,8,1024]{2,1,0:T(8,128)(2,1)S(1)} %collective-permute-done.4), channel_id=1, source_target_pairs={{0,1},{1,2},{2,3},{3,4},{4,5},{5,6},{6,7},{7,8},{8,9},{9,10},{10,1... | collective-permute-start | bytes 786440 | tf_op jit(solution)/shard_map/ppermute | solution.py:28
  95.3 13.7 %collective-permute-start.7 = (bf16[16,8,1024]{2,1,0:T(8,128)(2,1)S(1)}, bf16[16,8,1024]{2,1,0:T(8,128)(2,1)S(1)}, u32[]{:S(2)}, u32[]{:S(2)}) collective-permute-start(bf16[16,8,1024]{2,1,0:T(8,128)(2,1)S(1)} %collective-permute-done.5), channel_id=1, source_target_pairs={{0,15},{1,0},{2,1},{3,2},{4,3},{5,4},{6,5},{7,6},{8,7},{9,8},{10,9... | collective-permute-start | bytes 786440 | tf_op jit(solution)/shard_map/ppermute | solution.py:33
  100.9 13.1 %collective-permute-start.8 = (bf16[16,8,1024]{2,1,0:T(8,128)(2,1)S(1)}, bf16[16,8,1024]{2,1,0:T(8,128)(2,1)S(1)}, u32[]{:S(2)}, u32[]{:S(2)}) collective-permute-start(bf16[16,8,1024]{2,1,0:T(8,128)(2,1)S(1)} %collective-permute-done.6), channel_id=1, source_target_pairs={{0,1},{1,2},{2,3},{3,4},{4,5},{5,6},{6,7},{7,8},{8,9},{9,10},{10,1... | collective-permute-start | bytes 786440 | tf_op jit(solution)/shard_map/ppermute | solution.py:28
  109.0 12.3 %collective-permute-start.9 = (bf16[16,8,1024]{2,1,0:T(8,128)(2,1)S(1)}, bf16[16,8,1024]{2,1,0:T(8,128)(2,1)S(1)}, u32[]{:S(2)}, u32[]{:S(2)}) collective-permute-start(bf16[16,8,1024]{2,1,0:T(8,128)(2,1)S(1)} %collective-permute-done.7), channel_id=1, source_target_pairs={{0,15},{1,0},{2,1},{3,2},{4,3},{5,4},{6,5},{7,6},{8,7},{9,8},{10,9... | collective-permute-start | bytes 786440 | tf_op jit(solution)/shard_map/ppermute | solution.py:33
  114.0 12.9 %collective-permute-start.10 = (bf16[16,8,1024]{2,1,0:T(8,128)(2,1)S(1)}, bf16[16,8,1024]{2,1,0:T(8,128)(2,1)S(1)}, u32[]{:S(2)}, u32[]{:S(2)}) collective-permute-start(bf16[16,8,1024]{2,1,0:T(8,128)(2,1)S(1)} %collective-permute-done.8), channel_id=1, source_target_pairs={{0,1},{1,2},{2,3},{3,4},{4,5},{5,6},{6,7},{7,8},{8,9},{9,10},{10,1... | collective-permute-start | bytes 786440 | tf_op jit(solution)/shard_map/ppermute | solution.py:28
  121.3 9.5 %collective-permute-start.11 = (bf16[16,8,1024]{2,1,0:T(8,128)(2,1)S(1)}, bf16[16,8,1024]{2,1,0:T(8,128)(2,1)S(1)}, u32[]{:S(2)}, u32[]{:S(2)}) collective-permute-start(bf16[16,8,1024]{2,1,0:T(8,128)(2,1)S(1)} %collective-permute-done.9), channel_id=1, source_target_pairs={{0,15},{1,0},{2,1},{3,2},{4,3},{5,4},{6,5},{7,6},{8,7},{9,8},{10,9... | collective-permute-start | bytes 786440 | tf_op jit(solution)/shard_map/ppermute | solution.py:33
  126.9 9.5 %collective-permute-start.12 = (bf16[16,8,1024]{2,1,0:T(8,128)(2,1)S(1)}, bf16[16,8,1024]{2,1,0:T(8,128)(2,1)S(1)}, u32[]{:S(2)}, u32[]{:S(2)}) collective-permute-start(bf16[16,8,1024]{2,1,0:T(8,128)(2,1)S(1)} %collective-permute-done.10), channel_id=1, source_target_pairs={{0,1},{1,2},{2,3},{3,4},{4,5},{5,6},{6,7},{7,8},{8,9},{9,10},{10,1... | collective-permute-start | bytes 786440 | tf_op jit(solution)/shard_map/ppermute | solution.py:28
  130.8 9.5 %collective-permute-start.13 = (bf16[16,8,1024]{2,1,0:T(8,128)(2,1)S(1)}, bf16[16,8,1024]{2,1,0:T(8,128)(2,1)S(1)}, u32[]{:S(2)}, u32[]{:S(2)}) collective-permute-start(bf16[16,8,1024]{2,1,0:T(8,128)(2,1)S(1)} %collective-permute-done.11), channel_id=1, source_target_pairs={{0,15},{1,0},{2,1},{3,2},{4,3},{5,4},{6,5},{7,6},{8,7},{9,8},{10,9... | collective-permute-start | bytes 786440 | tf_op jit(solution)/shard_map/ppermute | solution.py:33
  136.4 9.5 %collective-permute-start.14 = (bf16[16,8,1024]{2,1,0:T(8,128)(2,1)S(1)}, bf16[16,8,1024]{2,1,0:T(8,128)(2,1)S(1)}, u32[]{:S(2)}, u32[]{:S(2)}) collective-permute-start(bf16[16,8,1024]{2,1,0:T(8,128)(2,1)S(1)} %collective-permute-done.12), channel_id=1, source_target_pairs={{0,1},{1,2},{2,3},{3,4},{4,5},{5,6},{6,7},{7,8},{8,9},{9,10},{10,1... | collective-permute-start | bytes 786440 | tf_op jit(solution)/shard_map/ppermute | solution.py:28
  147.2 8.4 %collective-permute-start.15 = (bf16[2,128,256]{2,1,0:T(8,128)(2,1)S(1)}, bf16[2,128,256]{2,1,0:T(8,128)(2,1)S(1)}, u32[]{:S(2)}, u32[]{:S(2)}) collective-permute-start(bf16[2,128,256]{2,1,0:T(8,128)(2,1)S(1)} %bitcast.47), channel_id=1, source_target_pairs={{0,16},{16,32},{32,48},{48,64},{64,80},{80,96},{96,112},{112,128},... | collective-permute-start | bytes 393224 | tf_op jit(solution)/shard_map/ppermute | solution.py:19
  150.5 8.4 %collective-permute-start.16 = (bf16[2,128,256]{2,1,0:T(8,128)(2,1)S(1)}, bf16[2,128,256]{2,1,0:T(8,128)(2,1)S(1)}, u32[]{:S(2)}, u32[]{:S(2)}) collective-permute-start(bf16[2,128,256]{2,1,0:T(8,128)(2,1)S(1)} %bitcast.46), channel_id=1, source_target_pairs={{0,16},{16,32},{32,48},{48,64},{64,80},{80,96},{96,112},{112,128},... | collective-permute-start | bytes 393224 | tf_op jit(solution)/shard_map/ppermute | solution.py:19
  (4 other events, 71.7 us)
Sparse Core Ops, SparseCore 0:
  9.4 118.3 all-gather.1
  181.6 73.5 reduce-scatter.1

commit v2 on v1

--- a/solution.py
+++ b/solution.py
@@ -19,20 +19,49 @@
     return lax.ppermute(block, axis, route)
 
 
+def ring_shift(block, axis, distance):
+    count = lax.axis_size(axis)
+    return lax.ppermute(block, axis, [(i, (i + distance) % count) for i in range(count)])
+
+
 def ring_gather(block, axis, dim):
     count = lax.axis_size(axis)
-    pieces = [block]
+    before = []
+    after = []
     right = block
     left = block
     for step in range(count // 2):
-        right = lax.ppermute(
-            right, axis, [(i, (i + 1) % count) for i in range(count)]
-        )
-        pieces.append(right)
+        right = ring_shift(right, axis, 1)
+        before.insert(0, right)
         if step < count - 1 - count // 2:
-            left = lax.ppermute(left, axis, [(i, (i - 1) % count) for i in range(count)])
-            pieces.append(left)
-    return jnp.concatenate(pieces, axis=dim)
+            left = ring_shift(left, axis, -1)
+            after.append(left)
+    return jnp.concatenate(before + [block] + after, axis=dim)
+
+
+def ring_reduce_scatter(partial, axis):
+    count = lax.axis_size(axis)
+    index = lax.axis_index(axis)
+    rows = partial.shape[0] // count
+
+    def part(offset):
+        start = ((index + offset) % count) * rows
+        return lax.dynamic_slice_in_dim(partial, start, rows).astype(jnp.float32)
+
+    reach_right = count // 2
+    reach_left = count - 1 - reach_right
+    right = part(reach_right).astype(jnp.bfloat16)
+    for step in range(1, reach_right + 1):
+        right = ring_shift(right, axis, 1)
+        if step < reach_right:
+            right = (right.astype(jnp.float32) + part(reach_right - step)).astype(jnp.bfloat16)
+    left = part(-reach_left).astype(jnp.bfloat16)
+    for step in range(1, reach_left + 1):
+        left = ring_shift(left, axis, -1)
+        if step < reach_left:
+            left = (left.astype(jnp.float32) + part(step - reach_left)).astype(jnp.bfloat16)
+    total = part(0) + right.astype(jnp.float32) + left.astype(jnp.float32)
+    return total.astype(jnp.bfloat16)
 
 
 def project_rows(rows, weight):
@@ -62,10 +91,14 @@
     head_width = query_weight.shape[1]
     head_count = head_width // HS
     slot_cap = -(-rows_dev // ctx_count)
-    whole = lax.all_gather(hidden, "tp", axis=1, tiled=True)
+    tp_count = lax.axis_size("tp")
+    tp_index = lax.axis_index("tp")
+    whole = ring_gather(hidden, "tp", 1)
+    rotation = ((tp_index - tp_count // 2) % tp_count) * hidden.shape[1]
+    gain = lax.dynamic_slice_in_dim(jnp.concatenate([norm_gain, norm_gain]), rotation, whole.shape[1])
     values_wide = whole.astype(jnp.float32)
     mean_square = jnp.mean(values_wide * values_wide, axis=1, keepdims=True)
-    normed = (values_wide * lax.rsqrt(mean_square + epsilon) * norm_gain[None, :]).astype(
+    normed = (values_wide * lax.rsqrt(mean_square + epsilon) * gain[None, :]).astype(
         jnp.bfloat16
     )
     query_full = lax.all_to_all(
@@ -75,6 +108,9 @@
         concat_axis=0,
         tiled=True,
     ).reshape(-1, query_weight.shape[1])
+    query_full = lax.dynamic_slice_in_dim(
+        jnp.concatenate([query_full, query_full]), rotation, query_full.shape[0]
+    )
     query_sum = jnp.dot(normed, query_full, preferred_element_type=jnp.float32)
     queries = (query_sum * HS ** (-0.5)).astype(jnp.bfloat16)
     storage = row_place[neighbour_ids.reshape(-1)].reshape(ctx_count, rows_dev)
@@ -140,11 +176,9 @@
     position = ctx_index * tok_dev + jnp.arange(tok_dev)
     valid = position % LENGTH >= CH - 1
     attended = jnp.where(valid[:, None], blended, jnp.zeros_like(blended)).astype(jnp.bfloat16)
-    return lax.psum_scatter(
+    return ring_reduce_scatter(
         jnp.dot(attended, out_weight, preferred_element_type=jnp.float32).astype(jnp.bfloat16),
         "tp",
-        scatter_dimension=0,
-        tiled=True,
     )
 
 

time: 264 us -> 311 us (1.18)
  starting transfers between devices: 78 us -> 183 us
  waiting for transfers between devices: 132 us -> 47.8 us
  local copies, waits for them, and re-layouts: 15.6 us -> 44.3 us
  between operations: 14 us -> 1.57 us
  other arithmetic: 9.33 us -> 17.3 us
    ppermute x15 -> x45, starting transfers between devices: 58.2 us -> 163 us  [ring_shift(): lax.ppermute(block, axis, [(i, (i + distance) % count) for i in range(cou...]
    reduce_scatter x1 -> x0, waiting for transfers between devices: 73.8 us -> none  [local(): lax.psum_scatter(jnp.dot(attended, out_weight, preferred_element_type=jnp...]
    unnamed x31 -> x74, local copies, waits for them, and re-layouts: 1.17 us -> 27.4 us
    convert_element_type x0 -> x8, other arithmetic: none -> 9.67 us  [the longest x7 7.92 us: ring_reduce_scatter(): (right.astype(jnp.float32) + part(reach_right - step)).astype(jnp.bfloat16)]
    ppermute x15 -> x45, waiting for transfers between devices: 43.5 us -> 39 us  [ring_shift(): lax.ppermute(block, axis, [(i, (i + distance) % count) for i in range(cou...]
    ppermute x2, waiting for transfers between devices: 4.65 us -> 1.47 us  [shifted(): return lax.ppermute(block, axis, route)]
  transfers between devices with their start and end apart: 21 -> 49, of which waited for: 13 -> 17; matrix products, arithmetic and copies ran while one was open for 9% -> 15% of each run, Pallas kernels for 0% -> 0%
where the time goes in v2:
time: 311 us; the launch traced here: 306 us
  starting transfers between devices  183 us (59%)
  waiting for transfers between devices  47.8 us (15%)
  local copies, waits for them, and re-layouts  44.3 us (14%)
  other arithmetic  17.3 us (6%)
  matrix products  12.1 us (4%)
    ppermute x45, starting transfers between devices, ring_shift(): lax.ppermute(block, axis, [(i, (i + distance) % count) for i in range(cou...  163 us
    ppermute x45, waiting for transfers between devices, ring_shift(): lax.ppermute(block, axis, [(i, (i + distance) % count) for i in range(cou...  39 us
    unnamed x74, local copies, waits for them, and re-layouts  27.4 us
    convert_element_type x7, other arithmetic, ring_reduce_scatter(): (right.astype(jnp.float32) + part(reach_right - step)).astype(jnp.bfloat16)  7.92 us
    all_to_all x1, starting transfers between devices, local(): lax.all_to_all(outgoing, 'ctx', split_axis=0, concat_axis=0, tiled=True)  7.48 us
    all_to_all x1, waiting for transfers between devices, local(): lax.all_to_all(outgoing, 'ctx', split_axis=0, concat_axis=0, tiled=True)  7.3 us
    all_to_all x1, starting transfers between devices, local(): lax.all_to_all(jnp.broadcast_to(query_weight[None], (ctx_count,) + query_...  7.11 us
  transfers between devices with their start and end apart: 49, of which 17 were waited for; matrix products, arithmetic and copies ran while one was open for 15% of the time, Pallas kernels for 0%

profile of v2, /device:TPU:24, one launch (start us, length us, event | category | flops | bytes accessed | tf_op | source)
XLA Modules:
  0.0 306.1 jit_solution(3679630928184992122)
XLA Ops:
  4.0 9.5 %collective-permute-start.24 = (bf16[512,256]{1,0:T(8,128)(2,1)}, bf16[512,256]{1,0:T(8,128)(2,1)S(1)}, u32[]{:S(2)}, u32[]{:S(2)}) collective-permute-start(bf16[512,256]{1,0:T(8,128)(2,1)} %param.10), channel_id=1, source_target_pairs={{0,15},{1,0},{2,1},{3,2},{4,3},{5,4},{6,5},{7,6},{8,7},{9,8},{10,9... | collective-permute-start | bytes 786440 | tf_op jit(solution)/shard_map/ppermute | solution.py:24
  21.1 7.5 %all-to-all-start = ((bf16[32,1,8,1024]{3,2,1,0:T(8,128)(2,1)}), bf16[32,1,8,1024]{3,2,1,0:T(8,128)(2,1)S(1)}, u32[]{:S(2)}, u32[]{:S(2)}) async-start(bf16[32,1,8,1024]{3,2,1,0:T(8,128)(2,1)} %bitcast_multiply_fusion), calls=%async_computation | async-start | bytes 1048576 | tf_op jit(solution)/shard_map/all_to_all | solution.py:127
  30.8 7.3 %all-to-all-done = bf16[32,1,8,1024]{3,2,1,0:T(8,128)(2,1)S(1)} async-done(((bf16[32,1,8,1024]{3,2,1,0:T(8,128)(2,1)}), bf16[32,1,8,1024]{3,2,1,0:T(8,128)(2,1)S(1)}, u32[]{:S(2)}, u32[]{:S(2)}) %all-to-all-start) | async-done | bytes 524320 | tf_op jit(solution)/shard_map/all_to_all | solution.py:127
  40.6 5.1 %collective-permute-start.8 = (bf16[16,8,1024]{2,1,0:T(8,128)(2,1)S(1)}, bf16[16,8,1024]{2,1,0:T(8,128)(2,1)S(1)}, u32[]{:S(2)}, u32[]{:S(2)}) collective-permute-start(bf16[16,8,1024]{2,1,0:T(8,128)(2,1)S(1)} %gather_fusion.2), channel_id=1, source_target_pairs={{0,15},{1,0},{2,1},{3,2},{4,3},{5,4},{6,5},{7,6},{8,7},{9,8},{10,9... | collective-permute-start | bytes 786440 | tf_op jit(solution)/shard_map/ppermute | solution.py:24
  47.7 5.1 %collective-permute-start.25 = (bf16[512,256]{1,0:T(8,128)(2,1)S(1)}, bf16[512,256]{1,0:T(8,128)(2,1)S(1)}, u32[]{:S(2)}, u32[]{:S(2)}) collective-permute-start(bf16[512,256]{1,0:T(8,128)(2,1)S(1)} %collective-permute-done.24), channel_id=1, source_target_pairs={{0,15},{1,0},{2,1},{3,2},{4,3},{5,4},{6,5},{7,6},{8,7},{9,8},{10,9... | collective-permute-start | bytes 786440 | tf_op jit(solution)/shard_map/ppermute | solution.py:24
  54.8 5.1 %collective-permute-start.9 = (bf16[16,8,1024]{2,1,0:T(8,128)(2,1)S(1)}, bf16[16,8,1024]{2,1,0:T(8,128)(2,1)S(1)}, u32[]{:S(2)}, u32[]{:S(2)}) collective-permute-start(bf16[16,8,1024]{2,1,0:T(8,128)(2,1)S(1)} %collective-permute-done.8), channel_id=1, source_target_pairs={{0,15},{1,0},{2,1},{3,2},{4,3},{5,4},{6,5},{7,6},{8,7},{9,8},{10,9... | collective-permute-start | bytes 786440 | tf_op jit(solution)/shard_map/ppermute | solution.py:24
  61.9 5.1 %collective-permute-start.26 = (bf16[512,256]{1,0:T(8,128)(2,1)S(1)}, bf16[512,256]{1,0:T(8,128)(2,1)}, u32[]{:S(2)}, u32[]{:S(2)}) collective-permute-start(bf16[512,256]{1,0:T(8,128)(2,1)S(1)} %collective-permute-done.25), channel_id=1, source_target_pairs={{0,15},{1,0},{2,1},{3,2},{4,3},{5,4},{6,5},{7,6},{8,7},{9,8},{10,9... | collective-permute-start | bytes 786440 | tf_op jit(solution)/shard_map/ppermute | solution.py:24
  69.0 5.1 %collective-permute-start.10 = (bf16[16,8,1024]{2,1,0:T(8,128)(2,1)S(1)}, bf16[16,8,1024]{2,1,0:T(8,128)(2,1)S(1)}, u32[]{:S(2)}, u32[]{:S(2)}) collective-permute-start(bf16[16,8,1024]{2,1,0:T(8,128)(2,1)S(1)} %collective-permute-done.9), channel_id=1, source_target_pairs={{0,15},{1,0},{2,1},{3,2},{4,3},{5,4},{6,5},{7,6},{8,7},{9,8},{10,9... | collective-permute-start | bytes 786440 | tf_op jit(solution)/shard_map/ppermute | solution.py:24
  76.1 5.1 %collective-permute-start.27 = (bf16[512,256]{1,0:T(8,128)(2,1)}, bf16[512,256]{1,0:T(8,128)(2,1)}, u32[]{:S(2)}, u32[]{:S(2)}) collective-permute-start(bf16[512,256]{1,0:T(8,128)(2,1)} %collective-permute-done.26), channel_id=1, source_target_pairs={{0,15},{1,0},{2,1},{3,2},{4,3},{5,4},{6,5},{7,6},{8,7},{9,8},{10,9... | collective-permute-start | bytes 786440 | tf_op jit(solution)/shard_map/ppermute | solution.py:24
  83.2 5.1 %collective-permute-start.11 = (bf16[16,8,1024]{2,1,0:T(8,128)(2,1)S(1)}, bf16[16,8,1024]{2,1,0:T(8,128)(2,1)}, u32[]{:S(2)}, u32[]{:S(2)}) collective-permute-start(bf16[16,8,1024]{2,1,0:T(8,128)(2,1)S(1)} %collective-permute-done.10), channel_id=1, source_target_pairs={{0,15},{1,0},{2,1},{3,2},{4,3},{5,4},{6,5},{7,6},{8,7},{9,8},{10,9... | collective-permute-start | bytes 786440 | tf_op jit(solution)/shard_map/ppermute | solution.py:24
  92.0 7.1 %all-to-all-start.1 = ((bf16[32,128,256]{2,1,0:T(8,128)(2,1)}), bf16[32,128,256]{2,1,0:T(8,128)(2,1)}, u32[]{:S(2)}, u32[]{:S(2)}) async-start(bf16[32,128,256]{2,1,0:T(8,128)(2,1)} %broadcast_in_dim.30), calls=%async_computation.1 | async-start | bytes 4194304 | tf_op jit(solution)/shard_map/all_to_all | solution.py:104
  99.1 5.1 %collective-permute-start.28 = (bf16[512,256]{1,0:T(8,128)(2,1)}, bf16[512,256]{1,0:T(8,128)(2,1)}, u32[]{:S(2)}, u32[]{:S(2)}) collective-permute-start(bf16[512,256]{1,0:T(8,128)(2,1)} %collective-permute-done.27), channel_id=1, source_target_pairs={{0,15},{1,0},{2,1},{3,2},{4,3},{5,4},{6,5},{7,6},{8,7},{9,8},{10,9... | collective-permute-start | bytes 786440 | tf_op jit(solution)/shard_map/ppermute | solution.py:24
  106.2 5.1 %collective-permute-start.12 = (bf16[16,8,1024]{2,1,0:T(8,128)(2,1)}, bf16[16,8,1024]{2,1,0:T(8,128)(2,1)}, u32[]{:S(2)}, u32[]{:S(2)}) collective-permute-start(bf16[16,8,1024]{2,1,0:T(8,128)(2,1)} %collective-permute-done.11), channel_id=1, source_target_pairs={{0,15},{1,0},{2,1},{3,2},{4,3},{5,4},{6,5},{7,6},{8,7},{9,8},{10,9... | collective-permute-start | bytes 786440 | tf_op jit(solution)/shard_map/ppermute | solution.py:24
  114.2 5.1 %collective-permute-start.29 = (bf16[512,256]{1,0:T(8,128)(2,1)}, bf16[512,256]{1,0:T(8,128)(2,1)}, u32[]{:S(2)}, u32[]{:S(2)}) collective-permute-start(bf16[512,256]{1,0:T(8,128)(2,1)} %collective-permute-done.28), channel_id=1, source_target_pairs={{0,15},{1,0},{2,1},{3,2},{4,3},{5,4},{6,5},{7,6},{8,7},{9,8},{10,9... | collective-permute-start | bytes 786440 | tf_op jit(solution)/shard_map/ppermute | solution.py:24
  121.3 5.1 %collective-permute-start.13 = (bf16[16,8,1024]{2,1,0:T(8,128)(2,1)}, bf16[16,8,1024]{2,1,0:T(8,128)(2,1)}, u32[]{:S(2)}, u32[]{:S(2)}) collective-permute-start(bf16[16,8,1024]{2,1,0:T(8,128)(2,1)} %collective-permute-done.12), channel_id=1, source_target_pairs={{0,15},{1,0},{2,1},{3,2},{4,3},{5,4},{6,5},{7,6},{8,7},{9,8},{10,9... | collective-permute-start | bytes 786440 | tf_op jit(solution)/shard_map/ppermute | solution.py:24
  129.3 5.1 %collective-permute-start.30 = (bf16[512,256]{1,0:T(8,128)(2,1)}, bf16[512,256]{1,0:T(8,128)(2,1)S(1)}, u32[]{:S(2)}, u32[]{:S(2)}) collective-permute-start(bf16[512,256]{1,0:T(8,128)(2,1)} %collective-permute-done.29), channel_id=1, source_target_pairs={{0,15},{1,0},{2,1},{3,2},{4,3},{5,4},{6,5},{7,6},{8,7},{9,8},{10,9... | collective-permute-start | bytes 786440 | tf_op jit(solution)/shard_map/ppermute | solution.py:24
  136.4 5.1 %collective-permute-start.14 = (bf16[16,8,1024]{2,1,0:T(8,128)(2,1)}, bf16[16,8,1024]{2,1,0:T(8,128)(2,1)}, u32[]{:S(2)}, u32[]{:S(2)}) collective-permute-start(bf16[16,8,1024]{2,1,0:T(8,128)(2,1)} %collective-permute-done.13), channel_id=1, source_target_pairs={{0,15},{1,0},{2,1},{3,2},{4,3},{5,4},{6,5},{7,6},{8,7},{9,8},{10,9... | collective-permute-start | bytes 786440 | tf_op jit(solution)/shard_map/ppermute | solution.py:24
  207.1 5.1 %collective-permute-start.40 = (bf16[32,4096]{1,0:T(8,128)(2,1)S(1)}, bf16[32,4096]{1,0:T(8,128)(2,1)S(1)}, u32[]{:S(2)}, u32[]{:S(2)}) collective-permute-start(bf16[32,4096]{1,0:T(8,128)(2,1)S(1)} %get-tuple-element.23), channel_id=1, source_target_pairs={{0,15},{1,0},{2,1},{3,2},{4,3},{5,4},{6,5},{7,6},{8,7},{9,8},{10,9... | collective-permute-start | bytes 786440 | tf_op jit(solution)/shard_map/ppermute | solution.py:24
  218.0 7.5 %collective-permute-done.33 = bf16[32,4096]{1,0:T(8,128)(2,1)S(1)} collective-permute-done((bf16[32,4096]{1,0:T(8,128)(2,1)S(1)}, bf16[32,4096]{1,0:T(8,128)(2,1)S(1)}, u32[]{:S(2)}, u32[]{:S(2)}) %collective-permute-start.33) | collective-permute-done | bytes 262176 | tf_op jit(solution)/shard_map/ppermute | solution.py:24
  228.6 5.1 %collective-permute-start.41 = (bf16[32,4096]{1,0:T(8,128)(2,1)S(1)}, bf16[32,4096]{1,0:T(8,128)(2,1)S(1)}, u32[]{:S(2)}, u32[]{:S(2)}) collective-permute-start(bf16[32,4096]{1,0:T(8,128)(2,1)S(1)} %get-tuple-element.21), channel_id=1, source_target_pairs={{0,15},{1,0},{2,1},{3,2},{4,3},{5,4},{6,5},{7,6},{8,7},{9,8},{10,9... | collective-permute-start | bytes 786440 | tf_op jit(solution)/shard_map/ppermute | solution.py:24
  240.7 5.6 %collective-permute-start.42 = (bf16[32,4096]{1,0:T(8,128)(2,1)S(1)}, bf16[32,4096]{1,0:T(8,128)(2,1)S(1)}, u32[]{:S(2)}, u32[]{:S(2)}) collective-permute-start(bf16[32,4096]{1,0:T(8,128)(2,1)S(1)} %get-tuple-element.19), channel_id=1, source_target_pairs={{0,15},{1,0},{2,1},{3,2},{4,3},{5,4},{6,5},{7,6},{8,7},{9,8},{10,9... | collective-permute-start | bytes 786440 | tf_op jit(solution)/shard_map/ppermute | solution.py:24
  253.2 5.6 %collective-permute-start.43 = (bf16[32,4096]{1,0:T(8,128)(2,1)S(1)}, bf16[32,4096]{1,0:T(8,128)(2,1)S(1)}, u32[]{:S(2)}, u32[]{:S(2)}) collective-permute-start(bf16[32,4096]{1,0:T(8,128)(2,1)S(1)} %get-tuple-element.17), channel_id=1, source_target_pairs={{0,15},{1,0},{2,1},{3,2},{4,3},{5,4},{6,5},{7,6},{8,7},{9,8},{10,9... | collective-permute-start | bytes 786440 | tf_op jit(solution)/shard_map/ppermute | solution.py:24
  266.4 5.0 %collective-permute-start.44 = (bf16[32,4096]{1,0:T(8,128)(2,1)S(1)}, bf16[32,4096]{1,0:T(8,128)(2,1)S(1)}, u32[]{:S(2)}, u32[]{:S(2)}) collective-permute-start(bf16[32,4096]{1,0:T(8,128)(2,1)S(1)} %get-tuple-element.15), channel_id=1, source_target_pairs={{0,15},{1,0},{2,1},{3,2},{4,3},{5,4},{6,5},{7,6},{8,7},{9,8},{10,9... | collective-permute-start | bytes 786440 | tf_op jit(solution)/shard_map/ppermute | solution.py:24
  290.0 5.9 %collective-permute-start.39 = (bf16[32,4096]{1,0:T(8,128)(2,1)S(1)}, bf16[32,4096]{1,0:T(8,128)(2,1)S(1)}, u32[]{:S(2)}, u32[]{:S(2)}) collective-permute-start(bf16[32,4096]{1,0:T(8,128)(2,1)S(1)} %get-tuple-element.10), channel_id=1, source_target_pairs={{0,1},{1,2},{2,3},{3,4},{4,5},{5,6},{6,7},{7,8},{8,9},{9,10},{10,1... | collective-permute-start | bytes 786440 | tf_op jit(solution)/shard_map/ppermute | solution.py:24
  (207 shorter events, 166.6 us)
Async XLA Ops:
  0.0 28.8 %collective-permute-start.16 = (bf16[512,256]{1,0:T(8,128)(2,1)}, bf16[512,256]{1,0:T(8,128)(2,1)S(1)}, u32[]{:S(2)}, u32[]{:S(2)}) collective-permute-start(bf16[512,256]{1,0:T(8,128)(2,1)} %param.10), channel_id=1, source_target_pairs={{0,1},{1,2},{2,3},{3,4},{4,5},{5,6},{6,7},{7,8},{8,9},{9,10},{10,1... | collective-permute-start | bytes 786440 | tf_op jit(solution)/shard_map/ppermute | solution.py:24
  4.0 43.7 %collective-permute-start.24 = (bf16[512,256]{1,0:T(8,128)(2,1)}, bf16[512,256]{1,0:T(8,128)(2,1)S(1)}, u32[]{:S(2)}, u32[]{:S(2)}) collective-permute-start(bf16[512,256]{1,0:T(8,128)(2,1)} %param.10), channel_id=1, source_target_pairs={{0,15},{1,0},{2,1},{3,2},{4,3},{5,4},{6,5},{7,6},{8,7},{9,8},{10,9... | collective-permute-start | bytes 786440 | tf_op jit(solution)/shard_map/ppermute | solution.py:24
  21.1 17.0 %all-to-all-start = ((bf16[32,1,8,1024]{3,2,1,0:T(8,128)(2,1)}), bf16[32,1,8,1024]{3,2,1,0:T(8,128)(2,1)S(1)}, u32[]{:S(2)}, u32[]{:S(2)}) async-start(bf16[32,1,8,1024]{3,2,1,0:T(8,128)(2,1)} %bitcast_multiply_fusion), calls=%async_computation | async-start | bytes 1048576 | tf_op jit(solution)/shard_map/all_to_all | solution.py:127
  28.8 16.9 %collective-permute-start.17 = (bf16[512,256]{1,0:T(8,128)(2,1)S(1)}, bf16[512,256]{1,0:T(8,128)(2,1)}, u32[]{:S(2)}, u32[]{:S(2)}) collective-permute-start(bf16[512,256]{1,0:T(8,128)(2,1)S(1)} %collective-permute-done.16), channel_id=1, source_target_pairs={{0,1},{1,2},{2,3},{3,4},{4,5},{5,6},{6,7},{7,8},{8,9},{9,10},{10,1... | collective-permute-start | bytes 786440 | tf_op jit(solution)/shard_map/ppermute | solution.py:24
  54.8 14.2 %collective-permute-start.9 = (bf16[16,8,1024]{2,1,0:T(8,128)(2,1)S(1)}, bf16[16,8,1024]{2,1,0:T(8,128)(2,1)S(1)}, u32[]{:S(2)}, u32[]{:S(2)}) collective-permute-start(bf16[16,8,1024]{2,1,0:T(8,128)(2,1)S(1)} %collective-permute-done.8), channel_id=1, source_target_pairs={{0,15},{1,0},{2,1},{3,2},{4,3},{5,4},{6,5},{7,6},{8,7},{9,8},{10,9... | collective-permute-start | bytes 786440 | tf_op jit(solution)/shard_map/ppermute | solution.py:24
  59.9 14.2 %collective-permute-start.19 = (bf16[512,256]{1,0:T(8,128)(2,1)S(1)}, bf16[512,256]{1,0:T(8,128)(2,1)S(1)}, u32[]{:S(2)}, u32[]{:S(2)}) collective-permute-start(bf16[512,256]{1,0:T(8,128)(2,1)S(1)} %collective-permute-done.18), channel_id=1, source_target_pairs={{0,1},{1,2},{2,3},{3,4},{4,5},{5,6},{6,7},{7,8},{8,9},{9,10},{10,1... | collective-permute-start | bytes 786440 | tf_op jit(solution)/shard_map/ppermute | solution.py:24
  61.9 14.2 %collective-permute-start.26 = (bf16[512,256]{1,0:T(8,128)(2,1)S(1)}, bf16[512,256]{1,0:T(8,128)(2,1)}, u32[]{:S(2)}, u32[]{:S(2)}) collective-permute-start(bf16[512,256]{1,0:T(8,128)(2,1)S(1)} %collective-permute-done.25), channel_id=1, source_target_pairs={{0,15},{1,0},{2,1},{3,2},{4,3},{5,4},{6,5},{7,6},{8,7},{9,8},{10,9... | collective-permute-start | bytes 786440 | tf_op jit(solution)/shard_map/ppermute | solution.py:24
  67.0 14.2 %collective-permute-start.2 = (bf16[16,8,1024]{2,1,0:T(8,128)(2,1)S(1)}, bf16[16,8,1024]{2,1,0:T(8,128)(2,1)}, u32[]{:S(2)}, u32[]{:S(2)}) collective-permute-start(bf16[16,8,1024]{2,1,0:T(8,128)(2,1)S(1)} %collective-permute-done.1), channel_id=1, source_target_pairs={{0,1},{1,2},{2,3},{3,4},{4,5},{5,6},{6,7},{7,8},{8,9},{9,10},{10,1... | collective-permute-start | bytes 786440 | tf_op jit(solution)/shard_map/ppermute | solution.py:24
  76.1 23.0 %collective-permute-start.27 = (bf16[512,256]{1,0:T(8,128)(2,1)}, bf16[512,256]{1,0:T(8,128)(2,1)}, u32[]{:S(2)}, u32[]{:S(2)}) collective-permute-start(bf16[512,256]{1,0:T(8,128)(2,1)} %collective-permute-done.26), channel_id=1, source_target_pairs={{0,15},{1,0},{2,1},{3,2},{4,3},{5,4},{6,5},{7,6},{8,7},{9,8},{10,9... | collective-permute-start | bytes 786440 | tf_op jit(solution)/shard_map/ppermute | solution.py:24
  81.3 23.0 %collective-permute-start.3 = (bf16[16,8,1024]{2,1,0:T(8,128)(2,1)}, bf16[16,8,1024]{2,1,0:T(8,128)(2,1)}, u32[]{:S(2)}, u32[]{:S(2)}) collective-permute-start(bf16[16,8,1024]{2,1,0:T(8,128)(2,1)} %collective-permute-done.2), channel_id=1, source_target_pairs={{0,1},{1,2},{2,3},{3,4},{4,5},{5,6},{6,7},{7,8},{8,9},{9,10},{10,1... | collective-permute-start | bytes 786440 | tf_op jit(solution)/shard_map/ppermute | solution.py:24
  83.2 23.0 %collective-permute-start.11 = (bf16[16,8,1024]{2,1,0:T(8,128)(2,1)S(1)}, bf16[16,8,1024]{2,1,0:T(8,128)(2,1)}, u32[]{:S(2)}, u32[]{:S(2)}) collective-permute-start(bf16[16,8,1024]{2,1,0:T(8,128)(2,1)S(1)} %collective-permute-done.10), channel_id=1, source_target_pairs={{0,15},{1,0},{2,1},{3,2},{4,3},{5,4},{6,5},{7,6},{8,7},{9,8},{10,9... | collective-permute-start | bytes 786440 | tf_op jit(solution)/shard_map/ppermute | solution.py:24
  88.4 22.9 %collective-permute-start.21 = (bf16[512,256]{1,0:T(8,128)(2,1)}, bf16[512,256]{1,0:T(8,128)(2,1)}, u32[]{:S(2)}, u32[]{:S(2)}) collective-permute-start(bf16[512,256]{1,0:T(8,128)(2,1)} %collective-permute-done.20), channel_id=1, source_target_pairs={{0,1},{1,2},{2,3},{3,4},{4,5},{5,6},{6,7},{7,8},{8,9},{9,10},{10,1... | collective-permute-start | bytes 786440 | tf_op jit(solution)/shard_map/ppermute | solution.py:24
  92.0 65.4 %all-to-all-start.1 = ((bf16[32,128,256]{2,1,0:T(8,128)(2,1)}), bf16[32,128,256]{2,1,0:T(8,128)(2,1)}, u32[]{:S(2)}, u32[]{:S(2)}) async-start(bf16[32,128,256]{2,1,0:T(8,128)(2,1)} %broadcast_in_dim.30), calls=%async_computation.1 | async-start | bytes 4194304 | tf_op jit(solution)/shard_map/all_to_all | solution.py:104
  99.1 15.1 %collective-permute-start.28 = (bf16[512,256]{1,0:T(8,128)(2,1)}, bf16[512,256]{1,0:T(8,128)(2,1)}, u32[]{:S(2)}, u32[]{:S(2)}) collective-permute-start(bf16[512,256]{1,0:T(8,128)(2,1)} %collective-permute-done.27), channel_id=1, source_target_pairs={{0,15},{1,0},{2,1},{3,2},{4,3},{5,4},{6,5},{7,6},{8,7},{9,8},{10,9... | collective-permute-start | bytes 786440 | tf_op jit(solution)/shard_map/ppermute | solution.py:24
  104.3 15.1 %collective-permute-start.4 = (bf16[16,8,1024]{2,1,0:T(8,128)(2,1)}, bf16[16,8,1024]{2,1,0:T(8,128)(2,1)}, u32[]{:S(2)}, u32[]{:S(2)}) collective-permute-start(bf16[16,8,1024]{2,1,0:T(8,128)(2,1)} %collective-permute-done.3), channel_id=1, source_target_pairs={{0,1},{1,2},{2,3},{3,4},{4,5},{5,6},{6,7},{7,8},{8,9},{9,10},{10,1... | collective-permute-start | bytes 786440 | tf_op jit(solution)/shard_map/ppermute | solution.py:24
  106.2 15.1 %collective-permute-start.12 = (bf16[16,8,1024]{2,1,0:T(8,128)(2,1)}, bf16[16,8,1024]{2,1,0:T(8,128)(2,1)}, u32[]{:S(2)}, u32[]{:S(2)}) collective-permute-start(bf16[16,8,1024]{2,1,0:T(8,128)(2,1)} %collective-permute-done.11), channel_id=1, source_target_pairs={{0,15},{1,0},{2,1},{3,2},{4,3},{5,4},{6,5},{7,6},{8,7},{9,8},{10,9... | collective-permute-start | bytes 786440 | tf_op jit(solution)/shard_map/ppermute | solution.py:24
  111.3 15.1 %collective-permute-start.22 = (bf16[512,256]{1,0:T(8,128)(2,1)}, bf16[512,256]{1,0:T(8,128)(2,1)}, u32[]{:S(2)}, u32[]{:S(2)}) collective-permute-start(bf16[512,256]{1,0:T(8,128)(2,1)} %collective-permute-done.21), channel_id=1, source_target_pairs={{0,1},{1,2},{2,3},{3,4},{4,5},{5,6},{6,7},{7,8},{8,9},{9,10},{10,1... | collective-permute-start | bytes 786440 | tf_op jit(solution)/shard_map/ppermute | solution.py:24
  114.2 15.1 %collective-permute-start.29 = (bf16[512,256]{1,0:T(8,128)(2,1)}, bf16[512,256]{1,0:T(8,128)(2,1)}, u32[]{:S(2)}, u32[]{:S(2)}) collective-permute-start(bf16[512,256]{1,0:T(8,128)(2,1)} %collective-permute-done.28), channel_id=1, source_target_pairs={{0,15},{1,0},{2,1},{3,2},{4,3},{5,4},{6,5},{7,6},{8,7},{9,8},{10,9... | collective-permute-start | bytes 786440 | tf_op jit(solution)/shard_map/ppermute | solution.py:24
  119.3 15.1 %collective-permute-start.5 = (bf16[16,8,1024]{2,1,0:T(8,128)(2,1)}, bf16[16,8,1024]{2,1,0:T(8,128)(2,1)}, u32[]{:S(2)}, u32[]{:S(2)}) collective-permute-start(bf16[16,8,1024]{2,1,0:T(8,128)(2,1)} %collective-permute-done.4), channel_id=1, source_target_pairs={{0,1},{1,2},{2,3},{3,4},{4,5},{5,6},{6,7},{7,8},{8,9},{9,10},{10,1... | collective-permute-start | bytes 786440 | tf_op jit(solution)/shard_map/ppermute | solution.py:24
  121.3 15.1 %collective-permute-start.13 = (bf16[16,8,1024]{2,1,0:T(8,128)(2,1)}, bf16[16,8,1024]{2,1,0:T(8,128)(2,1)}, u32[]{:S(2)}, u32[]{:S(2)}) collective-permute-start(bf16[16,8,1024]{2,1,0:T(8,128)(2,1)} %collective-permute-done.12), channel_id=1, source_target_pairs={{0,15},{1,0},{2,1},{3,2},{4,3},{5,4},{6,5},{7,6},{8,7},{9,8},{10,9... | collective-permute-start | bytes 786440 | tf_op jit(solution)/shard_map/ppermute | solution.py:24
  126.4 15.1 %collective-permute-start.23 = (bf16[512,256]{1,0:T(8,128)(2,1)}, bf16[512,256]{1,0:T(8,128)(2,1)}, u32[]{:S(2)}, u32[]{:S(2)}) collective-permute-start(bf16[512,256]{1,0:T(8,128)(2,1)} %collective-permute-done.22), channel_id=1, source_target_pairs={{0,1},{1,2},{2,3},{3,4},{4,5},{5,6},{6,7},{7,8},{8,9},{9,10},{10,1... | collective-permute-start | bytes 786440 | tf_op jit(solution)/shard_map/ppermute | solution.py:24
  129.3 23.2 %collective-permute-start.30 = (bf16[512,256]{1,0:T(8,128)(2,1)}, bf16[512,256]{1,0:T(8,128)(2,1)S(1)}, u32[]{:S(2)}, u32[]{:S(2)}) collective-permute-start(bf16[512,256]{1,0:T(8,128)(2,1)} %collective-permute-done.29), channel_id=1, source_target_pairs={{0,15},{1,0},{2,1},{3,2},{4,3},{5,4},{6,5},{7,6},{8,7},{9,8},{10,9... | collective-permute-start | bytes 786440 | tf_op jit(solution)/shard_map/ppermute | solution.py:24
  134.4 21.0 %collective-permute-start.6 = (bf16[16,8,1024]{2,1,0:T(8,128)(2,1)}, bf16[16,8,1024]{2,1,0:T(8,128)(2,1)}, u32[]{:S(2)}, u32[]{:S(2)}) collective-permute-start(bf16[16,8,1024]{2,1,0:T(8,128)(2,1)} %collective-permute-done.5), channel_id=1, source_target_pairs={{0,1},{1,2},{2,3},{3,4},{4,5},{5,6},{6,7},{7,8},{8,9},{9,10},{10,1... | collective-permute-start | bytes 786440 | tf_op jit(solution)/shard_map/ppermute | solution.py:24
  136.4 40.7 %collective-permute-start.14 = (bf16[16,8,1024]{2,1,0:T(8,128)(2,1)}, bf16[16,8,1024]{2,1,0:T(8,128)(2,1)}, u32[]{:S(2)}, u32[]{:S(2)}) collective-permute-start(bf16[16,8,1024]{2,1,0:T(8,128)(2,1)} %collective-permute-done.13), channel_id=1, source_target_pairs={{0,15},{1,0},{2,1},{3,2},{4,3},{5,4},{6,5},{7,6},{8,7},{9,8},{10,9... | collective-permute-start | bytes 786440 | tf_op jit(solution)/shard_map/ppermute | solution.py:24
  (46 other events, 1046.3 us)

commit v3 on v2

--- a/solution.py
+++ b/solution.py
@@ -1,6 +1,10 @@
+import functools
+
 import jax
 import jax.numpy as jnp
 from jax import lax
+from jax.experimental import pallas as pl
+from jax.experimental.pallas import tpu as pltpu
 from jax.sharding import PartitionSpec as P
 
 HS = 128
@@ -37,6 +41,63 @@
             left = ring_shift(left, axis, -1)
             after.append(left)
     return jnp.concatenate(before + [block] + after, axis=dim)
+
+
+def ring_gather_kernel(x_ref, o_ref, send_sem, recv_sem, *, count, axis, other):
+    me = lax.axis_index(axis)
+    row = lax.axis_index(other)
+    right = lax.rem(me + 1, count)
+    left = lax.rem(me + count - 1, count)
+    half = count // 2
+    mesh_ids = pl.DeviceIdType.MESH
+    barrier = pltpu.get_barrier_semaphore()
+    for neighbour in (left, right):
+        pl.semaphore_signal(barrier, inc=1, device_id=(row, neighbour), device_id_type=mesh_ids)
+    pl.semaphore_wait(barrier, 2)
+    o_ref[half] = x_ref[...]
+    for step in range(1, half + 1):
+        copies = []
+        slot = half - step
+        copies.append(
+            pltpu.make_async_remote_copy(
+                src_ref=x_ref if step == 1 else o_ref.at[slot + 1],
+                dst_ref=o_ref.at[slot],
+                send_sem=send_sem.at[slot],
+                recv_sem=recv_sem.at[slot],
+                device_id=(row, right),
+                device_id_type=mesh_ids,
+            )
+        )
+        if step < count - half:
+            slot = half + step
+            copies.append(
+                pltpu.make_async_remote_copy(
+                    src_ref=x_ref if step == 1 else o_ref.at[slot - 1],
+                    dst_ref=o_ref.at[slot],
+                    send_sem=send_sem.at[slot],
+                    recv_sem=recv_sem.at[slot],
+                    device_id=(row, left),
+                    device_id_type=mesh_ids,
+                )
+            )
+        for copy in copies:
+            copy.start()
+        for copy in copies:
+            copy.wait_recv()
+        for copy in copies:
+            copy.wait_send()
+
+
+def kernel_gather(block, axis, other, collective_id):
+    count = lax.axis_size(axis)
+    return pl.pallas_call(
+        functools.partial(ring_gather_kernel, count=count, axis=axis, other=other),
+        out_shape=jax.ShapeDtypeStruct((count,) + block.shape, block.dtype),
+        in_specs=[pl.BlockSpec(memory_space=pltpu.VMEM)],
+        out_specs=pl.BlockSpec(memory_space=pltpu.VMEM),
+        scratch_shapes=[pltpu.SemaphoreType.DMA((count,)), pltpu.SemaphoreType.DMA((count,))],
+        compiler_params=pltpu.CompilerParams(collective_id=collective_id, has_side_effects=True),
+    )(block)
 
 
 def ring_reduce_scatter(partial, axis):
@@ -93,7 +154,7 @@
     slot_cap = -(-rows_dev // ctx_count)
     tp_count = lax.axis_size("tp")
     tp_index = lax.axis_index("tp")
-    whole = ring_gather(hidden, "tp", 1)
+    whole = jnp.swapaxes(kernel_gather(hidden, "tp", "ctx", 0), 0, 1).reshape(hidden.shape[0], -1)
     rotation = ((tp_index - tp_count // 2) % tp_count) * hidden.shape[1]
     gain = lax.dynamic_slice_in_dim(jnp.concatenate([norm_gain, norm_gain]), rotation, whole.shape[1])
     values_wide = whole.astype(jnp.float32)
@@ -134,7 +195,9 @@
     flat_index = own_sources * slot_cap + own_rank
     picked = incoming.reshape(ctx_count * slot_cap, slice_tokens, enc_width)[flat_index]
     row_total = picked.shape[0]
-    full_rows = ring_gather(picked, "tp", 1)
+    full_rows = jnp.swapaxes(kernel_gather(picked, "tp", "ctx", 1), 0, 1).reshape(
+        picked.shape[0], -1, picked.shape[2]
+    )
     keys = project_rows(full_rows, key_weight).reshape(row_total, -1, head_width)
     values = project_rows(full_rows, value_weight).reshape(row_total, -1, head_width)
     neighbour_len = keys.shape[1]
@@ -176,9 +239,11 @@
     position = ctx_index * tok_dev + jnp.arange(tok_dev)
     valid = position % LENGTH >= CH - 1
     attended = jnp.where(valid[:, None], blended, jnp.zeros_like(blended)).astype(jnp.bfloat16)
-    return ring_reduce_scatter(
+    return lax.psum_scatter(
         jnp.dot(attended, out_weight, preferred_element_type=jnp.float32).astype(jnp.bfloat16),
         "tp",
+        scatter_dimension=0,
+        tiled=True,
     )
 
 

time: 311 us -> 305 us (0.981); the launches traced: 306 us -> 304 us
  starting transfers between devices: 183 us -> 23.6 us
  Pallas kernels: 0 us -> 129 us
  waiting for transfers between devices: 47.8 us -> 76.3 us
  local copies, waits for them, and re-layouts: 44.3 us -> 29.4 us
  between operations: 1.57 us -> 13.8 us
    ppermute x45 -> x0, starting transfers between devices: 163 us -> none  [ring_shift(): lax.ppermute(block, axis, [(i, (i + distance) % count) for i in range(cou...]
    pallas_call x0 -> x2, Pallas kernels: none -> 129 us  [kernel_gather(): pl.pallas_call(functools.partial(ring_gather_kernel, count=count, axis=ax...]
    reduce_scatter x0 -> x1, waiting for transfers between devices: none -> 76.1 us  [local(): lax.psum_scatter(jnp.dot(attended, out_weight, preferred_element_type=jnp...]
    ppermute x45 -> x0, waiting for transfers between devices: 39 us -> none  [ring_shift(): lax.ppermute(block, axis, [(i, (i + distance) % count) for i in range(cou...]
    unnamed x74 -> x22, local copies, waits for them, and re-layouts: 27.4 us -> 1.06 us
    convert_element_type x0 -> x1, local copies, waits for them, and re-layouts: none -> 9.31 us  [local(): values_wide = whole.astype(jnp.float32)]
    all_to_all x1, waiting for transfers between devices: 7.3 us -> 0.01 us  [local(): lax.all_to_all(outgoing, 'ctx', split_axis=0, concat_axis=0, tiled=True)]
    convert_element_type x8 -> x2, other arithmetic: 9.67 us -> 11.7 us  [the longest x1 6.46 us: local(): values_wide = whole.astype(jnp.float32)]
  transfers between devices with their start and end apart: 49 -> 5, of which waited for: 17 -> 2; matrix products, arithmetic and copies ran while one was open for 15% -> 13% of each run, Pallas kernels for 0% -> 42%
where the time goes in v3:
time: 305 us; the launch traced here: 304 us
  Pallas kernels  129 us (42%)
  waiting for transfers between devices  76.3 us (25%)
  local copies, waits for them, and re-layouts  29.4 us (10%)
  starting transfers between devices  23.6 us (8%)
  other arithmetic  19.9 us (7%)
  between operations  13.8 us (5%)
  matrix products  12.1 us (4%)
    pallas_call x2, Pallas kernels, kernel_gather(): pl.pallas_call(functools.partial(ring_gather_kernel, count=count, axis=ax...  129 us
    reduce_scatter x1, waiting for transfers between devices, local(): lax.psum_scatter(jnp.dot(attended, out_weight, preferred_element_type=jnp...  76.1 us
    convert_element_type x1, local copies, waits for them, and re-layouts, local(): values_wide = whole.astype(jnp.float32)  9.31 us
    all_to_all x1, starting transfers between devices, local(): lax.all_to_all(outgoing, 'ctx', split_axis=0, concat_axis=0, tiled=True)  9.29 us
    all_to_all x1, starting transfers between devices, local(): lax.all_to_all(jnp.broadcast_to(query_weight[None], (ctx_count,) + query_...  7.44 us
    ppermute x2, starting transfers between devices, shifted(): return lax.ppermute(block, axis, route)  6.79 us
    convert_element_type x1, other arithmetic, local(): values_wide = whole.astype(jnp.float32)  6.46 us
  transfers between devices with their start and end apart: 5, of which 2 were waited for; matrix products, arithmetic and copies ran while one was open for 13% of the time, Pallas kernels for 42%

profile of v3, /device:TPU:24, one launch (start us, length us, event | category | flops | bytes accessed | tf_op | source)
XLA Modules:
  0.0 304.2 jit_solution(11799494521751662203)
XLA Ops:
  7.7 3.6 %gather_fusion = s32[512]{0:T(512)S(1)} fusion(s32[512]{0:T(512)} %param.17, s32[1024]{0:T(1024)S(1)} %pad_clamp_fusion.2), kind=kCustom, calls=%fused_computation | custom fusion | bytes 6144 | tf_op jit(solution)/shard_map/gather | solution.py:177
  13.4 9.3 %all-to-all-start = ((bf16[32,1,8,1024]{3,2,1,0:T(8,128)(2,1)}), bf16[32,1,8,1024]{3,2,1,0:T(8,128)(2,1)S(1)}, u32[]{:S(2)}, u32[]{:S(2)}) async-start(bf16[32,1,8,1024]{3,2,1,0:T(8,128)(2,1)} %bitcast_multiply_fusion.1), calls=%async_computation | async-start | bytes 1048576 | tf_op jit(solution)/shard_map/all_to_all | solution.py:188
  22.7 68.1 %shard_map.101 = bf16[16,512,256]{2,1,0:T(8,128)(2,1)} custom-call(bf16[512,256]{1,0:T(8,128)(2,1)} %x_ref.1), custom_call_target="tpu_custom_call" | custom-call | tf_op jit(solution)/shard_map/pallas_call | solution.py:93
  90.8 6.5 %convert_bitcast_fusion = f32[512,16,256]{2,0,1:T(8,128)} fusion(bf16[16,512,256]{2,1,0:T(8,128)(2,1)} %shard_map.101), kind=kLoop, calls=%fused_computation.4 | loop fusion | flops 2097152 | bytes 12582912 | tf_op jit(solution)/shard_map/convert_element_type | solution.py:160
  98.2 9.3 %copy.28 = f32[512,16,256]{0,2,1:T(8,128)} copy(f32[512,16,256]{2,0,1:T(8,128)} %convert_bitcast_fusion) | data formatting | bytes 16777216 | tf_op jit(solution)/shard_map/convert_element_type | solution.py:160
  109.4 1.6 broadcast_in_dim.30
  111.0 7.4 %all-to-all-start.1 = ((bf16[32,128,256]{2,1,0:T(8,128)(2,1)}), bf16[32,128,256]{2,1,0:T(8,128)(2,1)}, u32[]{:S(2)}, u32[]{:S(2)}) async-start(bf16[32,128,256]{2,1,0:T(8,128)(2,1)} %broadcast_in_dim.30), calls=%async_computation.1 | async-start | bytes 4194304 | tf_op jit(solution)/shard_map/all_to_all | solution.py:165
  118.5 5.2 %fusion.2 = bf16[512,4096]{0,1:T(8,128)(2,1)} fusion(f32[512,16,256]{0,2,1:T(8,128)} %copy.28, f32[4096]{0:T(1024)S(1)} %fusion.26, f32[512]{0:T(512)S(1)} %add_rsqrt_fusion), kind=kLoop, calls=%fused_computation.8 | loop fusion | flops 6291456 | bytes 12601344 | tf_op jit(solution)/shard_map/convert_element_type | solution.py:162
  123.7 1.3 gather_fusion.2
  124.9 61.1 %shard_map.100 = bf16[16,16,8,1024]{3,2,1,0:T(8,128)(2,1)} custom-call(bf16[16,8,1024]{2,1,0:T(8,128)(2,1)} %gather_fusion.2), custom_call_target="tpu_custom_call" | custom-call | tf_op jit(solution)/shard_map/pallas_call | solution.py:93
  186.0 2.7 copy.27
  188.7 1.3 convolution_convert_fusion.1
  190.0 1.9 collective-permute-start.1
  192.0 1.3 convolution_convert_fusion.2
  193.3 4.9 %collective-permute-start = (bf16[2,128,256]{2,1,0:T(8,128)(2,1)S(1)}, bf16[2,128,256]{2,1,0:T(8,128)(2,1)S(1)}, u32[]{:S(2)}, u32[]{:S(2)}) collective-permute-start(bf16[2,128,256]{2,1,0:T(8,128)(2,1)S(1)} %bitcast.58), channel_id=1, source_target_pairs={{0,16},{16,32},{32,48},{48,64},{64,80},{80,96},{96,112},{112,128},... | collective-permute-start | bytes 393224 | tf_op jit(solution)/shard_map/ppermute | solution.py:23
  198.4 1.1 pad_maximum_fusion
  199.6 2.8 reshape.191
  202.3 2.4 pad_maximum_fusion.1
  204.7 3.5 %reshape.187 = bf16[9,256,2,128]{3,2,1,0:T(2,128)(2,1)} reshape(bf16[18,128,256]{2,1,0:T(8,128)(2,1)} %pad_maximum_fusion.1) | data formatting | bytes 2359296 | tf_op jit(solution)/shard_map/reshape | solution.py:210
  208.2 4.2 %fusion.10 = bf16[512,256]{1,0:T(8,128)(2,1)S(1)} fusion(bf16[512,4096]{0,1:T(8,128)(2,1)} %fusion.2, s32[]{:T(128)S(6)} %select_n.104, bf16[4096,256]{1,0:T(8,128)(2,1)} %bitcast.15), kind=kOutput, calls=%fused_computation.20 | convolution fusion | flops 1078198272 | bytes 6553604 | tf_op jit(solution)/shard_map/dot_general | solution.py:175
  213.4 1.7 reshape.189
  215.1 1.7 fusion.42
  218.1 3.2 %convolution_convert_fusion = bf16[512,4096]{1,0:T(8,128)(2,1)} fusion(bf16[256,4096]{1,0:T(8,128)(2,1)S(1)} %copy-done, bf16[576,256]{1,0:T(8,128)(2,1)S(1)} %bitcast.57, pred[512]{0:T(512)(128)(4,1)S(1)} %fusion.32), kind=kOutput, calls=%fused_computation.9 | convolution fusion | flops 1075970048 | bytes 6554112 | tf_op jit(solution)/shard_map/dot_general | solution.py:243
  221.3 76.1 %reduce-scatter.2.cloned.1.call-done = bf16[32,4096]{1,0:T(8,128)(2,1)} async-done(((bf16[512,4096]{1,0:T(8,128)(2,1)}), bf16[32,4096]{1,0:T(8,128)(2,1)}) %reduce-scatter.2.cloned.1.call-update) | async-done | bytes 262160 | tf_op jit(solution)/shard_map/reduce_scatter | solution.py:242
  (63 shorter events, 8.5 us)
Async XLA Ops:
  6.5 211.5 %copy-start = (bf16[256,4096]{1,0:T(8,128)(2,1)S(1)}, bf16[256,4096]{1,0:T(8,128)(2,1)}, u32[]{:S(2)}) copy-start(bf16[256,4096]{1,0:T(8,128)(2,1)} %param.15) | copy-start | bytes 6291460
  6.5 5.3 %copy-start.4 = (bf16[16,8,1024]{2,1,0:T(8,128)(2,1)S(1)}, bf16[16,8,1024]{2,1,0:T(8,128)(2,1)}, u32[]{:S(2)}) copy-start(bf16[16,8,1024]{2,1,0:T(8,128)(2,1)} %param.16) | copy-start | bytes 786436
  13.4 96.0 %all-to-all-start = ((bf16[32,1,8,1024]{3,2,1,0:T(8,128)(2,1)}), bf16[32,1,8,1024]{3,2,1,0:T(8,128)(2,1)S(1)}, u32[]{:S(2)}, u32[]{:S(2)}) async-start(bf16[32,1,8,1024]{3,2,1,0:T(8,128)(2,1)} %bitcast_multiply_fusion.1), calls=%async_computation | async-start | bytes 1048576 | tf_op jit(solution)/shard_map/all_to_all | solution.py:188
  90.8 6.5 %copy-start.1 = (bf16[16,512,256]{2,1,0:T(8,128)(2,1)S(1)}, bf16[16,512,256]{2,1,0:T(8,128)(2,1)}, u32[]{:S(2)}) copy-start(bf16[16,512,256]{2,1,0:T(8,128)(2,1)} %shard_map.101) | copy-start | bytes 12582916
  98.1 9.7 %copy-start.9 = (s32[256]{0:T(256)S(1)}, s32[256]{0:T(256)}, u32[]{:S(2)}) copy-start(s32[256]{0:T(256)} %param.19) | copy-start | bytes 3076
  98.2 10.3 %copy-start.6 = (f32[4096]{0:T(1024)S(1)}, f32[4096]{0:T(1024)}, u32[]{:S(2)}) copy-start(f32[4096]{0:T(1024)} %param.11) | copy-start | bytes 49156
  98.2 11.2 %copy-start.5 = (bf16[128,256]{1,0:T(8,128)(2,1)S(1)}, bf16[128,256]{1,0:T(8,128)(2,1)}, u32[]{:S(2)}) copy-start(bf16[128,256]{1,0:T(8,128)(2,1)} %param.12) | copy-start | bytes 196612
  111.0 97.3 %all-to-all-start.1 = ((bf16[32,128,256]{2,1,0:T(8,128)(2,1)}), bf16[32,128,256]{2,1,0:T(8,128)(2,1)}, u32[]{:S(2)}, u32[]{:S(2)}) async-start(bf16[32,128,256]{2,1,0:T(8,128)(2,1)} %broadcast_in_dim.30), calls=%async_computation.1 | async-start | bytes 4194304 | tf_op jit(solution)/shard_map/all_to_all | solution.py:165
  118.4 179.0 %reduce-scatter.2.cloned.1.call-start = ((), (), s32[]{:S(2)}) async-start(), calls=%async_computation.3 | async-start | bytes 4456448 | tf_op jit(solution)/shard_map/reduce_scatter | solution.py:242
  186.0 2.7 copy-start.7
  188.7 3.2 %copy-start.8 = (bf16[1024,256]{1,0:T(8,128)(2,1)S(1)}, bf16[1024,256]{1,0:T(8,128)(2,1)}, u32[]{:S(2)}) copy-start(bf16[1024,256]{1,0:T(8,128)(2,1)} %param.14) | copy-start | bytes 1572868
  190.0 8.4 %collective-permute-start.1 = (bf16[2,128,256]{2,1,0:T(8,128)(2,1)S(1)}, bf16[2,128,256]{2,1,0:T(8,128)(2,1)S(1)}, u32[]{:S(2)}, u32[]{:S(2)}) collective-permute-start(bf16[2,128,256]{2,1,0:T(8,128)(2,1)S(1)} %bitcast.59), channel_id=1, source_target_pairs={{0,16},{16,32},{32,48},{48,64},{64,80},{80,96},{96,112},{112,128},... | collective-permute-start | bytes 393224 | tf_op jit(solution)/shard_map/ppermute | solution.py:23
  193.3 5.2 %copy-start.2 = (bf16[2048,256]{1,0:T(8,128)(2,1)}, bf16[2048,256]{1,0:T(8,128)(2,1)S(1)}, u32[]{:S(2)}) copy-start(bf16[2048,256]{1,0:T(8,128)(2,1)S(1)} %convolution_convert_fusion.2) | copy-start | bytes 3145732
  193.3 9.0 %collective-permute-start = (bf16[2,128,256]{2,1,0:T(8,128)(2,1)S(1)}, bf16[2,128,256]{2,1,0:T(8,128)(2,1)S(1)}, u32[]{:S(2)}, u32[]{:S(2)}) collective-permute-start(bf16[2,128,256]{2,1,0:T(8,128)(2,1)S(1)} %bitcast.58), channel_id=1, source_target_pairs={{0,16},{16,32},{32,48},{48,64},{64,80},{80,96},{96,112},{112,128},... | collective-permute-start | bytes 393224 | tf_op jit(solution)/shard_map/ppermute | solution.py:23
  215.1 2.1 copy-start.3
Sparse Core Ops, SparseCore 0:
  221.4 75.8 reduce-scatter.1

commit v4 on v3

--- a/solution.py
+++ b/solution.py
@@ -21,26 +21,6 @@
     devices = range(lax.axis_size(axis))
     route = [(i - distance, i) for i in devices if i - distance in devices]
     return lax.ppermute(block, axis, route)
-
-
-def ring_shift(block, axis, distance):
-    count = lax.axis_size(axis)
-    return lax.ppermute(block, axis, [(i, (i + distance) % count) for i in range(count)])
-
-
-def ring_gather(block, axis, dim):
-    count = lax.axis_size(axis)
-    before = []
-    after = []
-    right = block
-    left = block
-    for step in range(count // 2):
-        right = ring_shift(right, axis, 1)
-        before.insert(0, right)
-        if step < count - 1 - count // 2:
-            left = ring_shift(left, axis, -1)
-            after.append(left)
-    return jnp.concatenate(before + [block] + after, axis=dim)
 
 
 def ring_gather_kernel(x_ref, o_ref, send_sem, recv_sem, *, count, axis, other):
@@ -100,31 +80,6 @@
     )(block)
 
 
-def ring_reduce_scatter(partial, axis):
-    count = lax.axis_size(axis)
-    index = lax.axis_index(axis)
-    rows = partial.shape[0] // count
-
-    def part(offset):
-        start = ((index + offset) % count) * rows
-        return lax.dynamic_slice_in_dim(partial, start, rows).astype(jnp.float32)
-
-    reach_right = count // 2
-    reach_left = count - 1 - reach_right
-    right = part(reach_right).astype(jnp.bfloat16)
-    for step in range(1, reach_right + 1):
-        right = ring_shift(right, axis, 1)
-        if step < reach_right:
-            right = (right.astype(jnp.float32) + part(reach_right - step)).astype(jnp.bfloat16)
-    left = part(-reach_left).astype(jnp.bfloat16)
-    for step in range(1, reach_left + 1):
-        left = ring_shift(left, axis, -1)
-        if step < reach_left:
-            left = (left.astype(jnp.float32) + part(step - reach_left)).astype(jnp.bfloat16)
-    total = part(0) + right.astype(jnp.float32) + left.astype(jnp.float32)
-    return total.astype(jnp.bfloat16)
-
-
 def project_rows(rows, weight):
     flat = rows.reshape(-1, rows.shape[-1])
     return jnp.dot(flat, weight, preferred_element_type=jnp.float32).astype(jnp.bfloat16)
@@ -152,14 +107,10 @@
     head_width = query_weight.shape[1]
     head_count = head_width // HS
     slot_cap = -(-rows_dev // ctx_count)
-    tp_count = lax.axis_size("tp")
-    tp_index = lax.axis_index("tp")
-    whole = jnp.swapaxes(kernel_gather(hidden, "tp", "ctx", 0), 0, 1).reshape(hidden.shape[0], -1)
-    rotation = ((tp_index - tp_count // 2) % tp_count) * hidden.shape[1]
-    gain = lax.dynamic_slice_in_dim(jnp.concatenate([norm_gain, norm_gain]), rotation, whole.shape[1])
+    whole = lax.all_gather(hidden, "tp", axis=1, tiled=True)
     values_wide = whole.astype(jnp.float32)
     mean_square = jnp.mean(values_wide * values_wide, axis=1, keepdims=True)
-    normed = (values_wide * lax.rsqrt(mean_square + epsilon) * gain[None, :]).astype(
+    normed = (values_wide * lax.rsqrt(mean_square + epsilon) * norm_gain[None, :]).astype(
         jnp.bfloat16
     )
     query_full = lax.all_to_all(
@@ -169,9 +120,6 @@
         concat_axis=0,
         tiled=True,
     ).reshape(-1, query_weight.shape[1])
-    query_full = lax.dynamic_slice_in_dim(
-        jnp.concatenate([query_full, query_full]), rotation, query_full.shape[0]
-    )
     query_sum = jnp.dot(normed, query_full, preferred_element_type=jnp.float32)
     queries = (query_sum * HS ** (-0.5)).astype(jnp.bfloat16)
     storage = row_place[neighbour_ids.reshape(-1)].reshape(ctx_count, rows_dev)
@@ -195,7 +143,7 @@
     flat_index = own_sources * slot_cap + own_rank
     picked = incoming.reshape(ctx_count * slot_cap, slice_tokens, enc_width)[flat_index]
     row_total = picked.shape[0]
-    full_rows = jnp.swapaxes(kernel_gather(picked, "tp", "ctx", 1), 0, 1).reshape(
+    full_rows = jnp.swapaxes(kernel_gather(picked, "tp", "ctx", 0), 0, 1).reshape(
         picked.shape[0], -1, picked.shape[2]
     )
     keys = project_rows(full_rows, key_weight).reshape(row_total, -1, head_width)

time: 305 us -> 257 us (0.84)
  Pallas kernels: 129 us -> 93.9 us
  other arithmetic: 19.9 us -> 10.3 us
  local copies, waits for them, and re-layouts: 29.4 us -> 19.9 us
  waiting for transfers between devices: 76.3 us -> 84.5 us
    pallas_call x2 -> x1, Pallas kernels: 129 us -> 93.9 us  [kernel_gather(): pl.pallas_call(functools.partial(ring_gather_kernel, count=count, axis=ax...]
    convert_element_type x2 -> x0, other arithmetic: 11.7 us -> none  [the longest x1 6.46 us: local(): values_wide = whole.astype(jnp.float32)]
    convert_element_type x1 -> x0, local copies, waits for them, and re-layouts: 9.31 us -> none  [local(): values_wide = whole.astype(jnp.float32)]
    all_to_all x1, waiting for transfers between devices: 0.01 us -> 8.55 us  [local(): lax.all_to_all(outgoing, 'ctx', split_axis=0, concat_axis=0, tiled=True)]
  transfers between devices with their start and end apart: 5 -> 6, of which waited for: 2 -> 3; matrix products, arithmetic and copies ran while one was open for 13% -> 11% of each run, Pallas kernels for 42% -> 37%
where the time goes in v4:
time: 257 us; the launch traced here: 256 us
  Pallas kernels  93.9 us (37%)
  waiting for transfers between devices  84.5 us (33%)
  starting transfers between devices  21.6 us (8%)
  local copies, waits for them, and re-layouts  19.9 us (8%)
  between operations  13.7 us (5%)
  matrix products  12.1 us (5%)
  other arithmetic  10.3 us (4%)
    pallas_call x1, Pallas kernels, kernel_gather(): pl.pallas_call(functools.partial(ring_gather_kernel, count=count, axis=ax...  93.9 us
    reduce_scatter x1, waiting for transfers between devices, local(): lax.psum_scatter(jnp.dot(attended, out_weight, preferred_element_type=jnp...  73.5 us
    all_to_all x1, starting transfers between devices, local(): lax.all_to_all(outgoing, 'ctx', split_axis=0, concat_axis=0, tiled=True)  9.29 us
    all_to_all x1, waiting for transfers between devices, local(): lax.all_to_all(outgoing, 'ctx', split_axis=0, concat_axis=0, tiled=True)  8.55 us
    all_to_all x1, starting transfers between devices, local(): lax.all_to_all(jnp.broadcast_to(query_weight[None], (ctx_count,) + query_...  7 us
    ppermute x2, starting transfers between devices, shifted(): return lax.ppermute(block, axis, route)  5.3 us
  transfers between devices with their start and end apart: 6, of which 3 were waited for; matrix products, arithmetic and copies ran while one was open for 11% of the time, Pallas kernels for 37%

profile of v4, /device:TPU:24, one launch (start us, length us, event | category | flops | bytes accessed | tf_op | source)
XLA Modules:
  0.0 256.2 jit_solution(17683911218123796583)
XLA Ops:
  8.3 3.6 %gather_fusion = s32[512]{0:T(512)S(1)} fusion(s32[512]{0:T(512)} %param.17, s32[1024]{0:T(1024)S(1)} %pad_clamp_fusion.2), kind=kCustom, calls=%fused_computation | custom fusion | bytes 6144 | tf_op jit(solution)/shard_map/gather | solution.py:125
  13.9 9.3 %all-to-all-start = ((bf16[32,1,8,1024]{3,2,1,0:T(8,128)(2,1)}), bf16[32,1,8,1024]{3,2,1,0:T(8,128)(2,1)S(1)}, u32[]{:S(2)}, u32[]{:S(2)}) async-start(bf16[32,1,8,1024]{3,2,1,0:T(8,128)(2,1)} %bitcast_multiply_fusion), calls=%async_computation | async-start | bytes 1048576 | tf_op jit(solution)/shard_map/all_to_all | solution.py:136
  24.2 8.6 %all-to-all-done = bf16[32,1,8,1024]{3,2,1,0:T(8,128)(2,1)S(1)} async-done(((bf16[32,1,8,1024]{3,2,1,0:T(8,128)(2,1)}), bf16[32,1,8,1024]{3,2,1,0:T(8,128)(2,1)S(1)}, u32[]{:S(2)}, u32[]{:S(2)}) %all-to-all-start) | async-done | bytes 524320 | tf_op jit(solution)/shard_map/all_to_all | solution.py:136
  32.7 1.5 broadcast_in_dim.30
  34.3 7.0 %all-to-all-start.1 = ((bf16[32,128,256]{2,1,0:T(8,128)(2,1)}), bf16[32,128,256]{2,1,0:T(8,128)(2,1)}, u32[]{:S(2)}, u32[]{:S(2)}) async-start(bf16[32,128,256]{2,1,0:T(8,128)(2,1)} %broadcast_in_dim.30), calls=%async_computation.1 | async-start | bytes 4194304 | tf_op jit(solution)/shard_map/all_to_all | solution.py:116
  42.2 1.3 gather_fusion.2
  43.5 93.9 %shard_map.100 = bf16[16,16,8,1024]{3,2,1,0:T(8,128)(2,1)} custom-call(bf16[16,8,1024]{2,1,0:T(8,128)(2,1)} %gather_fusion.2), custom_call_target="tpu_custom_call" | custom-call | tf_op jit(solution)/shard_map/pallas_call | solution.py:73
  137.4 2.7 %copy.25 = bf16[16,16,8,1024]{3,2,1,0:T(8,128)(2,1)S(1)} copy(bf16[16,16,8,1024]{3,2,0,1:T(8,128)(2,1)} %bitcast.42) | data formatting | bytes 8388608 | tf_op jit(solution)/shard_map/transpose | solution.py:146
  140.1 1.3 convolution_convert_fusion.1
  141.4 1.9 collective-permute-start.1
  143.3 1.3 convolution_convert_fusion.2
  144.6 3.4 %collective-permute-start = (bf16[2,128,256]{2,1,0:T(8,128)(2,1)S(1)}, bf16[2,128,256]{2,1,0:T(8,128)(2,1)S(1)}, u32[]{:S(2)}, u32[]{:S(2)}) collective-permute-start(bf16[2,128,256]{2,1,0:T(8,128)(2,1)S(1)} %bitcast.50), channel_id=1, source_target_pairs={{0,16},{16,32},{32,48},{48,64},{64,80},{80,96},{96,112},{112,128},... | collective-permute-start | bytes 393224 | tf_op jit(solution)/shard_map/ppermute | solution.py:23
  148.0 1.7 collective-permute-done.1
  149.8 1.1 pad_maximum_fusion
  150.9 2.8 %reshape.188 = bf16[9,256,2,128]{3,2,1,0:T(2,128)(2,1)S(1)} reshape(bf16[18,128,256]{2,1,0:T(8,128)(2,1)} %pad_maximum_fusion) | data formatting | bytes 2359296 | tf_op jit(solution)/shard_map/reshape | solution.py:157
  153.7 2.4 pad_maximum_fusion.1
  156.1 3.5 %reshape.184 = bf16[9,256,2,128]{3,2,1,0:T(2,128)(2,1)} reshape(bf16[18,128,256]{2,1,0:T(8,128)(2,1)} %pad_maximum_fusion.1) | data formatting | bytes 2359296 | tf_op jit(solution)/shard_map/reshape | solution.py:158
  159.6 3.1 %fusion = f32[512]{0:T(512)S(1)} fusion(bf16[512,4096]{1,0:T(8,128)(2,1)} %all-gather.2.cloned.1.call-done), kind=kLoop, calls=%fused_computation.5 | loop fusion | flops 6290944 | bytes 4196352 | tf_op jit(solution)/shard_map/reduce_sum | solution.py:112
  162.7 4.2 %fusion.11 = bf16[512,256]{1,0:T(8,128)(2,1)S(1)} fusion(bf16[4096,256]{1,0:T(8,128)(2,1)} %bitcast.13, bf16[512,4096]{1,0:T(8,128)(2,1)} %all-gather.2.cloned.1.call-done, f32[4096]{0:T(1024)S(1)} %copy-done.7, f32[512]{0:T(512)S(1)} %add_rsqrt_fusion), kind=kOutput, calls=%fused_computation.18 | convolution fusion | flops 1082392576 | bytes 6572032 | tf_op jit(solution)/shard_map/dot_general | solution.py:123
  166.9 0.9 maximum_maximum_fusion
  167.8 1.7 reshape.186
  169.6 1.7 fusion.40
  172.5 3.2 %convolution_convert_fusion = bf16[512,4096]{1,0:T(8,128)(2,1)} fusion(bf16[256,4096]{1,0:T(8,128)(2,1)S(1)} %copy-done, bf16[576,256]{1,0:T(8,128)(2,1)S(1)} %bitcast.49, pred[512]{0:T(512)(128)(4,1)S(1)} %fusion.32), kind=kOutput, calls=%fused_computation.8 | convolution fusion | flops 1075970048 | bytes 6554112 | tf_op jit(solution)/shard_map/dot_general | solution.py:191
  175.8 73.5 %reduce-scatter.2.cloned.1.call-done = bf16[32,4096]{1,0:T(8,128)(2,1)} async-done(((bf16[512,4096]{1,0:T(8,128)(2,1)}), bf16[32,4096]{1,0:T(8,128)(2,1)}) %reduce-scatter.2.cloned.1.call-update) | async-done | bytes 262160 | tf_op jit(solution)/shard_map/reduce_scatter | solution.py:190
  (59 shorter events, 6.8 us)
Async XLA Ops:
  6.5 166.0 %copy-start = (bf16[256,4096]{1,0:T(8,128)(2,1)S(1)}, bf16[256,4096]{1,0:T(8,128)(2,1)}, u32[]{:S(2)}) copy-start(bf16[256,4096]{1,0:T(8,128)(2,1)} %param.15) | copy-start | bytes 6291460
  6.5 5.9 %copy-start.3 = (bf16[16,8,1024]{2,1,0:T(8,128)(2,1)S(1)}, bf16[16,8,1024]{2,1,0:T(8,128)(2,1)}, u32[]{:S(2)}) copy-start(bf16[16,8,1024]{2,1,0:T(8,128)(2,1)} %param.16) | copy-start | bytes 786436
  6.5 153.1 %all-gather.2.cloned.1.call-start = ((), (), s32[]{:S(2)}) async-start(), calls=%async_computation.3 | async-start | bytes 4456448 | tf_op jit(solution)/shard_map/all_gather | solution.py:110
  11.9 11.4 %copy-start.8 = (s32[256]{0:T(256)S(1)}, s32[256]{0:T(256)}, u32[]{:S(2)}) copy-start(s32[256]{0:T(256)} %param.19) | copy-start | bytes 3076
  11.9 20.8 %copy-start.4 = (bf16[128,256]{1,0:T(8,128)(2,1)S(1)}, bf16[128,256]{1,0:T(8,128)(2,1)}, u32[]{:S(2)}) copy-start(bf16[128,256]{1,0:T(8,128)(2,1)} %param.12) | copy-start | bytes 196612
  13.9 18.8 %all-to-all-start = ((bf16[32,1,8,1024]{3,2,1,0:T(8,128)(2,1)}), bf16[32,1,8,1024]{3,2,1,0:T(8,128)(2,1)S(1)}, u32[]{:S(2)}, u32[]{:S(2)}) async-start(bf16[32,1,8,1024]{3,2,1,0:T(8,128)(2,1)} %bitcast_multiply_fusion), calls=%async_computation | async-start | bytes 1048576 | tf_op jit(solution)/shard_map/all_to_all | solution.py:136
  34.3 128.4 %all-to-all-start.1 = ((bf16[32,128,256]{2,1,0:T(8,128)(2,1)}), bf16[32,128,256]{2,1,0:T(8,128)(2,1)}, u32[]{:S(2)}, u32[]{:S(2)}) async-start(bf16[32,128,256]{2,1,0:T(8,128)(2,1)} %broadcast_in_dim.30), calls=%async_computation.1 | async-start | bytes 4194304 | tf_op jit(solution)/shard_map/all_to_all | solution.py:116
  41.3 208.1 %reduce-scatter.2.cloned.1.call-start = ((), (), s32[]{:S(2)}) async-start(), calls=%async_computation.4 | async-start | bytes 4456448 | tf_op jit(solution)/shard_map/reduce_scatter | solution.py:190
  137.4 2.7 %copy-start.5 = (bf16[1024,256]{1,0:T(8,128)(2,1)S(1)}, bf16[1024,256]{1,0:T(8,128)(2,1)}, u32[]{:S(2)}) copy-start(bf16[1024,256]{1,0:T(8,128)(2,1)} %param.13) | copy-start | bytes 1572868
  140.1 3.2 %copy-start.6 = (bf16[1024,256]{1,0:T(8,128)(2,1)S(1)}, bf16[1024,256]{1,0:T(8,128)(2,1)}, u32[]{:S(2)}) copy-start(bf16[1024,256]{1,0:T(8,128)(2,1)} %param.14) | copy-start | bytes 1572868
  141.4 8.4 %collective-permute-start.1 = (bf16[2,128,256]{2,1,0:T(8,128)(2,1)S(1)}, bf16[2,128,256]{2,1,0:T(8,128)(2,1)S(1)}, u32[]{:S(2)}, u32[]{:S(2)}) collective-permute-start(bf16[2,128,256]{2,1,0:T(8,128)(2,1)S(1)} %bitcast.51), channel_id=1, source_target_pairs={{0,16},{16,32},{32,48},{48,64},{64,80},{80,96},{96,112},{112,128},... | collective-permute-start | bytes 393224 | tf_op jit(solution)/shard_map/ppermute | solution.py:23
  144.6 5.2 %copy-start.1 = (bf16[2048,256]{1,0:T(8,128)(2,1)}, bf16[2048,256]{1,0:T(8,128)(2,1)S(1)}, u32[]{:S(2)}) copy-start(bf16[2048,256]{1,0:T(8,128)(2,1)S(1)} %convolution_convert_fusion.2) | copy-start | bytes 3145732
  144.6 9.0 %collective-permute-start = (bf16[2,128,256]{2,1,0:T(8,128)(2,1)S(1)}, bf16[2,128,256]{2,1,0:T(8,128)(2,1)S(1)}, u32[]{:S(2)}, u32[]{:S(2)}) collective-permute-start(bf16[2,128,256]{2,1,0:T(8,128)(2,1)S(1)} %bitcast.50), channel_id=1, source_target_pairs={{0,16},{16,32},{32,48},{48,64},{64,80},{80,96},{96,112},{112,128},... | collective-permute-start | bytes 393224 | tf_op jit(solution)/shard_map/ppermute | solution.py:23
  159.6 3.1 %copy-start.7 = (f32[4096]{0:T(1024)S(1)}, f32[4096]{0:T(1024)}, u32[]{:S(2)}) copy-start(f32[4096]{0:T(1024)} %param.11) | copy-start | bytes 49156
  169.6 2.1 copy-start.2
Sparse Core Ops, SparseCore 0:
  9.4 119.7 all-gather.1
  175.9 73.3 reduce-scatter.1

commit v5 on v4

--- a/solution.py
+++ b/solution.py
@@ -80,6 +80,91 @@
     )(block)
 
 
+def ring_sum_kernel(
+    p_ref, o_ref, right_in, right_out, left_in, left_out, sems, *, count, axis, other
+):
+    me = lax.axis_index(axis)
+    row = lax.axis_index(other)
+    right = lax.rem(me + 1, count)
+    left = lax.rem(me + count - 1, count)
+    reach_right = count // 2
+    reach_left = count - 1 - reach_right
+    mesh_ids = pl.DeviceIdType.MESH
+    barrier = pltpu.get_barrier_semaphore()
+    for neighbour in (left, right):
+        pl.semaphore_signal(barrier, inc=1, device_id=(row, neighbour), device_id_type=mesh_ids)
+    pl.semaphore_wait(barrier, 2)
+
+    def own(offset):
+        return p_ref[lax.rem(me + offset + 2 * count, count)].astype(jnp.float32)
+
+    for step in range(1, reach_right + 1):
+        copies = [
+            pltpu.make_async_remote_copy(
+                src_ref=p_ref.at[lax.rem(me + reach_right, count)]
+                if step == 1
+                else right_out.at[step - 2],
+                dst_ref=right_in.at[step - 1],
+                send_sem=sems.at[0, step - 1],
+                recv_sem=sems.at[1, step - 1],
+                device_id=(row, right),
+                device_id_type=mesh_ids,
+            )
+        ]
+        if step <= reach_left:
+            copies.append(
+                pltpu.make_async_remote_copy(
+                    src_ref=p_ref.at[lax.rem(me + count - reach_left, count)]
+                    if step == 1
+                    else left_out.at[step - 2],
+                    dst_ref=left_in.at[step - 1],
+                    send_sem=sems.at[2, step - 1],
+                    recv_sem=sems.at[3, step - 1],
+                    device_id=(row, left),
+                    device_id_type=mesh_ids,
+                )
+            )
+        for copy in copies:
+            copy.start()
+        for copy in copies:
+            copy.wait_recv()
+        for copy in copies:
+            copy.wait_send()
+        if step < reach_right:
+            right_out[step - 1] = (
+                right_in[step - 1].astype(jnp.float32) + own(reach_right - step)
+            ).astype(right_out.dtype)
+        if step < reach_left:
+            left_out[step - 1] = (
+                left_in[step - 1].astype(jnp.float32) + own(step - reach_left)
+            ).astype(left_out.dtype)
+    total = own(0) + right_in[reach_right - 1].astype(jnp.float32)
+    total = total + left_in[reach_left - 1].astype(jnp.float32)
+    o_ref[...] = total.astype(o_ref.dtype)
+
+
+def kernel_reduce_scatter(partial, axis, other, collective_id):
+    count = lax.axis_size(axis)
+    blocks = partial.reshape((count, partial.shape[0] // count) + partial.shape[1:])
+    block = blocks.shape[1:]
+    reach_right = count // 2
+    reach_left = count - 1 - reach_right
+    return pl.pallas_call(
+        functools.partial(ring_sum_kernel, count=count, axis=axis, other=other),
+        out_shape=jax.ShapeDtypeStruct(block, partial.dtype),
+        in_specs=[pl.BlockSpec(memory_space=pltpu.VMEM)],
+        out_specs=pl.BlockSpec(memory_space=pltpu.VMEM),
+        scratch_shapes=[
+            pltpu.VMEM((reach_right,) + block, partial.dtype),
+            pltpu.VMEM((reach_right,) + block, partial.dtype),
+            pltpu.VMEM((reach_left,) + block, partial.dtype),
+            pltpu.VMEM((reach_left,) + block, partial.dtype),
+            pltpu.SemaphoreType.DMA((4, reach_right)),
+        ],
+        compiler_params=pltpu.CompilerParams(collective_id=collective_id, has_side_effects=True),
+    )(blocks)
+
+
 def project_rows(rows, weight):
     flat = rows.reshape(-1, rows.shape[-1])
     return jnp.dot(flat, weight, preferred_element_type=jnp.float32).astype(jnp.bfloat16)
@@ -187,11 +272,16 @@
     position = ctx_index * tok_dev + jnp.arange(tok_dev)
     valid = position % LENGTH >= CH - 1
     attended = jnp.where(valid[:, None], blended, jnp.zeros_like(blended)).astype(jnp.bfloat16)
-    return lax.psum_scatter(
-        jnp.dot(attended, out_weight, preferred_element_type=jnp.float32).astype(jnp.bfloat16),
-        "tp",
-        scatter_dimension=0,
-        tiled=True,
+    mixed_part = jnp.dot(attended, out_weight, preferred_element_type=jnp.float32).astype(
+        jnp.bfloat16
+    )
+    split = mixed_part.shape[1] // 2
+    return jnp.concatenate(
+        [
+            lax.psum_scatter(mixed_part[:, :split], "tp", scatter_dimension=0, tiled=True),
+            kernel_reduce_scatter(mixed_part[:, split:], "tp", "ctx", 1),
+        ],
+        axis=1,
     )
 
 

time: 257 us -> 256 us (level)
  waiting for transfers between devices: 84.5 us -> 25.8 us
  Pallas kernels: 93.9 us -> 149 us
    reduce_scatter x1, waiting for transfers between devices: 73.5 us -> 14.8 us  [local(): lax.psum_scatter(mixed_part[:, :split], 'tp', scatter_dimension=0, tiled=...]
    pallas_call x0 -> x1, Pallas kernels: none -> 54.9 us  [kernel_reduce_scatter(): pl.pallas_call(functools.partial(ring_sum_kernel, count=count, axis=axis,...]
  transfers between devices with their start and end apart: 6 -> 6, of which waited for: 3 -> 3; matrix products, arithmetic and copies ran while one was open for 11% -> 12% of each run, Pallas kernels for 37% -> 58%
where the time goes in v5:
time: 256 us; the launch traced here: 254 us
  Pallas kernels  149 us (58%)
  waiting for transfers between devices  25.8 us (10%)
  local copies, waits for them, and re-layouts  22.4 us (9%)
  starting transfers between devices  21.6 us (8%)
  between operations  13.7 us (5%)
  other arithmetic  12 us (5%)
  matrix products  10.2 us (4%)
    pallas_call x1, Pallas kernels, kernel_gather(): pl.pallas_call(functools.partial(ring_gather_kernel, count=count, axis=ax...  93.9 us
    pallas_call x1, Pallas kernels, kernel_reduce_scatter(): pl.pallas_call(functools.partial(ring_sum_kernel, count=count, axis=axis,...  54.9 us
    reduce_scatter x1, waiting for transfers between devices, local(): lax.psum_scatter(mixed_part[:, :split], 'tp', scatter_dimension=0, tiled=...  14.8 us
    all_to_all x1, starting transfers between devices, local(): lax.all_to_all(outgoing, 'ctx', split_axis=0, concat_axis=0, tiled=True)  9.29 us
    all_to_all x1, waiting for transfers between devices, local(): lax.all_to_all(outgoing, 'ctx', split_axis=0, concat_axis=0, tiled=True)  8.55 us
    all_to_all x1, starting transfers between devices, local(): lax.all_to_all(jnp.broadcast_to(query_weight[None], (ctx_count,) + query_...  7 us
    ppermute x2, starting transfers between devices, shifted(): return lax.ppermute(block, axis, route)  5.3 us
  transfers between devices with their start and end apart: 6, of which 3 were waited for; matrix products, arithmetic and copies ran while one was open for 12% of the time, Pallas kernels for 58%

profile of v5, /device:TPU:24, one launch (start us, length us, event | category | flops | bytes accessed | tf_op | source)
XLA Modules:
  0.0 254.5 jit_solution(8474678884144649618)
XLA Ops:
  8.3 3.6 %gather_fusion = s32[512]{0:T(512)S(1)} fusion(s32[512]{0:T(512)} %param.17, s32[1024]{0:T(1024)S(1)} %pad_clamp_fusion.2), kind=kCustom, calls=%fused_computation | custom fusion | bytes 6144 | tf_op jit(solution)/shard_map/gather | solution.py:210
  13.9 9.3 %all-to-all-start = ((bf16[32,1,8,1024]{3,2,1,0:T(8,128)(2,1)}), bf16[32,1,8,1024]{3,2,1,0:T(8,128)(2,1)S(1)}, u32[]{:S(2)}, u32[]{:S(2)}) async-start(bf16[32,1,8,1024]{3,2,1,0:T(8,128)(2,1)} %bitcast_multiply_fusion), calls=%async_computation | async-start | bytes 1048576 | tf_op jit(solution)/shard_map/all_to_all | solution.py:221
  24.2 8.6 %all-to-all-done = bf16[32,1,8,1024]{3,2,1,0:T(8,128)(2,1)S(1)} async-done(((bf16[32,1,8,1024]{3,2,1,0:T(8,128)(2,1)}), bf16[32,1,8,1024]{3,2,1,0:T(8,128)(2,1)S(1)}, u32[]{:S(2)}, u32[]{:S(2)}) %all-to-all-start) | async-done | bytes 524320 | tf_op jit(solution)/shard_map/all_to_all | solution.py:221
  32.7 1.5 broadcast_in_dim.30
  34.3 7.0 %all-to-all-start.1 = ((bf16[32,128,256]{2,1,0:T(8,128)(2,1)}), bf16[32,128,256]{2,1,0:T(8,128)(2,1)}, u32[]{:S(2)}, u32[]{:S(2)}) async-start(bf16[32,128,256]{2,1,0:T(8,128)(2,1)} %broadcast_in_dim.30), calls=%async_computation.1 | async-start | bytes 4194304 | tf_op jit(solution)/shard_map/all_to_all | solution.py:201
  43.5 93.9 %shard_map.100 = bf16[16,16,8,1024]{3,2,1,0:T(8,128)(2,1)} custom-call(bf16[16,8,1024]{2,1,0:T(8,128)(2,1)} %gather_fusion.2), custom_call_target="tpu_custom_call" | custom-call | tf_op jit(solution)/shard_map/pallas_call | solution.py:73
  137.4 2.7 %copy.25 = bf16[16,16,8,1024]{3,2,1,0:T(8,128)(2,1)S(1)} copy(bf16[16,16,8,1024]{3,2,0,1:T(8,128)(2,1)} %bitcast.43) | data formatting | bytes 8388608 | tf_op jit(solution)/shard_map/transpose | solution.py:231
  140.1 1.3 convolution_convert_fusion.1
  141.4 1.9 collective-permute-start.1
  143.3 1.3 convolution_convert_fusion.2
  144.6 3.4 %collective-permute-start = (bf16[2,128,256]{2,1,0:T(8,128)(2,1)S(1)}, bf16[2,128,256]{2,1,0:T(8,128)(2,1)S(1)}, u32[]{:S(2)}, u32[]{:S(2)}) collective-permute-start(bf16[2,128,256]{2,1,0:T(8,128)(2,1)S(1)} %bitcast.52), channel_id=1, source_target_pairs={{0,16},{16,32},{32,48},{48,64},{64,80},{80,96},{96,112},{112,128},... | collective-permute-start | bytes 393224 | tf_op jit(solution)/shard_map/ppermute | solution.py:23
  148.0 1.7 collective-permute-done.1
  150.9 2.8 %reshape.191 = bf16[9,256,2,128]{3,2,1,0:T(2,128)(2,1)S(1)} reshape(bf16[18,128,256]{2,1,0:T(8,128)(2,1)} %pad_maximum_fusion) | data formatting | bytes 2359296 | tf_op jit(solution)/shard_map/reshape | solution.py:242
  153.7 2.4 pad_maximum_fusion.1
  156.0 3.5 %reshape.187 = bf16[9,256,2,128]{3,2,1,0:T(2,128)(2,1)} reshape(bf16[18,128,256]{2,1,0:T(8,128)(2,1)} %pad_maximum_fusion.1) | data formatting | bytes 2359296 | tf_op jit(solution)/shard_map/reshape | solution.py:243
  159.6 3.1 %fusion = f32[512]{0:T(512)S(1)} fusion(bf16[512,4096]{1,0:T(8,128)(2,1)} %all-gather.2.cloned.1.call-done), kind=kLoop, calls=%fused_computation.5 | loop fusion | flops 6290944 | bytes 4196352 | tf_op jit(solution)/shard_map/reduce_sum | solution.py:197
  162.7 4.2 %fusion.11 = bf16[512,256]{1,0:T(8,128)(2,1)S(1)} fusion(bf16[4096,256]{1,0:T(8,128)(2,1)} %bitcast.13, bf16[512,4096]{1,0:T(8,128)(2,1)} %all-gather.2.cloned.1.call-done, f32[4096]{0:T(1024)S(1)} %copy-done.7, f32[512]{0:T(512)S(1)} %add_rsqrt_fusion), kind=kOutput, calls=%fused_computation.18 | convolution fusion | flops 1082392576 | bytes 6572032 | tf_op jit(solution)/shard_map/dot_general | solution.py:208
  167.8 1.7 reshape.189
  169.5 1.7 fusion.41
  172.5 1.3 convolution_convert_fusion
  173.8 2.5 fusion.40
  176.3 54.9 %shard_map.101 = bf16[32,2048]{1,0:T(8,128)(2,1)} custom-call(bf16[16,32,2048]{2,1,0:T(8,128)(2,1)} %bitcast.44), custom_call_target="tpu_custom_call" | custom-call | tf_op jit(solution)/shard_map/pallas_call | solution.py:152
  231.2 14.8 %reduce-scatter.2.cloned.1.call-done = bf16[32,2048]{1,0:T(8,128)(2,1)} async-done(((bf16[512,2048]{1,0:T(8,128)(2,1)}), bf16[32,2048]{1,0:T(8,128)(2,1)}) %reduce-scatter.2.cloned.1.call-update) | async-done | bytes 131088 | tf_op jit(solution)/shard_map/reduce_scatter | solution.py:281
  245.9 1.7 pad_maximum_fusion.2
  (62 shorter events, 10.1 us)
Async XLA Ops:
  6.5 166.0 %copy-start = (bf16[256,4096]{1,0:T(8,128)(2,1)S(1)}, bf16[256,4096]{1,0:T(8,128)(2,1)}, u32[]{:S(2)}) copy-start(bf16[256,4096]{1,0:T(8,128)(2,1)} %param.15) | copy-start | bytes 6291460
  6.5 5.9 %copy-start.3 = (bf16[16,8,1024]{2,1,0:T(8,128)(2,1)S(1)}, bf16[16,8,1024]{2,1,0:T(8,128)(2,1)}, u32[]{:S(2)}) copy-start(bf16[16,8,1024]{2,1,0:T(8,128)(2,1)} %param.16) | copy-start | bytes 786436
  6.5 153.0 %all-gather.2.cloned.1.call-start = ((), (), s32[]{:S(2)}) async-start(), calls=%async_computation.3 | async-start | bytes 4456448 | tf_op jit(solution)/shard_map/all_gather | solution.py:195
  11.9 11.4 %copy-start.8 = (s32[256]{0:T(256)S(1)}, s32[256]{0:T(256)}, u32[]{:S(2)}) copy-start(s32[256]{0:T(256)} %param.19) | copy-start | bytes 3076
  11.9 20.8 %copy-start.4 = (bf16[128,256]{1,0:T(8,128)(2,1)S(1)}, bf16[128,256]{1,0:T(8,128)(2,1)}, u32[]{:S(2)}) copy-start(bf16[128,256]{1,0:T(8,128)(2,1)} %param.12) | copy-start | bytes 196612
  13.9 18.8 %all-to-all-start = ((bf16[32,1,8,1024]{3,2,1,0:T(8,128)(2,1)}), bf16[32,1,8,1024]{3,2,1,0:T(8,128)(2,1)S(1)}, u32[]{:S(2)}, u32[]{:S(2)}) async-start(bf16[32,1,8,1024]{3,2,1,0:T(8,128)(2,1)} %bitcast_multiply_fusion), calls=%async_computation | async-start | bytes 1048576 | tf_op jit(solution)/shard_map/all_to_all | solution.py:221
  34.3 128.4 %all-to-all-start.1 = ((bf16[32,128,256]{2,1,0:T(8,128)(2,1)}), bf16[32,128,256]{2,1,0:T(8,128)(2,1)}, u32[]{:S(2)}, u32[]{:S(2)}) async-start(bf16[32,128,256]{2,1,0:T(8,128)(2,1)} %broadcast_in_dim.30), calls=%async_computation.1 | async-start | bytes 4194304 | tf_op jit(solution)/shard_map/all_to_all | solution.py:201
  41.3 204.7 %reduce-scatter.2.cloned.1.call-start = ((), (), s32[]{:S(2)}) async-start(), calls=%async_computation.4 | async-start | bytes 2228224 | tf_op jit(solution)/shard_map/reduce_scatter | solution.py:281
  137.3 2.7 %copy-start.5 = (bf16[1024,256]{1,0:T(8,128)(2,1)S(1)}, bf16[1024,256]{1,0:T(8,128)(2,1)}, u32[]{:S(2)}) copy-start(bf16[1024,256]{1,0:T(8,128)(2,1)} %param.13) | copy-start | bytes 1572868
  140.1 3.2 %copy-start.6 = (bf16[1024,256]{1,0:T(8,128)(2,1)S(1)}, bf16[1024,256]{1,0:T(8,128)(2,1)}, u32[]{:S(2)}) copy-start(bf16[1024,256]{1,0:T(8,128)(2,1)} %param.14) | copy-start | bytes 1572868
  141.4 8.4 %collective-permute-start.1 = (bf16[2,128,256]{2,1,0:T(8,128)(2,1)S(1)}, bf16[2,128,256]{2,1,0:T(8,128)(2,1)S(1)}, u32[]{:S(2)}, u32[]{:S(2)}) collective-permute-start(bf16[2,128,256]{2,1,0:T(8,128)(2,1)S(1)} %bitcast.53), channel_id=1, source_target_pairs={{0,16},{16,32},{32,48},{48,64},{64,80},{80,96},{96,112},{112,128},... | collective-permute-start | bytes 393224 | tf_op jit(solution)/shard_map/ppermute | solution.py:23
  144.6 5.2 %copy-start.1 = (bf16[2048,256]{1,0:T(8,128)(2,1)}, bf16[2048,256]{1,0:T(8,128)(2,1)S(1)}, u32[]{:S(2)}) copy-start(bf16[2048,256]{1,0:T(8,128)(2,1)S(1)} %convolution_convert_fusion.2) | copy-start | bytes 3145732
  144.6 9.0 %collective-permute-start = (bf16[2,128,256]{2,1,0:T(8,128)(2,1)S(1)}, bf16[2,128,256]{2,1,0:T(8,128)(2,1)S(1)}, u32[]{:S(2)}, u32[]{:S(2)}) collective-permute-start(bf16[2,128,256]{2,1,0:T(8,128)(2,1)S(1)} %bitcast.52), channel_id=1, source_target_pairs={{0,16},{16,32},{32,48},{48,64},{64,80},{80,96},{96,112},{112,128},... | collective-permute-start | bytes 393224 | tf_op jit(solution)/shard_map/ppermute | solution.py:23
  159.6 3.1 %copy-start.7 = (f32[4096]{0:T(1024)S(1)}, f32[4096]{0:T(1024)}, u32[]{:S(2)}) copy-start(f32[4096]{0:T(1024)} %param.11) | copy-start | bytes 49156
  169.5 2.1 copy-start.2
Sparse Core Ops, SparseCore 0:
  9.4 119.7 all-gather.1
  176.4 69.4 reduce-scatter.1

commit v6 on v1

--- a/solution.py
+++ b/solution.py
@@ -1,6 +1,10 @@
+import functools
+
 import jax
 import jax.numpy as jnp
 from jax import lax
+from jax.experimental import pallas as pl
+from jax.experimental.pallas import tpu as pltpu
 from jax.sharding import PartitionSpec as P
 
 HS = 128
@@ -19,20 +23,136 @@
     return lax.ppermute(block, axis, route)
 
 
-def ring_gather(block, axis, dim):
+def greet_neighbours(me, row, count):
+    right = lax.rem(me + 1, count)
+    left = lax.rem(me + count - 1, count)
+    barrier = pltpu.get_barrier_semaphore()
+    for neighbour in (left, right):
+        pl.semaphore_signal(
+            barrier, inc=1, device_id=(row, neighbour), device_id_type=pl.DeviceIdType.MESH
+        )
+    pl.semaphore_wait(barrier, 2)
+    return right, left
+
+
+def ring_gather_kernel(x_ref, o_ref, send_sem, recv_sem, *, count, axis, other, pieces):
+    me = lax.axis_index(axis)
+    row = lax.axis_index(other)
+    right, left = greet_neighbours(me, row, count)
+    half = count // 2
+    size = x_ref.shape[0] // pieces
+    o_ref[half] = x_ref[...]
+    copies = {}
+    for step in range(1, half + 1):
+        for piece in range(pieces):
+            part = pl.ds(piece * size, size)
+            for toward in (0, 1):
+                if toward == 1 and step > count - 1 - half:
+                    continue
+                slot = half - step if toward == 0 else half + step
+                source = slot + 1 if toward == 0 else slot - 1
+                if step > 1:
+                    copies[(step - 1, toward, piece)].wait_recv()
+                copy = pltpu.make_async_remote_copy(
+                    src_ref=x_ref.at[part] if step == 1 else o_ref.at[source, part],
+                    dst_ref=o_ref.at[slot, part],
+                    send_sem=send_sem.at[slot, piece],
+                    recv_sem=recv_sem.at[slot, piece],
+                    device_id=(row, right if toward == 0 else left),
+                    device_id_type=pl.DeviceIdType.MESH,
+                )
+                copy.start()
+                copies[(step, toward, piece)] = copy
+    for piece in range(pieces):
+        copies[(half, 0, piece)].wait_recv()
+        copies[(count - 1 - half, 1, piece)].wait_recv()
+    for copy in copies.values():
+        copy.wait_send()
+
+
+def kernel_gather(block, axis, other, collective_id, pieces=4):
     count = lax.axis_size(axis)
-    pieces = [block]
-    right = block
-    left = block
-    for step in range(count // 2):
-        right = lax.ppermute(
-            right, axis, [(i, (i + 1) % count) for i in range(count)]
-        )
-        pieces.append(right)
-        if step < count - 1 - count // 2:
-            left = lax.ppermute(left, axis, [(i, (i - 1) % count) for i in range(count)])
-            pieces.append(left)
-    return jnp.concatenate(pieces, axis=dim)
+    return pl.pallas_call(
+        functools.partial(
+            ring_gather_kernel, count=count, axis=axis, other=other, pieces=pieces
+        ),
+        out_shape=jax.ShapeDtypeStruct((count,) + block.shape, block.dtype),
+        in_specs=[pl.BlockSpec(memory_space=pltpu.VMEM)],
+        out_specs=pl.BlockSpec(memory_space=pltpu.VMEM),
+        scratch_shapes=[
+            pltpu.SemaphoreType.DMA((count, pieces)),
+            pltpu.SemaphoreType.DMA((count, pieces)),
+        ],
+        compiler_params=pltpu.CompilerParams(collective_id=collective_id, has_side_effects=True),
+    )(block)
+
+
+def ring_sum_kernel(p_ref, o_ref, sums_in, sums_out, sems, *, count, axis, other, pieces):
+    me = lax.axis_index(axis)
+    row = lax.axis_index(other)
+    right, left = greet_neighbours(me, row, count)
+    reach = (count // 2, count - 1 - count // 2)
+    width = p_ref.shape[2] // pieces
+
+    def own(offset, part):
+        return p_ref[lax.rem(me + offset + 2 * count, count), :, part].astype(jnp.float32)
+
+    copies = {}
+    for step in range(1, reach[0] + 1):
+        for piece in range(pieces):
+            part = pl.ds(piece * width, width)
+            for toward in (0, 1):
+                if step > reach[toward]:
+                    continue
+                if step == 1:
+                    first = reach[0] if toward == 0 else count - reach[1]
+                    source = p_ref.at[lax.rem(me + first, count), :, part]
+                else:
+                    copies[(step - 1, toward, piece)].wait_recv()
+                    offset = reach[0] - step + 1 if toward == 0 else step - 1 - reach[1]
+                    sums_out[toward, step - 2, :, part] = (
+                        sums_in[toward, step - 2, :, part].astype(jnp.float32) + own(offset, part)
+                    ).astype(sums_out.dtype)
+                    source = sums_out.at[toward, step - 2, :, part]
+                copy = pltpu.make_async_remote_copy(
+                    src_ref=source,
+                    dst_ref=sums_in.at[toward, step - 1, :, part],
+                    send_sem=sems.at[0, toward, step - 1, piece],
+                    recv_sem=sems.at[1, toward, step - 1, piece],
+                    device_id=(row, right if toward == 0 else left),
+                    device_id_type=pl.DeviceIdType.MESH,
+                )
+                copy.start()
+                copies[(step, toward, piece)] = copy
+    for piece in range(pieces):
+        copies[(reach[0], 0, piece)].wait_recv()
+        copies[(reach[1], 1, piece)].wait_recv()
+    for copy in copies.values():
+        copy.wait_send()
+    total = p_ref[me].astype(jnp.float32) + sums_in[0, reach[0] - 1].astype(jnp.float32)
+    total = total + sums_in[1, reach[1] - 1].astype(jnp.float32)
+    o_ref[...] = total.astype(o_ref.dtype)
+
+
+def kernel_reduce_scatter(partial, axis, other, collective_id, pieces=4):
+    count = lax.axis_size(axis)
+    blocks = partial.reshape((count, partial.shape[0] // count) + partial.shape[1:])
+    block = blocks.shape[1:]
+    reach = count // 2
+    return pl.pallas_call(
+        functools.partial(
+            ring_sum_kernel, count=count, axis=axis, other=other, pieces=pieces
+        ),
+        out_shape=jax.ShapeDtypeStruct(block, partial.dtype),
+        in_specs=[pl.BlockSpec(memory_space=pltpu.VMEM)],
+        out_specs=pl.BlockSpec(memory_space=pltpu.VMEM),
+        scratch_shapes=[
+            pltpu.VMEM((2, reach) + block, partial.dtype),
+            pltpu.VMEM((2, reach) + block, partial.dtype),
+            pltpu.SemaphoreType.DMA((2, 2, reach, pieces)),
+        ],
+        compiler_params=pltpu.CompilerParams(collective_id=collective_id, has_side_effects=True),
+    )(blocks)
 
 
 def project_rows(rows, weight):
@@ -98,7 +218,9 @@
     flat_index = own_sources * slot_cap + own_rank
     picked = incoming.reshape(ctx_count * slot_cap, slice_tokens, enc_width)[flat_index]
     row_total = picked.shape[0]
-    full_rows = ring_gather(picked, "tp", 1)
+    full_rows = jnp.swapaxes(kernel_gather(picked, "tp", "ctx", 0), 0, 1).reshape(
+        picked.shape[0], -1, picked.shape[2]
+    )
     keys = project_rows(full_rows, key_weight).reshape(row_total, -1, head_width)
     values = project_rows(full_rows, value_weight).reshape(row_total, -1, head_width)
     neighbour_len = keys.shape[1]
@@ -140,11 +262,16 @@
     position = ctx_index * tok_dev + jnp.arange(tok_dev)
     valid = position % LENGTH >= CH - 1
     attended = jnp.where(valid[:, None], blended, jnp.zeros_like(blended)).astype(jnp.bfloat16)
-    return lax.psum_scatter(
-        jnp.dot(attended, out_weight, preferred_element_type=jnp.float32).astype(jnp.bfloat16),
-        "tp",
-        scatter_dimension=0,
-        tiled=True,
+    mixed_part = jnp.dot(attended, out_weight, preferred_element_type=jnp.float32).astype(
+        jnp.bfloat16
+    )
+    split = mixed_part.shape[1] // 2
+    return jnp.concatenate(
+        [
+            lax.psum_scatter(mixed_part[:, :split], "tp", scatter_dimension=0, tiled=True),
+            kernel_reduce_scatter(mixed_part[:, split:], "tp", "ctx", 1),
+        ],
+        axis=1,
     )
 
 

time: 264 us -> 246 us (0.932)
  Pallas kernels: 0 us -> 126 us
  waiting for transfers between devices: 132 us -> 38 us
  starting transfers between devices: 78 us -> 22.1 us
  local copies, waits for them, and re-layouts: 15.6 us -> 22.4 us
  matrix products: 13.3 us -> 10.2 us
  other arithmetic: 9.33 us -> 12 us
    pallas_call x0 -> x2, Pallas kernels: none -> 126 us  [the longest x1 86.8 us: kernel_gather(): pl.pallas_call(functools.partial(ring_gather_kernel, count=count, axis=ax...]
    ppermute x15 -> x0, starting transfers between devices: 58.2 us -> none  [the longest x7 41.8 us: ring_gather(): lax.ppermute(left, axis, [(i, (i - 1) % count) for i in range(count)])]
    reduce_scatter x1, waiting for transfers between devices: 73.8 us -> 27.4 us  [local(): lax.psum_scatter(mixed_part[:, :split], 'tp', scatter_dimension=0, tiled=...]
    ppermute x15 -> x0, waiting for transfers between devices: 43.5 us -> none  [the longest x7 28.8 us: ring_gather(): lax.ppermute(left, axis, [(i, (i - 1) % count) for i in range(count)])]
    ppermute x2, waiting for transfers between devices: 4.65 us -> 1.31 us  [shifted(): return lax.ppermute(block, axis, route)]
    transpose x0 -> x1, local copies, waits for them, and re-layouts: none -> 2.72 us  [local(): jnp.swapaxes(kernel_gather(picked, 'tp', 'ctx', 0), 0, 1)]
  transfers between devices with their start and end apart: 21 -> 6, of which waited for: 13 -> 3; matrix products, arithmetic and copies ran while one was open for 9% -> 12% of each run, Pallas kernels for 0% -> 52%
where the time goes in v6:
time: 246 us; the launch traced here: 245 us
  Pallas kernels  126 us (51%)
  waiting for transfers between devices  38 us (15%)
  local copies, waits for them, and re-layouts  22.4 us (9%)
  starting transfers between devices  22.1 us (9%)
  between operations  13.7 us (6%)
  other arithmetic  12 us (5%)
  matrix products  10.2 us (4%)
    pallas_call x1, Pallas kernels, kernel_gather(): pl.pallas_call(functools.partial(ring_gather_kernel, count=count, axis=ax...  86.8 us
    pallas_call x1, Pallas kernels, kernel_reduce_scatter(): pl.pallas_call(functools.partial(ring_sum_kernel, count=count, axis=axis,...  39.7 us
    reduce_scatter x1, waiting for transfers between devices, local(): lax.psum_scatter(mixed_part[:, :split], 'tp', scatter_dimension=0, tiled=...  27.4 us
    all_to_all x1, starting transfers between devices, local(): lax.all_to_all(outgoing, 'ctx', split_axis=0, concat_axis=0, tiled=True)  9.29 us
    all_to_all x1, waiting for transfers between devices, local(): lax.all_to_all(outgoing, 'ctx', split_axis=0, concat_axis=0, tiled=True)  8.55 us
    all_to_all x1, starting transfers between devices, local(): lax.all_to_all(jnp.broadcast_to(query_weight[None], (ctx_count,) + query_...  7 us
    ppermute x2, starting transfers between devices, shifted(): return lax.ppermute(block, axis, route)  5.74 us
  transfers between devices with their start and end apart: 6, of which 3 were waited for; matrix products, arithmetic and copies ran while one was open for 12% of the time, Pallas kernels for 52%

profile of v6, /device:TPU:24, one launch (start us, length us, event | category | flops | bytes accessed | tf_op | source)
XLA Modules:
  0.0 244.8 jit_solution(6026062515802112643)
XLA Ops:
  8.3 3.6 %gather_fusion = s32[512]{0:T(512)S(1)} fusion(s32[512]{0:T(512)} %param.17, s32[1024]{0:T(1024)S(1)} %pad_clamp_fusion.2), kind=kCustom, calls=%fused_computation | custom fusion | bytes 6144 | tf_op jit(solution)/shard_map/gather | solution.py:200
  13.9 9.3 %all-to-all-start = ((bf16[32,1,8,1024]{3,2,1,0:T(8,128)(2,1)}), bf16[32,1,8,1024]{3,2,1,0:T(8,128)(2,1)S(1)}, u32[]{:S(2)}, u32[]{:S(2)}) async-start(bf16[32,1,8,1024]{3,2,1,0:T(8,128)(2,1)} %bitcast_multiply_fusion), calls=%async_computation | async-start | bytes 1048576 | tf_op jit(solution)/shard_map/all_to_all | solution.py:211
  24.2 8.6 %all-to-all-done = bf16[32,1,8,1024]{3,2,1,0:T(8,128)(2,1)S(1)} async-done(((bf16[32,1,8,1024]{3,2,1,0:T(8,128)(2,1)}), bf16[32,1,8,1024]{3,2,1,0:T(8,128)(2,1)S(1)}, u32[]{:S(2)}, u32[]{:S(2)}) %all-to-all-start) | async-done | bytes 524320 | tf_op jit(solution)/shard_map/all_to_all | solution.py:211
  32.7 1.5 broadcast_in_dim.30
  34.3 7.0 %all-to-all-start.1 = ((bf16[32,128,256]{2,1,0:T(8,128)(2,1)}), bf16[32,128,256]{2,1,0:T(8,128)(2,1)}, u32[]{:S(2)}, u32[]{:S(2)}) async-start(bf16[32,128,256]{2,1,0:T(8,128)(2,1)} %broadcast_in_dim.30), calls=%async_computation.1 | async-start | bytes 4194304 | tf_op jit(solution)/shard_map/all_to_all | solution.py:191
  43.5 86.8 %shard_map.100 = bf16[16,16,8,1024]{3,2,1,0:T(8,128)(2,1)} custom-call(bf16[16,8,1024]{2,1,0:T(8,128)(2,1)} %gather_fusion.2), custom_call_target="tpu_custom_call" | custom-call | tf_op jit(solution)/shard_map/pallas_call | solution.py:75
  130.3 2.7 %copy.25 = bf16[16,16,8,1024]{3,2,1,0:T(8,128)(2,1)S(1)} copy(bf16[16,16,8,1024]{3,2,0,1:T(8,128)(2,1)} %bitcast.43) | data formatting | bytes 8388608 | tf_op jit(solution)/shard_map/transpose | solution.py:221
  133.0 1.3 convolution_convert_fusion.1
  134.3 1.9 collective-permute-start.1
  136.2 1.3 convolution_convert_fusion.2
  137.6 3.8 %collective-permute-start = (bf16[2,128,256]{2,1,0:T(8,128)(2,1)S(1)}, bf16[2,128,256]{2,1,0:T(8,128)(2,1)S(1)}, u32[]{:S(2)}, u32[]{:S(2)}) collective-permute-start(bf16[2,128,256]{2,1,0:T(8,128)(2,1)S(1)} %bitcast.52), channel_id=1, source_target_pairs={{0,16},{16,32},{32,48},{48,64},{64,80},{80,96},{96,112},{112,128},... | collective-permute-start | bytes 393224 | tf_op jit(solution)/shard_map/ppermute | solution.py:23
  141.4 1.3 collective-permute-done.1
  143.8 2.8 %reshape.191 = bf16[9,256,2,128]{3,2,1,0:T(2,128)(2,1)S(1)} reshape(bf16[18,128,256]{2,1,0:T(8,128)(2,1)} %pad_maximum_fusion) | data formatting | bytes 2359296 | tf_op jit(solution)/shard_map/reshape | solution.py:232
  146.6 2.4 pad_maximum_fusion.1
  149.0 3.5 %reshape.187 = bf16[9,256,2,128]{3,2,1,0:T(2,128)(2,1)} reshape(bf16[18,128,256]{2,1,0:T(8,128)(2,1)} %pad_maximum_fusion.1) | data formatting | bytes 2359296 | tf_op jit(solution)/shard_map/reshape | solution.py:233
  152.5 3.1 %fusion = f32[512]{0:T(512)S(1)} fusion(bf16[512,4096]{1,0:T(8,128)(2,1)} %all-gather.2.cloned.1.call-done), kind=kLoop, calls=%fused_computation.5 | loop fusion | flops 6290944 | bytes 4196352 | tf_op jit(solution)/shard_map/reduce_sum | solution.py:187
  155.6 4.2 %fusion.11 = bf16[512,256]{1,0:T(8,128)(2,1)S(1)} fusion(bf16[4096,256]{1,0:T(8,128)(2,1)} %bitcast.13, bf16[512,4096]{1,0:T(8,128)(2,1)} %all-gather.2.cloned.1.call-done, f32[4096]{0:T(1024)S(1)} %copy-done.7, f32[512]{0:T(512)S(1)} %add_rsqrt_fusion), kind=kOutput, calls=%fused_computation.18 | convolution fusion | flops 1082392576 | bytes 6572032 | tf_op jit(solution)/shard_map/dot_general | solution.py:198
  160.7 1.7 reshape.189
  162.5 1.7 fusion.41
  165.4 1.3 convolution_convert_fusion
  166.7 2.5 %fusion.40 = (bf16[512,2048]{1,0:T(8,128)(2,1)}, bf16[512,2048]{1,0:T(8,128)(2,1)}) fusion(bf16[512,4096]{1,0:T(8,128)(2,1)S(1)} %convolution_convert_fusion), kind=kLoop, calls=%fused_computation.78 | loop fusion | bytes 8388608 | tf_op jit(solution)/shard_map/slice | solution.py:271
  169.2 39.7 %shard_map.101 = bf16[32,2048]{1,0:T(8,128)(2,1)} custom-call(bf16[16,32,2048]{2,1,0:T(8,128)(2,1)} %bitcast.44), custom_call_target="tpu_custom_call" | custom-call | tf_op jit(solution)/shard_map/pallas_call | solution.py:142
  208.9 27.4 %reduce-scatter.2.cloned.1.call-done = bf16[32,2048]{1,0:T(8,128)(2,1)} async-done(((bf16[512,2048]{1,0:T(8,128)(2,1)}), bf16[32,2048]{1,0:T(8,128)(2,1)}) %reduce-scatter.2.cloned.1.call-update) | async-done | bytes 131088 | tf_op jit(solution)/shard_map/reduce_scatter | solution.py:271
  236.3 1.7 pad_maximum_fusion.2
  (62 shorter events, 10.1 us)
Async XLA Ops:
  6.5 158.9 %copy-start = (bf16[256,4096]{1,0:T(8,128)(2,1)S(1)}, bf16[256,4096]{1,0:T(8,128)(2,1)}, u32[]{:S(2)}) copy-start(bf16[256,4096]{1,0:T(8,128)(2,1)} %param.15) | copy-start | bytes 6291460
  6.5 5.9 %copy-start.3 = (bf16[16,8,1024]{2,1,0:T(8,128)(2,1)S(1)}, bf16[16,8,1024]{2,1,0:T(8,128)(2,1)}, u32[]{:S(2)}) copy-start(bf16[16,8,1024]{2,1,0:T(8,128)(2,1)} %param.16) | copy-start | bytes 786436
  6.5 146.0 %all-gather.2.cloned.1.call-start = ((), (), s32[]{:S(2)}) async-start(), calls=%async_computation.3 | async-start | bytes 4456448 | tf_op jit(solution)/shard_map/all_gather | solution.py:185
  11.9 11.4 %copy-start.8 = (s32[256]{0:T(256)S(1)}, s32[256]{0:T(256)}, u32[]{:S(2)}) copy-start(s32[256]{0:T(256)} %param.19) | copy-start | bytes 3076
  11.9 20.8 %copy-start.4 = (bf16[128,256]{1,0:T(8,128)(2,1)S(1)}, bf16[128,256]{1,0:T(8,128)(2,1)}, u32[]{:S(2)}) copy-start(bf16[128,256]{1,0:T(8,128)(2,1)} %param.12) | copy-start | bytes 196612
  13.9 18.8 %all-to-all-start = ((bf16[32,1,8,1024]{3,2,1,0:T(8,128)(2,1)}), bf16[32,1,8,1024]{3,2,1,0:T(8,128)(2,1)S(1)}, u32[]{:S(2)}, u32[]{:S(2)}) async-start(bf16[32,1,8,1024]{3,2,1,0:T(8,128)(2,1)} %bitcast_multiply_fusion), calls=%async_computation | async-start | bytes 1048576 | tf_op jit(solution)/shard_map/all_to_all | solution.py:211
  34.3 121.3 %all-to-all-start.1 = ((bf16[32,128,256]{2,1,0:T(8,128)(2,1)}), bf16[32,128,256]{2,1,0:T(8,128)(2,1)}, u32[]{:S(2)}, u32[]{:S(2)}) async-start(bf16[32,128,256]{2,1,0:T(8,128)(2,1)} %broadcast_in_dim.30), calls=%async_computation.1 | async-start | bytes 4194304 | tf_op jit(solution)/shard_map/all_to_all | solution.py:191
  41.3 195.0 %reduce-scatter.2.cloned.1.call-start = ((), (), s32[]{:S(2)}) async-start(), calls=%async_computation.4 | async-start | bytes 2228224 | tf_op jit(solution)/shard_map/reduce_scatter | solution.py:271
  130.2 2.7 %copy-start.5 = (bf16[1024,256]{1,0:T(8,128)(2,1)S(1)}, bf16[1024,256]{1,0:T(8,128)(2,1)}, u32[]{:S(2)}) copy-start(bf16[1024,256]{1,0:T(8,128)(2,1)} %param.13) | copy-start | bytes 1572868
  133.0 3.2 %copy-start.6 = (bf16[1024,256]{1,0:T(8,128)(2,1)S(1)}, bf16[1024,256]{1,0:T(8,128)(2,1)}, u32[]{:S(2)}) copy-start(bf16[1024,256]{1,0:T(8,128)(2,1)} %param.14) | copy-start | bytes 1572868
  134.3 8.4 %collective-permute-start.1 = (bf16[2,128,256]{2,1,0:T(8,128)(2,1)S(1)}, bf16[2,128,256]{2,1,0:T(8,128)(2,1)S(1)}, u32[]{:S(2)}, u32[]{:S(2)}) collective-permute-start(bf16[2,128,256]{2,1,0:T(8,128)(2,1)S(1)} %bitcast.53), channel_id=1, source_target_pairs={{0,16},{16,32},{32,48},{48,64},{64,80},{80,96},{96,112},{112,128},... | collective-permute-start | bytes 393224 | tf_op jit(solution)/shard_map/ppermute | solution.py:23
  137.5 5.2 %copy-start.1 = (bf16[2048,256]{1,0:T(8,128)(2,1)}, bf16[2048,256]{1,0:T(8,128)(2,1)S(1)}, u32[]{:S(2)}) copy-start(bf16[2048,256]{1,0:T(8,128)(2,1)S(1)} %convolution_convert_fusion.2) | copy-start | bytes 3145732
  137.6 9.0 %collective-permute-start = (bf16[2,128,256]{2,1,0:T(8,128)(2,1)S(1)}, bf16[2,128,256]{2,1,0:T(8,128)(2,1)S(1)}, u32[]{:S(2)}, u32[]{:S(2)}) collective-permute-start(bf16[2,128,256]{2,1,0:T(8,128)(2,1)S(1)} %bitcast.52), channel_id=1, source_target_pairs={{0,16},{16,32},{32,48},{48,64},{64,80},{80,96},{96,112},{112,128},... | collective-permute-start | bytes 393224 | tf_op jit(solution)/shard_map/ppermute | solution.py:23
  152.5 3.1 %copy-start.7 = (f32[4096]{0:T(1024)S(1)}, f32[4096]{0:T(1024)}, u32[]{:S(2)}) copy-start(f32[4096]{0:T(1024)} %param.11) | copy-start | bytes 49156
  162.5 2.1 copy-start.2
Sparse Core Ops, SparseCore 0:
  9.4 125.4 all-gather.1
  169.4 66.8 reduce-scatter.1

commit v7 on v6

--- a/solution.py
+++ b/solution.py
@@ -265,14 +265,7 @@
     mixed_part = jnp.dot(attended, out_weight, preferred_element_type=jnp.float32).astype(
         jnp.bfloat16
     )
-    split = mixed_part.shape[1] // 2
-    return jnp.concatenate(
-        [
-            lax.psum_scatter(mixed_part[:, :split], "tp", scatter_dimension=0, tiled=True),
-            kernel_reduce_scatter(mixed_part[:, split:], "tp", "ctx", 1),
-        ],
-        axis=1,
-    )
+    return kernel_reduce_scatter(mixed_part, "tp", "ctx", 1)
 
 
 def solution(mesh):

time: 246 us -> 230 us (0.935)
  waiting for transfers between devices: 38 us -> 10.7 us
  Pallas kernels: 126 us -> 139 us
    reduce_scatter x1 -> x0, waiting for transfers between devices: 27.4 us -> none  [local(): lax.psum_scatter(mixed_part[:, :split], 'tp', scatter_dimension=0, tiled=...]
    pallas_call x1, Pallas kernels: 39.7 us -> 52.2 us  [kernel_reduce_scatter(): pl.pallas_call(functools.partial(ring_sum_kernel, count=count, axis=axis,...]
    slice x1 -> x0, local copies, waits for them, and re-layouts: 2.46 us -> none  [local(): mixed_part[:, :split]]
  transfers between devices with their start and end apart: 6 -> 5, of which waited for: 3 -> 2; matrix products, arithmetic and copies ran while one was open for 12% -> 13% of each run, Pallas kernels for 52% -> 38%
where the time goes in v7:
time: 230 us; the launch traced here: 229 us
  Pallas kernels  139 us (60%)
  starting transfers between devices  21.9 us (10%)
  local copies, waits for them, and re-layouts  21.6 us (9%)
  between operations  13.7 us (6%)
  matrix products  12.1 us (5%)
  waiting for transfers between devices  10.7 us (5%)
  other arithmetic  10.3 us (4%)
    pallas_call x1, Pallas kernels, kernel_gather(): pl.pallas_call(functools.partial(ring_gather_kernel, count=count, axis=ax...  86.7 us
    pallas_call x1, Pallas kernels, kernel_reduce_scatter(): pl.pallas_call(functools.partial(ring_sum_kernel, count=count, axis=axis,...  52.2 us
    all_to_all x1, starting transfers between devices, local(): lax.all_to_all(outgoing, 'ctx', split_axis=0, concat_axis=0, tiled=True)  9.29 us
    all_to_all x1, waiting for transfers between devices, local(): lax.all_to_all(outgoing, 'ctx', split_axis=0, concat_axis=0, tiled=True)  8.55 us
    all_to_all x1, starting transfers between devices, local(): lax.all_to_all(jnp.broadcast_to(query_weight[None], (ctx_count,) + query_...  7 us
    ppermute x2, starting transfers between devices, shifted(): return lax.ppermute(block, axis, route)  5.61 us
  transfers between devices with their start and end apart: 5, of which 2 were waited for; matrix products, arithmetic and copies ran while one was open for 13% of the time, Pallas kernels for 38%

profile of v7, /device:TPU:24, one launch (start us, length us, event | category | flops | bytes accessed | tf_op | source)
XLA Modules:
  0.0 229.4 jit_solution(13380160359048596399)
XLA Ops:
  8.3 3.6 %gather_fusion = s32[512]{0:T(512)S(1)} fusion(s32[512]{0:T(512)} %param.17, s32[1024]{0:T(1024)S(1)} %pad_clamp_fusion.2), kind=kCustom, calls=%fused_computation | custom fusion | bytes 6144 | tf_op jit(solution)/shard_map/gather | solution.py:200
  13.9 9.3 %all-to-all-start = ((bf16[32,1,8,1024]{3,2,1,0:T(8,128)(2,1)}), bf16[32,1,8,1024]{3,2,1,0:T(8,128)(2,1)S(1)}, u32[]{:S(2)}, u32[]{:S(2)}) async-start(bf16[32,1,8,1024]{3,2,1,0:T(8,128)(2,1)} %bitcast_multiply_fusion), calls=%async_computation | async-start | bytes 1048576 | tf_op jit(solution)/shard_map/all_to_all | solution.py:211
  24.2 8.6 %all-to-all-done = bf16[32,1,8,1024]{3,2,1,0:T(8,128)(2,1)S(1)} async-done(((bf16[32,1,8,1024]{3,2,1,0:T(8,128)(2,1)}), bf16[32,1,8,1024]{3,2,1,0:T(8,128)(2,1)S(1)}, u32[]{:S(2)}, u32[]{:S(2)}) %all-to-all-start) | async-done | bytes 524320 | tf_op jit(solution)/shard_map/all_to_all | solution.py:211
  32.7 1.5 broadcast_in_dim.30
  34.3 7.0 %all-to-all-start.1 = ((bf16[32,128,256]{2,1,0:T(8,128)(2,1)}), bf16[32,128,256]{2,1,0:T(8,128)(2,1)}, u32[]{:S(2)}, u32[]{:S(2)}) async-start(bf16[32,128,256]{2,1,0:T(8,128)(2,1)} %broadcast_in_dim.30), calls=%async_computation.1 | async-start | bytes 4194304 | tf_op jit(solution)/shard_map/all_to_all | solution.py:191
  42.2 1.3 gather_fusion.2
  43.4 86.7 %shard_map.100 = bf16[16,16,8,1024]{3,2,1,0:T(8,128)(2,1)} custom-call(bf16[16,8,1024]{2,1,0:T(8,128)(2,1)} %gather_fusion.2), custom_call_target="tpu_custom_call" | custom-call | tf_op jit(solution)/shard_map/pallas_call | solution.py:75
  130.1 2.7 %copy.25 = bf16[16,16,8,1024]{3,2,1,0:T(8,128)(2,1)S(1)} copy(bf16[16,16,8,1024]{3,2,0,1:T(8,128)(2,1)} %bitcast.44) | data formatting | bytes 8388608 | tf_op jit(solution)/shard_map/transpose | solution.py:221
  132.9 1.3 convolution_convert_fusion.1
  134.2 1.9 collective-permute-start.1
  136.1 1.3 convolution_convert_fusion.2
  137.5 3.7 %collective-permute-start = (bf16[2,128,256]{2,1,0:T(8,128)(2,1)S(1)}, bf16[2,128,256]{2,1,0:T(8,128)(2,1)S(1)}, u32[]{:S(2)}, u32[]{:S(2)}) collective-permute-start(bf16[2,128,256]{2,1,0:T(8,128)(2,1)S(1)} %bitcast.52), channel_id=1, source_target_pairs={{0,16},{16,32},{32,48},{48,64},{64,80},{80,96},{96,112},{112,128},... | collective-permute-start | bytes 393224 | tf_op jit(solution)/shard_map/ppermute | solution.py:23
  141.2 1.4 collective-permute-done.1
  142.6 1.1 pad_maximum_fusion
  143.7 2.8 %reshape.191 = bf16[9,256,2,128]{3,2,1,0:T(2,128)(2,1)S(1)} reshape(bf16[18,128,256]{2,1,0:T(8,128)(2,1)} %pad_maximum_fusion) | data formatting | bytes 2359296 | tf_op jit(solution)/shard_map/reshape | solution.py:232
  146.5 2.4 %pad_maximum_fusion.1 = bf16[18,128,256]{2,1,0:T(8,128)(2,1)} fusion(bf16[16,128,256]{2,1,0:T(8,128)(2,1)} %bitcast.47, bf16[2,128,256]{2,1,0:T(8,128)(2,1)S(1)} %collective-permute-done), kind=kLoop, calls=%fused_computation.20 | loop fusion | flops 589824 | bytes 2359296 | tf_op jit(solution)/shard_map/concatenate | solution.py:231
  148.9 3.5 %reshape.187 = bf16[9,256,2,128]{3,2,1,0:T(2,128)(2,1)} reshape(bf16[18,128,256]{2,1,0:T(8,128)(2,1)} %pad_maximum_fusion.1) | data formatting | bytes 2359296 | tf_op jit(solution)/shard_map/reshape | solution.py:233
  152.4 3.1 %fusion = f32[512]{0:T(512)S(1)} fusion(bf16[512,4096]{1,0:T(8,128)(2,1)} %all-gather.2.cloned.1.call-done), kind=kLoop, calls=%fused_computation.5 | loop fusion | flops 6290944 | bytes 4196352 | tf_op jit(solution)/shard_map/reduce_sum | solution.py:187
  155.5 4.2 %fusion.11 = bf16[512,256]{1,0:T(8,128)(2,1)S(1)} fusion(bf16[4096,256]{1,0:T(8,128)(2,1)} %bitcast.13, bf16[512,4096]{1,0:T(8,128)(2,1)} %all-gather.2.cloned.1.call-done, f32[4096]{0:T(1024)S(1)} %copy-done.7, f32[512]{0:T(512)S(1)} %add_rsqrt_fusion), kind=kOutput, calls=%fused_computation.18 | convolution fusion | flops 1082392576 | bytes 6572032 | tf_op jit(solution)/shard_map/dot_general | solution.py:198
  160.6 1.7 reshape.189
  162.4 1.7 fusion.40
  165.4 3.2 %convolution_convert_fusion = bf16[512,4096]{1,0:T(8,128)(2,1)} fusion(bf16[256,4096]{1,0:T(8,128)(2,1)S(1)} %copy-done, bf16[576,256]{1,0:T(8,128)(2,1)S(1)} %bitcast.51, pred[512]{0:T(512)(128)(4,1)S(1)} %fusion.32), kind=kOutput, calls=%fused_computation.8 | convolution fusion | flops 1075970048 | bytes 6554112 | tf_op jit(solution)/shard_map/dot_general | solution.py:265
  168.6 52.2 %shard_map.101 = bf16[32,4096]{1,0:T(8,128)(2,1)} custom-call(bf16[16,32,4096]{2,1,0:T(8,128)(2,1)} %bitcast.43), custom_call_target="tpu_custom_call" | custom-call | tf_op jit(solution)/shard_map/pallas_call | solution.py:142
  220.8 1.7 copy.44
  (58 shorter events, 7.7 us)
Async XLA Ops:
  6.5 158.8 %copy-start = (bf16[256,4096]{1,0:T(8,128)(2,1)S(1)}, bf16[256,4096]{1,0:T(8,128)(2,1)}, u32[]{:S(2)}) copy-start(bf16[256,4096]{1,0:T(8,128)(2,1)} %param.15) | copy-start | bytes 6291460
  6.5 5.9 %copy-start.3 = (bf16[16,8,1024]{2,1,0:T(8,128)(2,1)S(1)}, bf16[16,8,1024]{2,1,0:T(8,128)(2,1)}, u32[]{:S(2)}) copy-start(bf16[16,8,1024]{2,1,0:T(8,128)(2,1)} %param.16) | copy-start | bytes 786436
  6.5 145.9 %all-gather.2.cloned.1.call-start = ((), (), s32[]{:S(2)}) async-start(), calls=%async_computation.2 | async-start | bytes 4456448 | tf_op jit(solution)/shard_map/all_gather | solution.py:185
  11.9 11.4 %copy-start.8 = (s32[256]{0:T(256)S(1)}, s32[256]{0:T(256)}, u32[]{:S(2)}) copy-start(s32[256]{0:T(256)} %param.19) | copy-start | bytes 3076
  11.9 20.8 %copy-start.4 = (bf16[128,256]{1,0:T(8,128)(2,1)S(1)}, bf16[128,256]{1,0:T(8,128)(2,1)}, u32[]{:S(2)}) copy-start(bf16[128,256]{1,0:T(8,128)(2,1)} %param.12) | copy-start | bytes 196612
  13.9 18.8 %all-to-all-start = ((bf16[32,1,8,1024]{3,2,1,0:T(8,128)(2,1)}), bf16[32,1,8,1024]{3,2,1,0:T(8,128)(2,1)S(1)}, u32[]{:S(2)}, u32[]{:S(2)}) async-start(bf16[32,1,8,1024]{3,2,1,0:T(8,128)(2,1)} %bitcast_multiply_fusion), calls=%async_computation | async-start | bytes 1048576 | tf_op jit(solution)/shard_map/all_to_all | solution.py:211
  34.3 121.3 %all-to-all-start.1 = ((bf16[32,128,256]{2,1,0:T(8,128)(2,1)}), bf16[32,128,256]{2,1,0:T(8,128)(2,1)}, u32[]{:S(2)}, u32[]{:S(2)}) async-start(bf16[32,128,256]{2,1,0:T(8,128)(2,1)} %broadcast_in_dim.30), calls=%async_computation.1 | async-start | bytes 4194304 | tf_op jit(solution)/shard_map/all_to_all | solution.py:191
  130.1 2.8 %copy-start.5 = (bf16[1024,256]{1,0:T(8,128)(2,1)S(1)}, bf16[1024,256]{1,0:T(8,128)(2,1)}, u32[]{:S(2)}) copy-start(bf16[1024,256]{1,0:T(8,128)(2,1)} %param.13) | copy-start | bytes 1572868
  132.9 3.2 %copy-start.6 = (bf16[1024,256]{1,0:T(8,128)(2,1)S(1)}, bf16[1024,256]{1,0:T(8,128)(2,1)}, u32[]{:S(2)}) copy-start(bf16[1024,256]{1,0:T(8,128)(2,1)} %param.14) | copy-start | bytes 1572868
  134.2 8.4 %collective-permute-start.1 = (bf16[2,128,256]{2,1,0:T(8,128)(2,1)S(1)}, bf16[2,128,256]{2,1,0:T(8,128)(2,1)S(1)}, u32[]{:S(2)}, u32[]{:S(2)}) collective-permute-start(bf16[2,128,256]{2,1,0:T(8,128)(2,1)S(1)} %bitcast.53), channel_id=1, source_target_pairs={{0,16},{16,32},{32,48},{48,64},{64,80},{80,96},{96,112},{112,128},... | collective-permute-start | bytes 393224 | tf_op jit(solution)/shard_map/ppermute | solution.py:23
  137.4 5.2 %copy-start.1 = (bf16[2048,256]{1,0:T(8,128)(2,1)}, bf16[2048,256]{1,0:T(8,128)(2,1)S(1)}, u32[]{:S(2)}) copy-start(bf16[2048,256]{1,0:T(8,128)(2,1)S(1)} %convolution_convert_fusion.2) | copy-start | bytes 3145732
  137.5 9.0 %collective-permute-start = (bf16[2,128,256]{2,1,0:T(8,128)(2,1)S(1)}, bf16[2,128,256]{2,1,0:T(8,128)(2,1)S(1)}, u32[]{:S(2)}, u32[]{:S(2)}) collective-permute-start(bf16[2,128,256]{2,1,0:T(8,128)(2,1)S(1)} %bitcast.52), channel_id=1, source_target_pairs={{0,16},{16,32},{32,48},{48,64},{64,80},{80,96},{96,112},{112,128},... | collective-permute-start | bytes 393224 | tf_op jit(solution)/shard_map/ppermute | solution.py:23
  152.4 3.1 %copy-start.7 = (f32[4096]{0:T(1024)S(1)}, f32[4096]{0:T(1024)}, u32[]{:S(2)}) copy-start(f32[4096]{0:T(1024)} %param.11) | copy-start | bytes 49156
  162.4 2.1 copy-start.2
Sparse Core Ops, SparseCore 0:
  9.4 125.5 all-gather.1

commit v8 on v7

--- a/solution.py
+++ b/solution.py
@@ -35,13 +35,13 @@
     return right, left
 
 
-def ring_gather_kernel(x_ref, o_ref, send_sem, recv_sem, *, count, axis, other, pieces):
+def ring_gather_kernel(x_ref, o_ref, send_sem, recv_sem, *, count, axis, other, pieces, view):
     me = lax.axis_index(axis)
     row = lax.axis_index(other)
     right, left = greet_neighbours(me, row, count)
     half = count // 2
     size = x_ref.shape[0] // pieces
-    o_ref[half] = x_ref[...]
+    view(o_ref, half, pl.ds(0, x_ref.shape[0]))[...] = x_ref[...]
     copies = {}
     for step in range(1, half + 1):
         for piece in range(pieces):
@@ -54,8 +54,8 @@
                 if step > 1:
                     copies[(step - 1, toward, piece)].wait_recv()
                 copy = pltpu.make_async_remote_copy(
-                    src_ref=x_ref.at[part] if step == 1 else o_ref.at[source, part],
-                    dst_ref=o_ref.at[slot, part],
+                    src_ref=x_ref.at[part] if step == 1 else view(o_ref, source, part),
+                    dst_ref=view(o_ref, slot, part),
                     send_sem=send_sem.at[slot, piece],
                     recv_sem=recv_sem.at[slot, piece],
                     device_id=(row, right if toward == 0 else left),
@@ -70,13 +70,22 @@
         copy.wait_send()
 
 
-def kernel_gather(block, axis, other, collective_id, pieces=4):
+def slot_stack(ref, slot, part):
+    return ref.at[part, slot]
+
+
+def slot_stripe(ref, slot, part):
+    width = ref.shape[1] // lax.axis_size("tp")
+    return ref.at[part, pl.ds(slot * width, width)]
+
+
+def kernel_gather(block, axis, other, collective_id, shape, view, pieces=4):
     count = lax.axis_size(axis)
     return pl.pallas_call(
         functools.partial(
-            ring_gather_kernel, count=count, axis=axis, other=other, pieces=pieces
+            ring_gather_kernel, count=count, axis=axis, other=other, pieces=pieces, view=view
         ),
-        out_shape=jax.ShapeDtypeStruct((count,) + block.shape, block.dtype),
+        out_shape=jax.ShapeDtypeStruct(shape, block.dtype),
         in_specs=[pl.BlockSpec(memory_space=pltpu.VMEM)],
         out_specs=pl.BlockSpec(memory_space=pltpu.VMEM),
         scratch_shapes=[
@@ -182,10 +191,16 @@
     head_width = query_weight.shape[1]
     head_count = head_width // HS
     slot_cap = -(-rows_dev // ctx_count)
-    whole = lax.all_gather(hidden, "tp", axis=1, tiled=True)
+    tp_count = lax.axis_size("tp")
+    tp_index = lax.axis_index("tp")
+    whole = kernel_gather(
+        hidden, "tp", "ctx", 2, (hidden.shape[0], tp_count * hidden.shape[1]), slot_stripe
+    )
+    rotation = ((tp_index - tp_count // 2) % tp_count) * hidden.shape[1]
+    gain = lax.dynamic_slice_in_dim(jnp.concatenate([norm_gain, norm_gain]), rotation, whole.shape[1])
     values_wide = whole.astype(jnp.float32)
     mean_square = jnp.mean(values_wide * values_wide, axis=1, keepdims=True)
-    normed = (values_wide * lax.rsqrt(mean_square + epsilon) * norm_gain[None, :]).astype(
+    normed = (values_wide * lax.rsqrt(mean_square + epsilon) * gain[None, :]).astype(
         jnp.bfloat16
     )
     query_full = lax.all_to_all(
@@ -195,6 +210,9 @@
         concat_axis=0,
         tiled=True,
     ).reshape(-1, query_weight.shape[1])
+    query_full = lax.dynamic_slice_in_dim(
+        jnp.concatenate([query_full, query_full]), rotation, query_full.shape[0]
+    )
     query_sum = jnp.dot(normed, query_full, preferred_element_type=jnp.float32)
     queries = (query_sum * HS ** (-0.5)).astype(jnp.bfloat16)
     storage = row_place[neighbour_ids.reshape(-1)].reshape(ctx_count, rows_dev)
@@ -218,9 +236,14 @@
     flat_index = own_sources * slot_cap + own_rank
     picked = incoming.reshape(ctx_count * slot_cap, slice_tokens, enc_width)[flat_index]
     row_total = picked.shape[0]
-    full_rows = jnp.swapaxes(kernel_gather(picked, "tp", "ctx", 0), 0, 1).reshape(
-        picked.shape[0], -1, picked.shape[2]
-    )
+    full_rows = kernel_gather(
+        picked,
+        "tp",
+        "ctx",
+        0,
+        (picked.shape[0], lax.axis_size("tp")) + picked.shape[1:],
+        slot_stack,
+    ).reshape(picked.shape[0], -1, picked.shape[2])
     keys = project_rows(full_rows, key_weight).reshape(row_total, -1, head_width)
     values = project_rows(full_rows, value_weight).reshape(row_total, -1, head_width)
     neighbour_len = keys.shape[1]

time: 230 us -> 241 us (1.048)
  Pallas kernels: 139 us -> 163 us
  between operations: 13.7 us -> 0.36 us
  local copies, waits for them, and re-layouts: 21.6 us -> 16.7 us
  matrix products: 12.1 us -> 15.2 us
    pallas_call x1 -> x2, Pallas kernels: 86.7 us -> 112 us  [kernel_gather(): pl.pallas_call(functools.partial(ring_gather_kernel, count=count, axis=ax...]
    transpose x1 -> x0, local copies, waits for them, and re-layouts: 2.73 us -> none  [local(): jnp.swapaxes(kernel_gather(picked, 'tp', 'ctx', 0), 0, 1)]
  transfers between devices with their start and end apart: 5 -> 4, of which waited for: 2 -> 3; matrix products, arithmetic and copies ran while one was open for 13% -> 8% of each run, Pallas kernels for 38% -> 47%
where the time goes in v8:
time: 241 us; the launch traced here: 240 us
  Pallas kernels  163 us (68%)
  starting transfers between devices  21.9 us (9%)
  local copies, waits for them, and re-layouts  16.7 us (7%)
  matrix products  15.2 us (6%)
  waiting for transfers between devices  12 us (5%)
  other arithmetic  10.6 us (4%)
    pallas_call x2, Pallas kernels, kernel_gather(): pl.pallas_call(functools.partial(ring_gather_kernel, count=count, axis=ax...  112 us
    pallas_call x1, Pallas kernels, kernel_reduce_scatter(): pl.pallas_call(functools.partial(ring_sum_kernel, count=count, axis=axis,...  50.7 us
    all_to_all x1, starting transfers between devices, local(): lax.all_to_all(outgoing, 'ctx', split_axis=0, concat_axis=0, tiled=True)  9.29 us
    all_to_all x1, waiting for transfers between devices, local(): lax.all_to_all(outgoing, 'ctx', split_axis=0, concat_axis=0, tiled=True)  8.54 us
    all_to_all x1, starting transfers between devices, local(): lax.all_to_all(jnp.broadcast_to(query_weight[None], (ctx_count,) + query_...  7 us
    ppermute x2, starting transfers between devices, shifted(): return lax.ppermute(block, axis, route)  5.59 us
    dot_general x1, matrix products, local(): query_sum = jnp.dot(normed, query_full, preferred_element_type=jnp.float32)  4.91 us
    dot_general x2, matrix products, project_rows(): jnp.dot(flat, weight, preferred_element_type=jnp.float32)  4.88 us
  transfers between devices with their start and end apart: 4, of which 3 were waited for; matrix products, arithmetic and copies ran while one was open for 8% of the time, Pallas kernels for 47%

profile of v8, /device:TPU:24, one launch (start us, length us, event | category | flops | bytes accessed | tf_op | source)
XLA Modules:
  0.0 239.7 jit_solution(15983020051156724025)
XLA Ops:
  1.1 3.6 %gather_fusion = s32[512]{0:T(512)S(1)} fusion(s32[512]{0:T(512)} %param.17, s32[1024]{0:T(1024)S(1)} %pad_clamp_fusion.2), kind=kCustom, calls=%fused_computation | custom fusion | bytes 6144 | tf_op jit(solution)/shard_map/gather | solution.py:218
  6.8 9.3 %all-to-all-start = ((bf16[32,1,8,1024]{3,2,1,0:T(8,128)(2,1)}), bf16[32,1,8,1024]{3,2,1,0:T(8,128)(2,1)S(1)}, u32[]{:S(2)}, u32[]{:S(2)}) async-start(bf16[32,1,8,1024]{3,2,1,0:T(8,128)(2,1)} %bitcast_multiply_fusion), calls=%async_computation | async-start | bytes 1048576 | tf_op jit(solution)/shard_map/all_to_all | solution.py:229
  17.1 8.5 %all-to-all-done = bf16[32,1,8,1024]{3,2,1,0:T(8,128)(2,1)S(1)} async-done(((bf16[32,1,8,1024]{3,2,1,0:T(8,128)(2,1)}), bf16[32,1,8,1024]{3,2,1,0:T(8,128)(2,1)S(1)}, u32[]{:S(2)}, u32[]{:S(2)}) %all-to-all-start) | async-done | bytes 524320 | tf_op jit(solution)/shard_map/all_to_all | solution.py:229
  25.6 1.5 broadcast_in_dim.30
  27.1 7.0 %all-to-all-start.1 = ((bf16[32,128,256]{2,1,0:T(8,128)(2,1)}), bf16[32,128,256]{2,1,0:T(8,128)(2,1)}, u32[]{:S(2)}, u32[]{:S(2)}) async-start(bf16[32,128,256]{2,1,0:T(8,128)(2,1)} %broadcast_in_dim.30), calls=%async_computation.1 | async-start | bytes 4194304 | tf_op jit(solution)/shard_map/all_to_all | solution.py:206
  34.9 59.2 %shard_map.101 = bf16[512,4096]{1,0:T(8,128)(2,1)} custom-call(bf16[512,256]{1,0:T(8,128)(2,1)} %x_ref.1), custom_call_target="tpu_custom_call" | custom-call | tf_op jit(solution)/shard_map/pallas_call | solution.py:84
  94.9 3.1 %fusion = f32[512]{0:T(512)S(1)} fusion(bf16[512,4096]{1,0:T(8,128)(2,1)} %shard_map.101), kind=kLoop, calls=%fused_computation.5 | loop fusion | flops 6290944 | bytes 4196352 | tf_op jit(solution)/shard_map/reduce_sum | solution.py:202
  98.6 1.3 gather_fusion.2
  99.9 53.1 %shard_map.100 = bf16[16,16,8,1024]{3,2,1,0:T(8,128)(2,1)} custom-call(bf16[16,8,1024]{2,1,0:T(8,128)(2,1)} %gather_fusion.2), custom_call_target="tpu_custom_call" | custom-call | tf_op jit(solution)/shard_map/pallas_call | solution.py:84
  153.0 3.6 %convolution_convert_fusion.2 = bf16[2048,256]{1,0:T(8,128)(2,1)S(1)} fusion(bf16[2048,1024]{1,0:T(8,128)(2,1)} %bitcast.42, bf16[1024,256]{1,0:T(8,128)(2,1)S(1)} %copy-done.9), kind=kOutput, calls=%fused_computation.15 | convolution fusion | flops 1074266112 | bytes 5767168 | tf_op jit(solution)/shard_map/dot_general | solution.py:169
  156.6 1.9 collective-permute-start
  158.5 1.3 convolution_convert_fusion.1
  159.9 3.7 %collective-permute-start.1 = (bf16[2,128,256]{2,1,0:T(8,128)(2,1)S(1)}, bf16[2,128,256]{2,1,0:T(8,128)(2,1)S(1)}, u32[]{:S(2)}, u32[]{:S(2)}) collective-permute-start(bf16[2,128,256]{2,1,0:T(8,128)(2,1)S(1)} %bitcast.49), channel_id=1, source_target_pairs={{0,16},{16,32},{32,48},{48,64},{64,80},{80,96},{96,112},{112,128},... | collective-permute-start | bytes 393224 | tf_op jit(solution)/shard_map/ppermute | solution.py:23
  163.5 1.4 collective-permute-done
  165.1 1.2 reshape.187
  166.3 2.0 collective-permute-done.1
  168.3 2.4 %pad_maximum_fusion = bf16[18,128,256]{2,1,0:T(8,128)(2,1)} fusion(bf16[16,128,256]{2,1,0:T(8,128)(2,1)} %bitcast.44, bf16[2,128,256]{2,1,0:T(8,128)(2,1)S(1)} %collective-permute-done.1), kind=kLoop, calls=%fused_computation.22 | loop fusion | flops 589824 | bytes 2359296 | tf_op jit(solution)/shard_map/concatenate | solution.py:253
  170.7 2.8 %reshape.191 = bf16[9,256,2,128]{3,2,1,0:T(2,128)(2,1)S(1)} reshape(bf16[18,128,256]{2,1,0:T(8,128)(2,1)} %pad_maximum_fusion) | data formatting | bytes 2359296 | tf_op jit(solution)/shard_map/reshape | solution.py:255
  173.5 4.9 %fusion.15 = bf16[512,256]{1,0:T(8,128)(2,1)S(1)} fusion(s32[]{:T(128)S(6)} %select_n.104, bf16[4096,256]{1,0:T(8,128)(2,1)} %bitcast.12, bf16[512,4096]{1,0:T(8,128)(2,1)} %shard_map.101, f32[4096]{0:T(1024)S(1)} %copy-done.7, f32[512]{0:T(512)S(1)} %copy-done.8), kind=kOutput, calls=%fused_computation.21 | convolution fusion | flops 1086586880 | bytes 6572036 | tf_op jit(solution)/shard_map/dot_general | solution.py:216
  179.3 1.7 reshape.189
  181.1 1.7 fusion.49
  184.0 3.2 %convolution_convert_fusion = bf16[512,4096]{1,0:T(8,128)(2,1)} fusion(bf16[256,4096]{1,0:T(8,128)(2,1)S(1)} %copy-done, bf16[576,256]{1,0:T(8,128)(2,1)S(1)} %bitcast.48, pred[512]{0:T(512)(128)(4,1)S(1)} %fusion.39), kind=kOutput, calls=%fused_computation.8 | convolution fusion | flops 1075970048 | bytes 6554112 | tf_op jit(solution)/shard_map/dot_general | solution.py:288
  187.3 50.7 %shard_map.102 = bf16[32,4096]{1,0:T(8,128)(2,1)} custom-call(bf16[16,32,4096]{2,1,0:T(8,128)(2,1)} %bitcast.41), custom_call_target="tpu_custom_call" | custom-call | tf_op jit(solution)/shard_map/pallas_call | solution.py:151
  238.0 1.7 copy.41
  (62 shorter events, 8.5 us)
Async XLA Ops:
  0.0 184.0 %copy-start = (bf16[256,4096]{1,0:T(8,128)(2,1)S(1)}, bf16[256,4096]{1,0:T(8,128)(2,1)}, u32[]{:S(2)}) copy-start(bf16[256,4096]{1,0:T(8,128)(2,1)} %param.15) | copy-start | bytes 6291460
  0.0 5.3 %copy-start.4 = (bf16[16,8,1024]{2,1,0:T(8,128)(2,1)S(1)}, bf16[16,8,1024]{2,1,0:T(8,128)(2,1)}, u32[]{:S(2)}) copy-start(bf16[16,8,1024]{2,1,0:T(8,128)(2,1)} %param.16) | copy-start | bytes 786436
  4.8 11.4 %copy-start.11 = (s32[256]{0:T(256)S(1)}, s32[256]{0:T(256)}, u32[]{:S(2)}) copy-start(s32[256]{0:T(256)} %param.19) | copy-start | bytes 3076
  4.8 20.8 %copy-start.5 = (bf16[128,256]{1,0:T(8,128)(2,1)S(1)}, bf16[128,256]{1,0:T(8,128)(2,1)}, u32[]{:S(2)}) copy-start(bf16[128,256]{1,0:T(8,128)(2,1)} %param.12) | copy-start | bytes 196612
  6.8 18.8 %all-to-all-start = ((bf16[32,1,8,1024]{3,2,1,0:T(8,128)(2,1)}), bf16[32,1,8,1024]{3,2,1,0:T(8,128)(2,1)S(1)}, u32[]{:S(2)}, u32[]{:S(2)}) async-start(bf16[32,1,8,1024]{3,2,1,0:T(8,128)(2,1)} %bitcast_multiply_fusion), calls=%async_computation | async-start | bytes 1048576 | tf_op jit(solution)/shard_map/all_to_all | solution.py:229
  27.1 146.3 %all-to-all-start.1 = ((bf16[32,128,256]{2,1,0:T(8,128)(2,1)}), bf16[32,128,256]{2,1,0:T(8,128)(2,1)}, u32[]{:S(2)}, u32[]{:S(2)}) async-start(bf16[32,128,256]{2,1,0:T(8,128)(2,1)} %broadcast_in_dim.30), calls=%async_computation.1 | async-start | bytes 4194304 | tf_op jit(solution)/shard_map/all_to_all | solution.py:206
  34.9 59.3 %copy-start.6 = (f32[4096]{0:T(1024)S(1)}, f32[4096]{0:T(1024)}, u32[]{:S(2)}) copy-start(f32[4096]{0:T(1024)} %param.11) | copy-start | bytes 49156
  99.9 53.1 %copy-start.9 = (bf16[1024,256]{1,0:T(8,128)(2,1)S(1)}, bf16[1024,256]{1,0:T(8,128)(2,1)}, u32[]{:S(2)}) copy-start(bf16[1024,256]{1,0:T(8,128)(2,1)} %param.14) | copy-start | bytes 1572868
  153.0 5.6 %copy-start.1 = (bf16[16,16,8,1024]{3,2,1,0:T(8,128)(2,1)S(1)}, bf16[16,16,8,1024]{3,2,1,0:T(8,128)(2,1)}, u32[]{:S(2)}) copy-start(bf16[16,16,8,1024]{3,2,1,0:T(8,128)(2,1)} %shard_map.100) | copy-start | bytes 12582916
  153.0 5.6 %copy-start.10 = (bf16[1024,256]{1,0:T(8,128)(2,1)S(1)}, bf16[1024,256]{1,0:T(8,128)(2,1)}, u32[]{:S(2)}) copy-start(bf16[1024,256]{1,0:T(8,128)(2,1)} %param.13) | copy-start | bytes 1572868
  156.6 8.4 %collective-permute-start = (bf16[2,128,256]{2,1,0:T(8,128)(2,1)S(1)}, bf16[2,128,256]{2,1,0:T(8,128)(2,1)S(1)}, u32[]{:S(2)}, u32[]{:S(2)}) collective-permute-start(bf16[2,128,256]{2,1,0:T(8,128)(2,1)S(1)} %bitcast.50), channel_id=1, source_target_pairs={{0,16},{16,32},{32,48},{48,64},{64,80},{80,96},{96,112},{112,128},... | collective-permute-start | bytes 393224 | tf_op jit(solution)/shard_map/ppermute | solution.py:23
  159.8 5.2 %copy-start.2 = (bf16[2048,256]{1,0:T(8,128)(2,1)}, bf16[2048,256]{1,0:T(8,128)(2,1)S(1)}, u32[]{:S(2)}) copy-start(bf16[2048,256]{1,0:T(8,128)(2,1)S(1)} %convolution_convert_fusion.1) | copy-start | bytes 3145732
  159.9 8.4 %collective-permute-start.1 = (bf16[2,128,256]{2,1,0:T(8,128)(2,1)S(1)}, bf16[2,128,256]{2,1,0:T(8,128)(2,1)S(1)}, u32[]{:S(2)}, u32[]{:S(2)}) collective-permute-start(bf16[2,128,256]{2,1,0:T(8,128)(2,1)S(1)} %bitcast.49), channel_id=1, source_target_pairs={{0,16},{16,32},{32,48},{48,64},{64,80},{80,96},{96,112},{112,128},... | collective-permute-start | bytes 393224 | tf_op jit(solution)/shard_map/ppermute | solution.py:23
  168.3 5.2 %copy-start.7 = (f32[4096]{0:T(1024)S(1)}, f32[4096]{0:T(1024)}, u32[]{:S(2)}) copy-start(f32[4096]{0:T(1024)} %fusion.33) | copy-start | bytes 49156
  168.3 5.2 %copy-start.8 = (f32[512]{0:T(512)S(1)}, f32[512]{0:T(512)}, u32[]{:S(2)}) copy-start(f32[512]{0:T(512)} %add_rsqrt_fusion) | copy-start | bytes 6148
  181.1 2.1 copy-start.3

commit v9 on v8

--- a/solution.py
+++ b/solution.py
@@ -72,11 +72,6 @@
 
 def slot_stack(ref, slot, part):
     return ref.at[part, slot]
-
-
-def slot_stripe(ref, slot, part):
-    width = ref.shape[1] // lax.axis_size("tp")
-    return ref.at[part, pl.ds(slot * width, width)]
 
 
 def kernel_gather(block, axis, other, collective_id, shape, view, pieces=4):
@@ -191,16 +186,10 @@
     head_width = query_weight.shape[1]
     head_count = head_width // HS
     slot_cap = -(-rows_dev // ctx_count)
-    tp_count = lax.axis_size("tp")
-    tp_index = lax.axis_index("tp")
-    whole = kernel_gather(
-        hidden, "tp", "ctx", 2, (hidden.shape[0], tp_count * hidden.shape[1]), slot_stripe
-    )
-    rotation = ((tp_index - tp_count // 2) % tp_count) * hidden.shape[1]
-    gain = lax.dynamic_slice_in_dim(jnp.concatenate([norm_gain, norm_gain]), rotation, whole.shape[1])
+    whole = lax.all_gather(hidden, "tp", axis=1, tiled=True)
     values_wide = whole.astype(jnp.float32)
     mean_square = jnp.mean(values_wide * values_wide, axis=1, keepdims=True)
-    normed = (values_wide * lax.rsqrt(mean_square + epsilon) * gain[None, :]).astype(
+    normed = (values_wide * lax.rsqrt(mean_square + epsilon) * norm_gain[None, :]).astype(
         jnp.bfloat16
     )
     query_full = lax.all_to_all(
@@ -210,9 +199,6 @@
         concat_axis=0,
         tiled=True,
     ).reshape(-1, query_weight.shape[1])
-    query_full = lax.dynamic_slice_in_dim(
-        jnp.concatenate([query_full, query_full]), rotation, query_full.shape[0]
-    )
     query_sum = jnp.dot(normed, query_full, preferred_element_type=jnp.float32)
     queries = (query_sum * HS ** (-0.5)).astype(jnp.bfloat16)
     storage = row_place[neighbour_ids.reshape(-1)].reshape(ctx_count, rows_dev)
@@ -243,6 +229,7 @@
         0,
         (picked.shape[0], lax.axis_size("tp")) + picked.shape[1:],
         slot_stack,
+        pieces=8,
     ).reshape(picked.shape[0], -1, picked.shape[2])
     keys = project_rows(full_rows, key_weight).reshape(row_total, -1, head_width)
     values = project_rows(full_rows, value_weight).reshape(row_total, -1, head_width)
@@ -288,7 +275,7 @@
     mixed_part = jnp.dot(attended, out_weight, preferred_element_type=jnp.float32).astype(
         jnp.bfloat16
     )
-    return kernel_reduce_scatter(mixed_part, "tp", "ctx", 1)
+    return kernel_reduce_scatter(mixed_part, "tp", "ctx", 1, pieces=8)
 
 
 def solution(mesh):

time: 241 us -> 233 us (0.967)
  Pallas kernels: 163 us -> 142 us
  between operations: 0.36 us -> 13.7 us
    pallas_call x2 -> x1, Pallas kernels: 112 us -> 88.2 us  [kernel_gather(): pl.pallas_call(functools.partial(ring_gather_kernel, count=count, axis=ax...]
    pallas_call x1, Pallas kernels: 50.7 us -> 53.5 us  [kernel_reduce_scatter(): pl.pallas_call(functools.partial(ring_sum_kernel, count=count, axis=axis,...]
  transfers between devices with their start and end apart: 4 -> 5, of which waited for: 3 -> 2; matrix products, arithmetic and copies ran while one was open for 8% -> 12% of each run, Pallas kernels for 47% -> 38%
where the time goes in v9:
time: 233 us; the launch traced here: 232 us
  Pallas kernels  142 us (61%)
  starting transfers between devices  21.9 us (9%)
  local copies, waits for them, and re-layouts  18.9 us (8%)
  matrix products  14.4 us (6%)
  between operations  13.7 us (6%)
  waiting for transfers between devices  10.7 us (5%)
  other arithmetic  10.3 us (4%)
    pallas_call x1, Pallas kernels, kernel_gather(): pl.pallas_call(functools.partial(ring_gather_kernel, count=count, axis=ax...  88.2 us
    pallas_call x1, Pallas kernels, kernel_reduce_scatter(): pl.pallas_call(functools.partial(ring_sum_kernel, count=count, axis=axis,...  53.5 us
    all_to_all x1, starting transfers between devices, local(): lax.all_to_all(outgoing, 'ctx', split_axis=0, concat_axis=0, tiled=True)  9.29 us
    all_to_all x1, waiting for transfers between devices, local(): lax.all_to_all(outgoing, 'ctx', split_axis=0, concat_axis=0, tiled=True)  8.55 us
    all_to_all x1, starting transfers between devices, local(): lax.all_to_all(jnp.broadcast_to(query_weight[None], (ctx_count,) + query_...  7 us
    ppermute x2, starting transfers between devices, shifted(): return lax.ppermute(block, axis, route)  5.59 us
    dot_general x2, matrix products, project_rows(): jnp.dot(flat, weight, preferred_element_type=jnp.float32)  4.88 us
  transfers between devices with their start and end apart: 5, of which 2 were waited for; matrix products, arithmetic and copies ran while one was open for 12% of the time, Pallas kernels for 38%

profile of v9, /device:TPU:24, one launch (start us, length us, event | category | flops | bytes accessed | tf_op | source)
XLA Modules:
  0.0 231.6 jit_solution(1751429321667772195)
XLA Ops:
  8.3 3.6 %gather_fusion = s32[512]{0:T(512)S(1)} fusion(s32[512]{0:T(512)} %param.17, s32[1024]{0:T(1024)S(1)} %pad_clamp_fusion.2), kind=kCustom, calls=%fused_computation | custom fusion | bytes 6144 | tf_op jit(solution)/shard_map/gather | solution.py:204
  13.9 9.3 %all-to-all-start = ((bf16[32,1,8,1024]{3,2,1,0:T(8,128)(2,1)}), bf16[32,1,8,1024]{3,2,1,0:T(8,128)(2,1)S(1)}, u32[]{:S(2)}, u32[]{:S(2)}) async-start(bf16[32,1,8,1024]{3,2,1,0:T(8,128)(2,1)} %bitcast_multiply_fusion), calls=%async_computation | async-start | bytes 1048576 | tf_op jit(solution)/shard_map/all_to_all | solution.py:215
  24.2 8.6 %all-to-all-done = bf16[32,1,8,1024]{3,2,1,0:T(8,128)(2,1)S(1)} async-done(((bf16[32,1,8,1024]{3,2,1,0:T(8,128)(2,1)}), bf16[32,1,8,1024]{3,2,1,0:T(8,128)(2,1)S(1)}, u32[]{:S(2)}, u32[]{:S(2)}) %all-to-all-start) | async-done | bytes 524320 | tf_op jit(solution)/shard_map/all_to_all | solution.py:215
  32.7 1.5 broadcast_in_dim.30
  34.3 7.0 %all-to-all-start.1 = ((bf16[32,128,256]{2,1,0:T(8,128)(2,1)}), bf16[32,128,256]{2,1,0:T(8,128)(2,1)}, u32[]{:S(2)}, u32[]{:S(2)}) async-start(bf16[32,128,256]{2,1,0:T(8,128)(2,1)} %broadcast_in_dim.30), calls=%async_computation.1 | async-start | bytes 4194304 | tf_op jit(solution)/shard_map/all_to_all | solution.py:195
  42.2 1.3 gather_fusion.2
  43.4 88.2 %shard_map.100 = bf16[16,16,8,1024]{3,2,1,0:T(8,128)(2,1)} custom-call(bf16[16,8,1024]{2,1,0:T(8,128)(2,1)} %gather_fusion.2), custom_call_target="tpu_custom_call" | custom-call | tf_op jit(solution)/shard_map/pallas_call | solution.py:79
  131.6 3.6 %convolution_convert_fusion.1 = bf16[2048,256]{1,0:T(8,128)(2,1)S(1)} fusion(bf16[2048,1024]{1,0:T(8,128)(2,1)} %bitcast.43, bf16[1024,256]{1,0:T(8,128)(2,1)S(1)} %copy-done.6), kind=kOutput, calls=%fused_computation.12 | convolution fusion | flops 1074266112 | bytes 5767168 | tf_op jit(solution)/shard_map/dot_general | solution.py:164
  135.2 1.9 collective-permute-start.1
  137.2 1.3 convolution_convert_fusion.2
  138.5 3.7 %collective-permute-start = (bf16[2,128,256]{2,1,0:T(8,128)(2,1)S(1)}, bf16[2,128,256]{2,1,0:T(8,128)(2,1)S(1)}, u32[]{:S(2)}, u32[]{:S(2)}) collective-permute-start(bf16[2,128,256]{2,1,0:T(8,128)(2,1)S(1)} %bitcast.50), channel_id=1, source_target_pairs={{0,16},{16,32},{32,48},{48,64},{64,80},{80,96},{96,112},{112,128},... | collective-permute-start | bytes 393224 | tf_op jit(solution)/shard_map/ppermute | solution.py:23
  142.2 1.5 collective-permute-done.1
  143.6 1.1 pad_maximum_fusion
  144.8 2.8 %reshape.191 = bf16[9,256,2,128]{3,2,1,0:T(2,128)(2,1)S(1)} reshape(bf16[18,128,256]{2,1,0:T(8,128)(2,1)} %pad_maximum_fusion) | data formatting | bytes 2359296 | tf_op jit(solution)/shard_map/reshape | solution.py:242
  147.5 2.4 %pad_maximum_fusion.1 = bf16[18,128,256]{2,1,0:T(8,128)(2,1)} fusion(bf16[16,128,256]{2,1,0:T(8,128)(2,1)} %bitcast.45, bf16[2,128,256]{2,1,0:T(8,128)(2,1)S(1)} %collective-permute-done), kind=kLoop, calls=%fused_computation.20 | loop fusion | flops 589824 | bytes 2359296 | tf_op jit(solution)/shard_map/concatenate | solution.py:241
  149.9 3.5 %reshape.187 = bf16[9,256,2,128]{3,2,1,0:T(2,128)(2,1)} reshape(bf16[18,128,256]{2,1,0:T(8,128)(2,1)} %pad_maximum_fusion.1) | data formatting | bytes 2359296 | tf_op jit(solution)/shard_map/reshape | solution.py:243
  153.4 3.1 %fusion = f32[512]{0:T(512)S(1)} fusion(bf16[512,4096]{1,0:T(8,128)(2,1)} %all-gather.2.cloned.1.call-done), kind=kLoop, calls=%fused_computation.5 | loop fusion | flops 6290944 | bytes 4196352 | tf_op jit(solution)/shard_map/reduce_sum | solution.py:191
  156.6 4.2 %fusion.11 = bf16[512,256]{1,0:T(8,128)(2,1)S(1)} fusion(bf16[4096,256]{1,0:T(8,128)(2,1)} %bitcast.12, bf16[512,4096]{1,0:T(8,128)(2,1)} %all-gather.2.cloned.1.call-done, f32[4096]{0:T(1024)S(1)} %copy-done.8, f32[512]{0:T(512)S(1)} %add_rsqrt_fusion), kind=kOutput, calls=%fused_computation.18 | convolution fusion | flops 1082392576 | bytes 6572032 | tf_op jit(solution)/shard_map/dot_general | solution.py:202
  160.7 0.9 maximum_maximum_fusion
  161.7 1.7 reshape.189
  163.4 1.7 fusion.40
  166.4 3.2 %convolution_convert_fusion = bf16[512,4096]{1,0:T(8,128)(2,1)} fusion(bf16[256,4096]{1,0:T(8,128)(2,1)S(1)} %copy-done, bf16[576,256]{1,0:T(8,128)(2,1)S(1)} %bitcast.49, pred[512]{0:T(512)(128)(4,1)S(1)} %fusion.32), kind=kOutput, calls=%fused_computation.8 | convolution fusion | flops 1075970048 | bytes 6554112 | tf_op jit(solution)/shard_map/dot_general | solution.py:275
  169.6 53.5 %shard_map.101 = bf16[32,4096]{1,0:T(8,128)(2,1)} custom-call(bf16[16,32,4096]{2,1,0:T(8,128)(2,1)} %bitcast.42), custom_call_target="tpu_custom_call" | custom-call | tf_op jit(solution)/shard_map/pallas_call | solution.py:146
  223.1 1.7 copy.41
  (59 shorter events, 6.8 us)
Async XLA Ops:
  6.5 159.8 %copy-start = (bf16[256,4096]{1,0:T(8,128)(2,1)S(1)}, bf16[256,4096]{1,0:T(8,128)(2,1)}, u32[]{:S(2)}) copy-start(bf16[256,4096]{1,0:T(8,128)(2,1)} %param.15) | copy-start | bytes 6291460
  6.5 5.9 %copy-start.4 = (bf16[16,8,1024]{2,1,0:T(8,128)(2,1)S(1)}, bf16[16,8,1024]{2,1,0:T(8,128)(2,1)}, u32[]{:S(2)}) copy-start(bf16[16,8,1024]{2,1,0:T(8,128)(2,1)} %param.16) | copy-start | bytes 786436
  6.5 146.9 %all-gather.2.cloned.1.call-start = ((), (), s32[]{:S(2)}) async-start(), calls=%async_computation.2 | async-start | bytes 4456448 | tf_op jit(solution)/shard_map/all_gather | solution.py:189
  11.9 11.4 %copy-start.9 = (s32[256]{0:T(256)S(1)}, s32[256]{0:T(256)}, u32[]{:S(2)}) copy-start(s32[256]{0:T(256)} %param.19) | copy-start | bytes 3076
  11.9 20.8 %copy-start.5 = (bf16[128,256]{1,0:T(8,128)(2,1)S(1)}, bf16[128,256]{1,0:T(8,128)(2,1)}, u32[]{:S(2)}) copy-start(bf16[128,256]{1,0:T(8,128)(2,1)} %param.12) | copy-start | bytes 196612
  13.9 18.8 %all-to-all-start = ((bf16[32,1,8,1024]{3,2,1,0:T(8,128)(2,1)}), bf16[32,1,8,1024]{3,2,1,0:T(8,128)(2,1)S(1)}, u32[]{:S(2)}, u32[]{:S(2)}) async-start(bf16[32,1,8,1024]{3,2,1,0:T(8,128)(2,1)} %bitcast_multiply_fusion), calls=%async_computation | async-start | bytes 1048576 | tf_op jit(solution)/shard_map/all_to_all | solution.py:215
  34.3 122.3 %all-to-all-start.1 = ((bf16[32,128,256]{2,1,0:T(8,128)(2,1)}), bf16[32,128,256]{2,1,0:T(8,128)(2,1)}, u32[]{:S(2)}, u32[]{:S(2)}) async-start(bf16[32,128,256]{2,1,0:T(8,128)(2,1)} %broadcast_in_dim.30), calls=%async_computation.1 | async-start | bytes 4194304 | tf_op jit(solution)/shard_map/all_to_all | solution.py:195
  43.4 88.2 %copy-start.6 = (bf16[1024,256]{1,0:T(8,128)(2,1)S(1)}, bf16[1024,256]{1,0:T(8,128)(2,1)}, u32[]{:S(2)}) copy-start(bf16[1024,256]{1,0:T(8,128)(2,1)} %param.13) | copy-start | bytes 1572868
  131.6 5.6 %copy-start.1 = (bf16[16,16,8,1024]{3,2,1,0:T(8,128)(2,1)S(1)}, bf16[16,16,8,1024]{3,2,1,0:T(8,128)(2,1)}, u32[]{:S(2)}) copy-start(bf16[16,16,8,1024]{3,2,1,0:T(8,128)(2,1)} %shard_map.100) | copy-start | bytes 12582916
  131.6 5.6 %copy-start.7 = (bf16[1024,256]{1,0:T(8,128)(2,1)S(1)}, bf16[1024,256]{1,0:T(8,128)(2,1)}, u32[]{:S(2)}) copy-start(bf16[1024,256]{1,0:T(8,128)(2,1)} %param.14) | copy-start | bytes 1572868
  135.2 8.4 %collective-permute-start.1 = (bf16[2,128,256]{2,1,0:T(8,128)(2,1)S(1)}, bf16[2,128,256]{2,1,0:T(8,128)(2,1)S(1)}, u32[]{:S(2)}, u32[]{:S(2)}) collective-permute-start(bf16[2,128,256]{2,1,0:T(8,128)(2,1)S(1)} %bitcast.51), channel_id=1, source_target_pairs={{0,16},{16,32},{32,48},{48,64},{64,80},{80,96},{96,112},{112,128},... | collective-permute-start | bytes 393224 | tf_op jit(solution)/shard_map/ppermute | solution.py:23
  138.5 5.2 %copy-start.2 = (bf16[2048,256]{1,0:T(8,128)(2,1)}, bf16[2048,256]{1,0:T(8,128)(2,1)S(1)}, u32[]{:S(2)}) copy-start(bf16[2048,256]{1,0:T(8,128)(2,1)S(1)} %convolution_convert_fusion.2) | copy-start | bytes 3145732
  138.5 9.0 %collective-permute-start = (bf16[2,128,256]{2,1,0:T(8,128)(2,1)S(1)}, bf16[2,128,256]{2,1,0:T(8,128)(2,1)S(1)}, u32[]{:S(2)}, u32[]{:S(2)}) collective-permute-start(bf16[2,128,256]{2,1,0:T(8,128)(2,1)S(1)} %bitcast.50), channel_id=1, source_target_pairs={{0,16},{16,32},{32,48},{48,64},{64,80},{80,96},{96,112},{112,128},... | collective-permute-start | bytes 393224 | tf_op jit(solution)/shard_map/ppermute | solution.py:23
  153.4 3.1 %copy-start.8 = (f32[4096]{0:T(1024)S(1)}, f32[4096]{0:T(1024)}, u32[]{:S(2)}) copy-start(f32[4096]{0:T(1024)} %param.11) | copy-start | bytes 49156
  163.4 2.1 copy-start.3
Sparse Core Ops, SparseCore 0:
  9.4 125.3 all-gather.1

commit v10 on v7

--- a/solution.py
+++ b/solution.py
@@ -224,13 +224,15 @@
     keys = project_rows(full_rows, key_weight).reshape(row_total, -1, head_width)
     values = project_rows(full_rows, value_weight).reshape(row_total, -1, head_width)
     neighbour_len = keys.shape[1]
-    prior_keys, prior_values = shifted(
-        (keys[row_total - KNB :], values[row_total - KNB :]), "ctx", 1
-    )
-    key_stack = jnp.concatenate([prior_keys, keys], axis=0)
-    value_stack = jnp.concatenate([prior_values, values], axis=0)
-    key_blocks = key_stack.reshape(span_dev + 1, KNB * neighbour_len, head_count, HS)
-    value_blocks = value_stack.reshape(span_dev + 1, KNB * neighbour_len, head_count, HS)
+    prior = shifted(
+        jnp.stack([keys[row_total - KNB :], values[row_total - KNB :]]), "ctx", 1
+    )
+    key_blocks = jnp.concatenate([prior[0], keys], axis=0).reshape(
+        span_dev + 1, KNB * neighbour_len, head_width
+    )
+    value_blocks = jnp.concatenate([prior[1], values], axis=0).reshape(
+        span_dev + 1, KNB * neighbour_len, head_width
+    )
     first_span = ctx_index * span_dev
     local_counts = lax.dynamic_slice_in_dim(neighbour_counts, first_span, span_dev)
     prior_count = lax.dynamic_slice_in_dim(neighbour_counts, jnp.maximum(first_span - 1, 0), 1)
@@ -243,21 +245,28 @@
         ],
         axis=0,
     )
-    query_blocks = padded.reshape(span_dev + 1, CH, head_count, HS)
-    scores = jnp.einsum(
-        "wqhd,wkhd->whqk", query_blocks, key_blocks, preferred_element_type=jnp.float32
-    )
+    query_blocks = padded.reshape(span_dev + 1, CH, head_width)
     slot_of_key = jnp.arange(KNB * neighbour_len) // neighbour_len
     live = slot_of_key[None, :] < block_counts[:, None]
-    scores = jnp.where(live[:, None, None, :], scores, masked_score)
-    peak = jnp.max(scores, axis=3, keepdims=True)
-    expos = jnp.exp(scores - peak)
-    total = jnp.sum(expos, axis=3)
-    weights = expos.astype(jnp.bfloat16)
-    blended = jnp.einsum(
-        "whqk,wkhd->wqhd", weights, value_blocks, preferred_element_type=jnp.float32
-    )
-    blended = blended / jnp.swapaxes(total, 1, 2)[:, :, :, None]
+    heads = []
+    for head in range(head_count):
+        lanes = slice(head * HS, (head + 1) * HS)
+        scores = jnp.einsum(
+            "wqd,wkd->wqk",
+            query_blocks[:, :, lanes],
+            key_blocks[:, :, lanes],
+            preferred_element_type=jnp.float32,
+        )
+        scores = jnp.where(live[:, None, :], scores, masked_score)
+        peak = jnp.max(scores, axis=2, keepdims=True)
+        expos = jnp.exp(scores - peak)
+        total = jnp.sum(expos, axis=2, keepdims=True)
+        weights = expos.astype(jnp.bfloat16)
+        blended = jnp.einsum(
+            "wqk,wkd->wqd", weights, value_blocks[:, :, lanes], preferred_element_type=jnp.float32
+        )
+        heads.append(blended / total)
+    blended = jnp.concatenate(heads, axis=2)
     blended = blended.reshape((span_dev + 1) * CH, head_width)[1 : tok_dev + 1]
     position = ctx_index * tok_dev + jnp.arange(tok_dev)
     valid = position % LENGTH >= CH - 1

time: 230 us -> 219 us (0.952)
  local copies, waits for them, and re-layouts: 21.6 us -> 13.3 us
  waiting for transfers between devices: 10.7 us -> 16.1 us
  starting transfers between devices: 21.9 us -> 18.4 us
  other arithmetic: 10.3 us -> 7.5 us
    reshape x3 -> x0, local copies, waits for them, and re-layouts: 8.03 us -> none  [the longest x1 3.53 us: local(): value_stack.reshape(span_dev + 1, KNB * neighbour_len, head_count, HS)]
    ppermute x2 -> x1, waiting for transfers between devices: 1.44 us -> 6.85 us  [shifted(): return lax.ppermute(block, axis, route)]
    ppermute x2 -> x1, starting transfers between devices: 5.61 us -> 2.1 us  [shifted(): return lax.ppermute(block, axis, route)]
  transfers between devices with their start and end apart: 5 -> 4, of which waited for: 2 -> 2; matrix products, arithmetic and copies ran while one was open for 13% -> 10% of each run, Pallas kernels for 38% -> 40%
where the time goes in v10:
time: 219 us; the launch traced here: 218 us
  Pallas kernels  137 us (63%)
  starting transfers between devices  18.4 us (8%)
  waiting for transfers between devices  16.1 us (7%)
  between operations  13.7 us (6%)
  local copies, waits for them, and re-layouts  13.3 us (6%)
  matrix products  11.4 us (5%)
  other arithmetic  7.5 us (3%)
    pallas_call x1, Pallas kernels, kernel_gather(): pl.pallas_call(functools.partial(ring_gather_kernel, count=count, axis=ax...  86.6 us
    pallas_call x1, Pallas kernels, kernel_reduce_scatter(): pl.pallas_call(functools.partial(ring_sum_kernel, count=count, axis=axis,...  50.5 us
    all_to_all x1, starting transfers between devices, local(): lax.all_to_all(outgoing, 'ctx', split_axis=0, concat_axis=0, tiled=True)  9.29 us
    all_to_all x1, waiting for transfers between devices, local(): lax.all_to_all(outgoing, 'ctx', split_axis=0, concat_axis=0, tiled=True)  8.51 us
    all_to_all x1, starting transfers between devices, local(): lax.all_to_all(jnp.broadcast_to(query_weight[None], (ctx_count,) + query_...  7 us
    ppermute x1, waiting for transfers between devices, shifted(): return lax.ppermute(block, axis, route)  6.85 us
  transfers between devices with their start and end apart: 4, of which 2 were waited for; matrix products, arithmetic and copies ran while one was open for 10% of the time, Pallas kernels for 40%

profile of v10, /device:TPU:24, one launch (start us, length us, event | category | flops | bytes accessed | tf_op | source)
XLA Modules:
  0.0 217.5 jit_solution(6296475215799741866)
XLA Ops:
  6.5 0.7 all-gather.2.cloned.1.call-update
  7.3 0.8 copy.15
  8.3 3.6 %gather_fusion = s32[512]{0:T(512)S(1)} fusion(s32[512]{0:T(512)} %param.17, s32[1024]{0:T(1024)S(1)} %pad_clamp_fusion.2), kind=kCustom, calls=%fused_computation | custom fusion | bytes 6144 | tf_op jit(solution)/shard_map/gather | solution.py:200
  12.5 0.6 gather_fusion.1
  13.0 0.9 bitcast_multiply_fusion
  13.9 9.3 %all-to-all-start.1 = ((bf16[32,1,8,1024]{3,2,1,0:T(8,128)(2,1)}), bf16[32,1,8,1024]{3,2,1,0:T(8,128)(2,1)S(1)}, u32[]{:S(2)}, u32[]{:S(2)}) async-start(bf16[32,1,8,1024]{3,2,1,0:T(8,128)(2,1)} %bitcast_multiply_fusion), calls=%async_computation.1 | async-start | bytes 1048576 | tf_op jit(solution)/shard_map/all_to_all | solution.py:211
  23.3 0.6 dynamic_slice.10
  24.2 8.5 %all-to-all-done.1 = bf16[32,1,8,1024]{3,2,1,0:T(8,128)(2,1)S(1)} async-done(((bf16[32,1,8,1024]{3,2,1,0:T(8,128)(2,1)}), bf16[32,1,8,1024]{3,2,1,0:T(8,128)(2,1)S(1)}, u32[]{:S(2)}, u32[]{:S(2)}) %all-to-all-start.1) | async-done | bytes 524320 | tf_op jit(solution)/shard_map/all_to_all | solution.py:211
  32.7 1.5 broadcast_in_dim.34
  34.2 7.0 %all-to-all-start = ((bf16[32,128,256]{2,1,0:T(8,128)(2,1)}), bf16[32,128,256]{2,1,0:T(8,128)(2,1)}, u32[]{:S(2)}, u32[]{:S(2)}) async-start(bf16[32,128,256]{2,1,0:T(8,128)(2,1)} %broadcast_in_dim.34), calls=%async_computation | async-start | bytes 4194304 | tf_op jit(solution)/shard_map/all_to_all | solution.py:191
  41.2 1.3 gather_fusion.2
  42.5 86.6 %shard_map.100 = bf16[16,16,8,1024]{3,2,1,0:T(8,128)(2,1)} custom-call(bf16[16,8,1024]{2,1,0:T(8,128)(2,1)} %gather_fusion.2), custom_call_target="tpu_custom_call" | custom-call | tf_op jit(solution)/shard_map/pallas_call | solution.py:75
  129.1 2.7 %copy.16 = bf16[16,16,8,1024]{3,2,1,0:T(8,128)(2,1)S(1)} copy(bf16[16,16,8,1024]{3,2,0,1:T(8,128)(2,1)} %bitcast.42) | data formatting | bytes 8388608 | tf_op jit(solution)/shard_map/transpose | solution.py:221
  131.9 1.3 convolution_convert_fusion.2
  133.2 1.3 convolution_convert_fusion.1
  134.5 2.1 collective-permute-start
  136.6 0.7 pad_add_fusion
  137.5 6.9 %collective-permute-done = bf16[2,2,128,256]{3,2,1,0:T(8,128)(2,1)S(1)} collective-permute-done((bf16[2,2,128,256]{3,2,1,0:T(8,128)(2,1)S(1)}, bf16[2,2,128,256]{3,2,1,0:T(8,128)(2,1)S(1)}, u32[]{:S(2)}, u32[]{:S(2)}) %collective-permute-start) | collective-permute-done | bytes 262176 | tf_op jit(solution)/shard_map/ppermute | solution.py:23
  144.5 1.1 pad_maximum_fusion.1
  145.6 3.1 %fusion = f32[512]{0:T(512)S(1)} fusion(bf16[512,4096]{1,0:T(8,128)(2,1)} %all-gather.2.cloned.1.call-done), kind=kLoop, calls=%fused_computation.5 | loop fusion | flops 6290944 | bytes 4196352 | tf_op jit(solution)/shard_map/reduce_sum | solution.py:187
  148.7 4.2 %fusion.10 = bf16[512,256]{1,0:T(8,128)(2,1)S(1)} fusion(bf16[4096,256]{1,0:T(8,128)(2,1)} %bitcast, bf16[512,4096]{1,0:T(8,128)(2,1)} %all-gather.2.cloned.1.call-done, f32[4096]{0:T(1024)S(1)} %copy-done.6, f32[512]{0:T(512)S(1)} %add_rsqrt_fusion), kind=kOutput, calls=%fused_computation.17 | convolution fusion | flops 1082392576 | bytes 6572032 | tf_op jit(solution)/shard_map/dot_general | solution.py:198
  155.2 3.2 %convolution_convert_fusion = bf16[512,4096]{1,0:T(8,128)(2,1)} fusion(bf16[256,4096]{1,0:T(8,128)(2,1)S(1)} %copy-done, bf16[576,256]{1,0:T(8,128)(2,1)S(1)} %bitcast.54, pred[512]{0:T(512)(128)(4,1)S(1)} %fusion.38), kind=kOutput, calls=%fused_computation.8 | convolution fusion | flops 1075970048 | bytes 6554112 | tf_op jit(solution)/shard_map/dot_general | solution.py:274
  158.4 50.5 %shard_map.101 = bf16[32,4096]{1,0:T(8,128)(2,1)} custom-call(bf16[16,32,4096]{2,1,0:T(8,128)(2,1)} %bitcast.41), custom_call_target="tpu_custom_call" | custom-call | tf_op jit(solution)/shard_map/pallas_call | solution.py:142
  209.0 1.7 copy.18
  (55 shorter events, 3.6 us)
Async XLA Ops:
  6.5 148.7 %copy-start = (bf16[256,4096]{1,0:T(8,128)(2,1)S(1)}, bf16[256,4096]{1,0:T(8,128)(2,1)}, u32[]{:S(2)}) copy-start(bf16[256,4096]{1,0:T(8,128)(2,1)} %param.15) | copy-start | bytes 6291460
  6.5 5.9 %copy-start.2 = (bf16[16,8,1024]{2,1,0:T(8,128)(2,1)S(1)}, bf16[16,8,1024]{2,1,0:T(8,128)(2,1)}, u32[]{:S(2)}) copy-start(bf16[16,8,1024]{2,1,0:T(8,128)(2,1)} %param.16) | copy-start | bytes 786436
  6.5 139.0 %all-gather.2.cloned.1.call-start = ((), (), s32[]{:S(2)}) async-start(), calls=%async_computation.2 | async-start | bytes 4456448 | tf_op jit(solution)/shard_map/all_gather | solution.py:185
  11.9 11.4 %copy-start.7 = (s32[256]{0:T(256)S(1)}, s32[256]{0:T(256)}, u32[]{:S(2)}) copy-start(s32[256]{0:T(256)} %param.19) | copy-start | bytes 3076
  11.9 20.8 %copy-start.3 = (bf16[128,256]{1,0:T(8,128)(2,1)S(1)}, bf16[128,256]{1,0:T(8,128)(2,1)}, u32[]{:S(2)}) copy-start(bf16[128,256]{1,0:T(8,128)(2,1)} %param.12) | copy-start | bytes 196612
  13.9 18.8 %all-to-all-start.1 = ((bf16[32,1,8,1024]{3,2,1,0:T(8,128)(2,1)}), bf16[32,1,8,1024]{3,2,1,0:T(8,128)(2,1)S(1)}, u32[]{:S(2)}, u32[]{:S(2)}) async-start(bf16[32,1,8,1024]{3,2,1,0:T(8,128)(2,1)} %bitcast_multiply_fusion), calls=%async_computation.1 | async-start | bytes 1048576 | tf_op jit(solution)/shard_map/all_to_all | solution.py:211
  34.2 114.4 %all-to-all-start = ((bf16[32,128,256]{2,1,0:T(8,128)(2,1)}), bf16[32,128,256]{2,1,0:T(8,128)(2,1)}, u32[]{:S(2)}, u32[]{:S(2)}) async-start(bf16[32,128,256]{2,1,0:T(8,128)(2,1)} %broadcast_in_dim.34), calls=%async_computation | async-start | bytes 4194304 | tf_op jit(solution)/shard_map/all_to_all | solution.py:191
  129.1 2.7 %copy-start.4 = (bf16[1024,256]{1,0:T(8,128)(2,1)S(1)}, bf16[1024,256]{1,0:T(8,128)(2,1)}, u32[]{:S(2)}) copy-start(bf16[1024,256]{1,0:T(8,128)(2,1)} %param.13) | copy-start | bytes 1572868
  131.8 1.3 copy-start.5
  134.5 9.8 %collective-permute-start = (bf16[2,2,128,256]{3,2,1,0:T(8,128)(2,1)S(1)}, bf16[2,2,128,256]{3,2,1,0:T(8,128)(2,1)S(1)}, u32[]{:S(2)}, u32[]{:S(2)}) collective-permute-start(bf16[2,2,128,256]{3,2,1,0:T(8,128)(2,1)S(1)} %pad_maximum_fusion.3), channel_id=1, source_target_pairs={{0,16},{16,32},{32,48},{48,64},{64,80},{80,96},{96,112},{112,128},... | collective-permute-start | bytes 786440 | tf_op jit(solution)/shard_map/ppermute | solution.py:23
  145.6 3.1 %copy-start.6 = (f32[4096]{0:T(1024)S(1)}, f32[4096]{0:T(1024)}, u32[]{:S(2)}) copy-start(f32[4096]{0:T(1024)} %param.11) | copy-start | bytes 49156
  152.9 1.4 copy-start.1
Sparse Core Ops, SparseCore 0:
  9.4 125.7 all-gather.1

commit v11 on v10

--- a/solution.py
+++ b/solution.py
@@ -33,6 +33,13 @@
         )
     pl.semaphore_wait(barrier, 2)
     return right, left
+
+
+def ring_reach(count, piece, pieces):
+    far = count // 2
+    if count % 2 == 0 and piece >= pieces // 2:
+        return (far - 1, far)
+    return (far, count - 1 - far)
 
 
 def ring_gather_kernel(x_ref, o_ref, send_sem, recv_sem, *, count, axis, other, pieces):
@@ -46,26 +53,28 @@
     for step in range(1, half + 1):
         for piece in range(pieces):
             part = pl.ds(piece * size, size)
+            reach = ring_reach(count, piece, pieces)
             for toward in (0, 1):
-                if toward == 1 and step > count - 1 - half:
+                if step > reach[toward]:
                     continue
-                slot = half - step if toward == 0 else half + step
-                source = slot + 1 if toward == 0 else slot - 1
+                slot = (half - step) % count if toward == 0 else (half + step) % count
+                source = (slot + 1) % count if toward == 0 else (slot - 1) % count
                 if step > 1:
                     copies[(step - 1, toward, piece)].wait_recv()
                 copy = pltpu.make_async_remote_copy(
                     src_ref=x_ref.at[part] if step == 1 else o_ref.at[source, part],
                     dst_ref=o_ref.at[slot, part],
-                    send_sem=send_sem.at[slot, piece],
-                    recv_sem=recv_sem.at[slot, piece],
+                    send_sem=send_sem.at[toward, step - 1, piece],
+                    recv_sem=recv_sem.at[toward, step - 1, piece],
                     device_id=(row, right if toward == 0 else left),
                     device_id_type=pl.DeviceIdType.MESH,
                 )
                 copy.start()
                 copies[(step, toward, piece)] = copy
     for piece in range(pieces):
-        copies[(half, 0, piece)].wait_recv()
-        copies[(count - 1 - half, 1, piece)].wait_recv()
+        reach = ring_reach(count, piece, pieces)
+        copies[(reach[0], 0, piece)].wait_recv()
+        copies[(reach[1], 1, piece)].wait_recv()
     for copy in copies.values():
         copy.wait_send()
 
@@ -80,8 +89,8 @@
         in_specs=[pl.BlockSpec(memory_space=pltpu.VMEM)],
         out_specs=pl.BlockSpec(memory_space=pltpu.VMEM),
         scratch_shapes=[
-            pltpu.SemaphoreType.DMA((count, pieces)),
-            pltpu.SemaphoreType.DMA((count, pieces)),
+            pltpu.SemaphoreType.DMA((2, count // 2, pieces)),
+            pltpu.SemaphoreType.DMA((2, count // 2, pieces)),
         ],
         compiler_params=pltpu.CompilerParams(collective_id=collective_id, has_side_effects=True),
     )(block)
@@ -91,16 +100,16 @@
     me = lax.axis_index(axis)
     row = lax.axis_index(other)
     right, left = greet_neighbours(me, row, count)
-    reach = (count // 2, count - 1 - count // 2)
     width = p_ref.shape[2] // pieces
 
     def own(offset, part):
         return p_ref[lax.rem(me + offset + 2 * count, count), :, part].astype(jnp.float32)
 
     copies = {}
-    for step in range(1, reach[0] + 1):
+    for step in range(1, count // 2 + 1):
         for piece in range(pieces):
             part = pl.ds(piece * width, width)
+            reach = ring_reach(count, piece, pieces)
             for toward in (0, 1):
                 if step > reach[toward]:
                     continue
@@ -125,13 +134,17 @@
                 copy.start()
                 copies[(step, toward, piece)] = copy
     for piece in range(pieces):
+        reach = ring_reach(count, piece, pieces)
         copies[(reach[0], 0, piece)].wait_recv()
         copies[(reach[1], 1, piece)].wait_recv()
     for copy in copies.values():
         copy.wait_send()
-    total = p_ref[me].astype(jnp.float32) + sums_in[0, reach[0] - 1].astype(jnp.float32)
-    total = total + sums_in[1, reach[1] - 1].astype(jnp.float32)
-    o_ref[...] = total.astype(o_ref.dtype)
+    for piece in range(pieces):
+        part = pl.ds(piece * width, width)
+        reach = ring_reach(count, piece, pieces)
+        total = own(0, part) + sums_in[0, reach[0] - 1, :, part].astype(jnp.float32)
+        total = total + sums_in[1, reach[1] - 1, :, part].astype(jnp.float32)
+        o_ref[:, part] = total.astype(o_ref.dtype)
 
 
 def kernel_reduce_scatter(partial, axis, other, collective_id, pieces=4):

time: 219 us -> 212 us (0.968)
  Pallas kernels: 137 us -> 131 us
    pallas_call x1, Pallas kernels: 86.6 us -> 81.3 us  [kernel_gather(): pl.pallas_call(functools.partial(ring_gather_kernel, count=count, axis=ax...]
  transfers between devices with their start and end apart: 4 -> 4, of which waited for: 2 -> 2; matrix products, arithmetic and copies ran while one was open for 10% -> 10% of each run, Pallas kernels for 40% -> 38%
where the time goes in v11:
time: 212 us; the launch traced here: 211 us
  Pallas kernels  131 us (62%)
  starting transfers between devices  18.4 us (9%)
  waiting for transfers between devices  16.1 us (8%)
  between operations  13.7 us (6%)
  local copies, waits for them, and re-layouts  13.3 us (6%)
  matrix products  11.4 us (5%)
  other arithmetic  7.5 us (4%)
    pallas_call x1, Pallas kernels, kernel_gather(): pl.pallas_call(functools.partial(ring_gather_kernel, count=count, axis=ax...  81.3 us
    pallas_call x1, Pallas kernels, kernel_reduce_scatter(): pl.pallas_call(functools.partial(ring_sum_kernel, count=count, axis=axis,...  49.8 us
    all_to_all x1, starting transfers between devices, local(): lax.all_to_all(outgoing, 'ctx', split_axis=0, concat_axis=0, tiled=True)  9.29 us
    all_to_all x1, waiting for transfers between devices, local(): lax.all_to_all(outgoing, 'ctx', split_axis=0, concat_axis=0, tiled=True)  8.51 us
    all_to_all x1, starting transfers between devices, local(): lax.all_to_all(jnp.broadcast_to(query_weight[None], (ctx_count,) + query_...  7 us
    ppermute x1, waiting for transfers between devices, shifted(): return lax.ppermute(block, axis, route)  6.85 us
  transfers between devices with their start and end apart: 4, of which 2 were waited for; matrix products, arithmetic and copies ran while one was open for 10% of the time, Pallas kernels for 38%

profile of v11, /device:TPU:24, one launch (start us, length us, event | category | flops | bytes accessed | tf_op | source)
XLA Modules:
  0.0 211.5 jit_solution(12627678938671335247)
XLA Ops:
  6.5 0.7 all-gather.2.cloned.1.call-update
  7.3 0.8 copy.15
  8.3 3.6 %gather_fusion = s32[512]{0:T(512)S(1)} fusion(s32[512]{0:T(512)} %param.17, s32[1024]{0:T(1024)S(1)} %pad_clamp_fusion.2), kind=kCustom, calls=%fused_computation | custom fusion | bytes 6144 | tf_op jit(solution)/shard_map/gather | solution.py:213
  12.5 0.6 gather_fusion.1
  13.0 0.9 bitcast_multiply_fusion
  13.9 9.3 %all-to-all-start.1 = ((bf16[32,1,8,1024]{3,2,1,0:T(8,128)(2,1)}), bf16[32,1,8,1024]{3,2,1,0:T(8,128)(2,1)S(1)}, u32[]{:S(2)}, u32[]{:S(2)}) async-start(bf16[32,1,8,1024]{3,2,1,0:T(8,128)(2,1)} %bitcast_multiply_fusion), calls=%async_computation.1 | async-start | bytes 1048576 | tf_op jit(solution)/shard_map/all_to_all | solution.py:224
  23.3 0.6 dynamic_slice.10
  24.2 8.5 %all-to-all-done.1 = bf16[32,1,8,1024]{3,2,1,0:T(8,128)(2,1)S(1)} async-done(((bf16[32,1,8,1024]{3,2,1,0:T(8,128)(2,1)}), bf16[32,1,8,1024]{3,2,1,0:T(8,128)(2,1)S(1)}, u32[]{:S(2)}, u32[]{:S(2)}) %all-to-all-start.1) | async-done | bytes 524320 | tf_op jit(solution)/shard_map/all_to_all | solution.py:224
  32.7 1.5 broadcast_in_dim.34
  34.2 7.0 %all-to-all-start = ((bf16[32,128,256]{2,1,0:T(8,128)(2,1)}), bf16[32,128,256]{2,1,0:T(8,128)(2,1)}, u32[]{:S(2)}, u32[]{:S(2)}) async-start(bf16[32,128,256]{2,1,0:T(8,128)(2,1)} %broadcast_in_dim.34), calls=%async_computation | async-start | bytes 4194304 | tf_op jit(solution)/shard_map/all_to_all | solution.py:204
  41.2 1.3 gather_fusion.2
  42.5 81.3 %shard_map.100 = bf16[16,16,8,1024]{3,2,1,0:T(8,128)(2,1)} custom-call(bf16[16,8,1024]{2,1,0:T(8,128)(2,1)} %gather_fusion.2), custom_call_target="tpu_custom_call" | custom-call | tf_op jit(solution)/shard_map/pallas_call | solution.py:84
  123.8 2.7 %copy.16 = bf16[16,16,8,1024]{3,2,1,0:T(8,128)(2,1)S(1)} copy(bf16[16,16,8,1024]{3,2,0,1:T(8,128)(2,1)} %bitcast.42) | data formatting | bytes 8388608 | tf_op jit(solution)/shard_map/transpose | solution.py:234
  126.6 1.3 convolution_convert_fusion.2
  127.9 1.3 convolution_convert_fusion.1
  129.2 2.1 collective-permute-start
  131.3 0.7 pad_add_fusion
  132.2 6.9 %collective-permute-done = bf16[2,2,128,256]{3,2,1,0:T(8,128)(2,1)S(1)} collective-permute-done((bf16[2,2,128,256]{3,2,1,0:T(8,128)(2,1)S(1)}, bf16[2,2,128,256]{3,2,1,0:T(8,128)(2,1)S(1)}, u32[]{:S(2)}, u32[]{:S(2)}) %collective-permute-start) | collective-permute-done | bytes 262176 | tf_op jit(solution)/shard_map/ppermute | solution.py:23
  139.2 1.1 pad_maximum_fusion.1
  140.3 3.1 %fusion = f32[512]{0:T(512)S(1)} fusion(bf16[512,4096]{1,0:T(8,128)(2,1)} %all-gather.2.cloned.1.call-done), kind=kLoop, calls=%fused_computation.5 | loop fusion | flops 6290944 | bytes 4196352 | tf_op jit(solution)/shard_map/reduce_sum | solution.py:200
  143.4 4.2 %fusion.10 = bf16[512,256]{1,0:T(8,128)(2,1)S(1)} fusion(bf16[4096,256]{1,0:T(8,128)(2,1)} %bitcast, bf16[512,4096]{1,0:T(8,128)(2,1)} %all-gather.2.cloned.1.call-done, f32[4096]{0:T(1024)S(1)} %copy-done.6, f32[512]{0:T(512)S(1)} %add_rsqrt_fusion), kind=kOutput, calls=%fused_computation.17 | convolution fusion | flops 1082392576 | bytes 6572032 | tf_op jit(solution)/shard_map/dot_general | solution.py:211
  149.9 3.2 %convolution_convert_fusion = bf16[512,4096]{1,0:T(8,128)(2,1)} fusion(bf16[256,4096]{1,0:T(8,128)(2,1)S(1)} %copy-done, bf16[576,256]{1,0:T(8,128)(2,1)S(1)} %bitcast.54, pred[512]{0:T(512)(128)(4,1)S(1)} %fusion.38), kind=kOutput, calls=%fused_computation.8 | convolution fusion | flops 1075970048 | bytes 6554112 | tf_op jit(solution)/shard_map/dot_general | solution.py:287
  153.1 49.8 %shard_map.101 = bf16[32,4096]{1,0:T(8,128)(2,1)} custom-call(bf16[16,32,4096]{2,1,0:T(8,128)(2,1)} %bitcast.41), custom_call_target="tpu_custom_call" | custom-call | tf_op jit(solution)/shard_map/pallas_call | solution.py:155
  203.0 1.7 copy.18
  (55 shorter events, 3.6 us)
Async XLA Ops:
  6.5 143.4 %copy-start = (bf16[256,4096]{1,0:T(8,128)(2,1)S(1)}, bf16[256,4096]{1,0:T(8,128)(2,1)}, u32[]{:S(2)}) copy-start(bf16[256,4096]{1,0:T(8,128)(2,1)} %param.15) | copy-start | bytes 6291460
  6.5 5.9 %copy-start.2 = (bf16[16,8,1024]{2,1,0:T(8,128)(2,1)S(1)}, bf16[16,8,1024]{2,1,0:T(8,128)(2,1)}, u32[]{:S(2)}) copy-start(bf16[16,8,1024]{2,1,0:T(8,128)(2,1)} %param.16) | copy-start | bytes 786436
  6.5 133.7 %all-gather.2.cloned.1.call-start = ((), (), s32[]{:S(2)}) async-start(), calls=%async_computation.2 | async-start | bytes 4456448 | tf_op jit(solution)/shard_map/all_gather | solution.py:198
  11.9 11.4 %copy-start.7 = (s32[256]{0:T(256)S(1)}, s32[256]{0:T(256)}, u32[]{:S(2)}) copy-start(s32[256]{0:T(256)} %param.19) | copy-start | bytes 3076
  11.9 20.8 %copy-start.3 = (bf16[128,256]{1,0:T(8,128)(2,1)S(1)}, bf16[128,256]{1,0:T(8,128)(2,1)}, u32[]{:S(2)}) copy-start(bf16[128,256]{1,0:T(8,128)(2,1)} %param.12) | copy-start | bytes 196612
  13.9 18.8 %all-to-all-start.1 = ((bf16[32,1,8,1024]{3,2,1,0:T(8,128)(2,1)}), bf16[32,1,8,1024]{3,2,1,0:T(8,128)(2,1)S(1)}, u32[]{:S(2)}, u32[]{:S(2)}) async-start(bf16[32,1,8,1024]{3,2,1,0:T(8,128)(2,1)} %bitcast_multiply_fusion), calls=%async_computation.1 | async-start | bytes 1048576 | tf_op jit(solution)/shard_map/all_to_all | solution.py:224
  34.2 109.1 %all-to-all-start = ((bf16[32,128,256]{2,1,0:T(8,128)(2,1)}), bf16[32,128,256]{2,1,0:T(8,128)(2,1)}, u32[]{:S(2)}, u32[]{:S(2)}) async-start(bf16[32,128,256]{2,1,0:T(8,128)(2,1)} %broadcast_in_dim.34), calls=%async_computation | async-start | bytes 4194304 | tf_op jit(solution)/shard_map/all_to_all | solution.py:204
  123.8 2.7 %copy-start.4 = (bf16[1024,256]{1,0:T(8,128)(2,1)S(1)}, bf16[1024,256]{1,0:T(8,128)(2,1)}, u32[]{:S(2)}) copy-start(bf16[1024,256]{1,0:T(8,128)(2,1)} %param.13) | copy-start | bytes 1572868
  126.5 1.3 copy-start.5
  129.2 9.8 %collective-permute-start = (bf16[2,2,128,256]{3,2,1,0:T(8,128)(2,1)S(1)}, bf16[2,2,128,256]{3,2,1,0:T(8,128)(2,1)S(1)}, u32[]{:S(2)}, u32[]{:S(2)}) collective-permute-start(bf16[2,2,128,256]{3,2,1,0:T(8,128)(2,1)S(1)} %pad_maximum_fusion.3), channel_id=1, source_target_pairs={{0,16},{16,32},{32,48},{48,64},{64,80},{80,96},{96,112},{112,128},... | collective-permute-start | bytes 786440 | tf_op jit(solution)/shard_map/ppermute | solution.py:23
  140.3 3.1 %copy-start.6 = (f32[4096]{0:T(1024)S(1)}, f32[4096]{0:T(1024)}, u32[]{:S(2)}) copy-start(f32[4096]{0:T(1024)} %param.11) | copy-start | bytes 49156
  147.6 1.4 copy-start.1
Sparse Core Ops, SparseCore 0:
  9.4 123.3 all-gather.1

commit v12 on v11

--- a/solution.py
+++ b/solution.py
@@ -210,7 +210,10 @@
     ).reshape(-1, query_weight.shape[1])
     query_sum = jnp.dot(normed, query_full, preferred_element_type=jnp.float32)
     queries = (query_sum * HS ** (-0.5)).astype(jnp.bfloat16)
-    storage = row_place[neighbour_ids.reshape(-1)].reshape(ctx_count, rows_dev)
+    matches = neighbour_ids.reshape(-1)[:, None] == jnp.arange(row_place.shape[0])[None, :]
+    storage = jnp.sum(jnp.where(matches, row_place[None, :], 0), axis=1).reshape(
+        ctx_count, rows_dev
+    )
     sources = storage // rows_dev
     local_rows = storage % rows_dev
     from_here = sources == ctx_index

time: 212 us -> 210 us (level)
  local copies, waits for them, and re-layouts: 13.3 us -> 10.6 us
    gather x1 -> x0, local copies, waits for them, and re-layouts: 3.62 us -> none  [local(): storage = row_place[neighbour_ids.reshape(-1)].reshape(ctx_count, rows_dev)]
  transfers between devices with their start and end apart: 4 -> 4, of which waited for: 2 -> 2; matrix products, arithmetic and copies ran while one was open for 10% -> 9% of each run, Pallas kernels for 38% -> 38%
where the time goes in v12:
time: 210 us
  Pallas kernels  131 us (62%)
  starting transfers between devices  18.4 us (9%)
  waiting for transfers between devices  16.1 us (8%)
  between operations  13.7 us (7%)
  matrix products  11.4 us (5%)
  local copies, waits for them, and re-layouts  10.6 us (5%)
  other arithmetic  8.43 us (4%)
    pallas_call x1, Pallas kernels, kernel_gather(): pl.pallas_call(functools.partial(ring_gather_kernel, count=count, axis=ax...  80.4 us
    pallas_call x1, Pallas kernels, kernel_reduce_scatter(): pl.pallas_call(functools.partial(ring_sum_kernel, count=count, axis=axis,...  50.6 us
    all_to_all x1, starting transfers between devices, local(): lax.all_to_all(outgoing, 'ctx', split_axis=0, concat_axis=0, tiled=True)  9.29 us
    all_to_all x1, waiting for transfers between devices, local(): lax.all_to_all(outgoing, 'ctx', split_axis=0, concat_axis=0, tiled=True)  8.51 us
    all_to_all x1, starting transfers between devices, local(): lax.all_to_all(jnp.broadcast_to(query_weight[None], (ctx_count,) + query_...  6.99 us
    ppermute x1, waiting for transfers between devices, shifted(): return lax.ppermute(block, axis, route)  6.85 us
  transfers between devices with their start and end apart: 4, of which 2 were waited for; matrix products, arithmetic and copies ran while one was open for 9% of the time, Pallas kernels for 38%

profile of v12, /device:TPU:24, one launch (start us, length us, event | category | flops | bytes accessed | tf_op | source)
XLA Modules:
  0.0 209.5 jit_solution(5998908676276029994)
XLA Ops:
  6.5 0.7 all-gather.2.cloned.1.call-update
  7.3 0.8 copy.15
  8.2 0.9 select_reduce_fusion
  9.7 1.5 gather_fusion
  11.3 0.9 bitcast_multiply_fusion
  12.2 9.3 %all-to-all-start.1 = ((bf16[32,1,8,1024]{3,2,1,0:T(8,128)(2,1)}), bf16[32,1,8,1024]{3,2,1,0:T(8,128)(2,1)S(1)}, u32[]{:S(2)}, u32[]{:S(2)}) async-start(bf16[32,1,8,1024]{3,2,1,0:T(8,128)(2,1)} %bitcast_multiply_fusion), calls=%async_computation.1 | async-start | bytes 1048576 | tf_op jit(solution)/shard_map/all_to_all | solution.py:227
  21.5 0.6 dynamic_slice.10
  22.4 8.5 %all-to-all-done.1 = bf16[32,1,8,1024]{3,2,1,0:T(8,128)(2,1)S(1)} async-done(((bf16[32,1,8,1024]{3,2,1,0:T(8,128)(2,1)}), bf16[32,1,8,1024]{3,2,1,0:T(8,128)(2,1)S(1)}, u32[]{:S(2)}, u32[]{:S(2)}) %all-to-all-start.1) | async-done | bytes 524320 | tf_op jit(solution)/shard_map/all_to_all | solution.py:227
  30.9 1.5 broadcast_in_dim.46
  32.5 7.0 %all-to-all-start = ((bf16[32,128,256]{2,1,0:T(8,128)(2,1)}), bf16[32,128,256]{2,1,0:T(8,128)(2,1)}, u32[]{:S(2)}, u32[]{:S(2)}) async-start(bf16[32,128,256]{2,1,0:T(8,128)(2,1)} %broadcast_in_dim.46), calls=%async_computation | async-start | bytes 4194304 | tf_op jit(solution)/shard_map/all_to_all | solution.py:204
  39.5 1.3 gather_fusion.1
  40.7 80.4 %shard_map.100 = bf16[16,16,8,1024]{3,2,1,0:T(8,128)(2,1)} custom-call(bf16[16,8,1024]{2,1,0:T(8,128)(2,1)} %gather_fusion.1), custom_call_target="tpu_custom_call" | custom-call | tf_op jit(solution)/shard_map/pallas_call | solution.py:84
  121.1 2.7 %copy.16 = bf16[16,16,8,1024]{3,2,1,0:T(8,128)(2,1)S(1)} copy(bf16[16,16,8,1024]{3,2,0,1:T(8,128)(2,1)} %bitcast.41) | data formatting | bytes 8388608 | tf_op jit(solution)/shard_map/transpose | solution.py:237
  123.8 1.3 convolution_convert_fusion.2
  125.1 1.3 convolution_convert_fusion.1
  126.5 2.1 %collective-permute-start = (bf16[2,2,128,256]{3,2,1,0:T(8,128)(2,1)S(1)}, bf16[2,2,128,256]{3,2,1,0:T(8,128)(2,1)S(1)}, u32[]{:S(2)}, u32[]{:S(2)}) collective-permute-start(bf16[2,2,128,256]{3,2,1,0:T(8,128)(2,1)S(1)} %pad_maximum_fusion.3), channel_id=1, source_target_pairs={{0,16},{16,32},{32,48},{48,64},{64,80},{80,96},{96,112},{112,128},... | collective-permute-start | bytes 786440 | tf_op jit(solution)/shard_map/ppermute | solution.py:23
  128.6 0.7 pad_add_fusion
  129.4 6.9 %collective-permute-done = bf16[2,2,128,256]{3,2,1,0:T(8,128)(2,1)S(1)} collective-permute-done((bf16[2,2,128,256]{3,2,1,0:T(8,128)(2,1)S(1)}, bf16[2,2,128,256]{3,2,1,0:T(8,128)(2,1)S(1)}, u32[]{:S(2)}, u32[]{:S(2)}) %collective-permute-start) | collective-permute-done | bytes 262176 | tf_op jit(solution)/shard_map/ppermute | solution.py:23
  136.4 1.1 pad_maximum_fusion.1
  137.5 3.1 %fusion = f32[512]{0:T(512)S(1)} fusion(bf16[512,4096]{1,0:T(8,128)(2,1)} %all-gather.2.cloned.1.call-done), kind=kLoop, calls=%fused_computation.4 | loop fusion | flops 6290944 | bytes 4196352 | tf_op jit(solution)/shard_map/reduce_sum | solution.py:200
  140.7 4.2 %fusion.10 = bf16[512,256]{1,0:T(8,128)(2,1)S(1)} fusion(bf16[4096,256]{1,0:T(8,128)(2,1)} %bitcast, bf16[512,4096]{1,0:T(8,128)(2,1)} %all-gather.2.cloned.1.call-done, f32[4096]{0:T(1024)S(1)} %copy-done.5, f32[512]{0:T(512)S(1)} %add_rsqrt_fusion), kind=kOutput, calls=%fused_computation.16 | convolution fusion | flops 1082392576 | bytes 6572032 | tf_op jit(solution)/shard_map/dot_general | solution.py:211
  147.2 3.2 %convolution_convert_fusion = bf16[512,4096]{1,0:T(8,128)(2,1)} fusion(bf16[256,4096]{1,0:T(8,128)(2,1)S(1)} %copy-done, bf16[576,256]{1,0:T(8,128)(2,1)S(1)} %bitcast.53, pred[512]{0:T(512)(128)(4,1)S(1)} %fusion.38), kind=kOutput, calls=%fused_computation.7 | convolution fusion | flops 1075970048 | bytes 6554112 | tf_op jit(solution)/shard_map/dot_general | solution.py:290
  150.4 50.6 %shard_map.101 = bf16[32,4096]{1,0:T(8,128)(2,1)} custom-call(bf16[16,32,4096]{2,1,0:T(8,128)(2,1)} %bitcast.40), custom_call_target="tpu_custom_call" | custom-call | tf_op jit(solution)/shard_map/pallas_call | solution.py:155
  201.0 1.7 copy.18
  (51 shorter events, 3.6 us)
Async XLA Ops:
  6.5 140.6 %copy-start = (bf16[256,4096]{1,0:T(8,128)(2,1)S(1)}, bf16[256,4096]{1,0:T(8,128)(2,1)}, u32[]{:S(2)}) copy-start(bf16[256,4096]{1,0:T(8,128)(2,1)} %param.15) | copy-start | bytes 6291460
  6.5 14.9 %copy-start.6 = (s32[256]{0:T(256)S(1)}, s32[256]{0:T(256)}, u32[]{:S(2)}) copy-start(s32[256]{0:T(256)} %param.19) | copy-start | bytes 3076
  6.5 24.4 %copy-start.2 = (bf16[128,256]{1,0:T(8,128)(2,1)S(1)}, bf16[128,256]{1,0:T(8,128)(2,1)}, u32[]{:S(2)}) copy-start(bf16[128,256]{1,0:T(8,128)(2,1)} %param.12) | copy-start | bytes 196612
  6.5 131.0 %all-gather.2.cloned.1.call-start = ((), (), s32[]{:S(2)}) async-start(), calls=%async_computation.2 | async-start | bytes 4456448 | tf_op jit(solution)/shard_map/all_gather | solution.py:198
  12.2 18.8 %all-to-all-start.1 = ((bf16[32,1,8,1024]{3,2,1,0:T(8,128)(2,1)}), bf16[32,1,8,1024]{3,2,1,0:T(8,128)(2,1)S(1)}, u32[]{:S(2)}, u32[]{:S(2)}) async-start(bf16[32,1,8,1024]{3,2,1,0:T(8,128)(2,1)} %bitcast_multiply_fusion), calls=%async_computation.1 | async-start | bytes 1048576 | tf_op jit(solution)/shard_map/all_to_all | solution.py:227
  32.5 108.2 %all-to-all-start = ((bf16[32,128,256]{2,1,0:T(8,128)(2,1)}), bf16[32,128,256]{2,1,0:T(8,128)(2,1)}, u32[]{:S(2)}, u32[]{:S(2)}) async-start(bf16[32,128,256]{2,1,0:T(8,128)(2,1)} %broadcast_in_dim.46), calls=%async_computation | async-start | bytes 4194304 | tf_op jit(solution)/shard_map/all_to_all | solution.py:204
  121.1 2.7 %copy-start.3 = (bf16[1024,256]{1,0:T(8,128)(2,1)S(1)}, bf16[1024,256]{1,0:T(8,128)(2,1)}, u32[]{:S(2)}) copy-start(bf16[1024,256]{1,0:T(8,128)(2,1)} %param.13) | copy-start | bytes 1572868
  123.8 1.3 copy-start.4
  126.5 9.8 %collective-permute-start = (bf16[2,2,128,256]{3,2,1,0:T(8,128)(2,1)S(1)}, bf16[2,2,128,256]{3,2,1,0:T(8,128)(2,1)S(1)}, u32[]{:S(2)}, u32[]{:S(2)}) collective-permute-start(bf16[2,2,128,256]{3,2,1,0:T(8,128)(2,1)S(1)} %pad_maximum_fusion.3), channel_id=1, source_target_pairs={{0,16},{16,32},{32,48},{48,64},{64,80},{80,96},{96,112},{112,128},... | collective-permute-start | bytes 786440 | tf_op jit(solution)/shard_map/ppermute | solution.py:23
  137.5 3.1 %copy-start.5 = (f32[4096]{0:T(1024)S(1)}, f32[4096]{0:T(1024)}, u32[]{:S(2)}) copy-start(f32[4096]{0:T(1024)} %param.11) | copy-start | bytes 49156
  144.8 1.4 copy-start.1
Sparse Core Ops, SparseCore 0:
  9.4 123.5 all-gather.1

commit v13 on v12

--- a/solution.py
+++ b/solution.py
@@ -142,9 +142,8 @@
     for piece in range(pieces):
         part = pl.ds(piece * width, width)
         reach = ring_reach(count, piece, pieces)
-        total = own(0, part) + sums_in[0, reach[0] - 1, :, part].astype(jnp.float32)
-        total = total + sums_in[1, reach[1] - 1, :, part].astype(jnp.float32)
-        o_ref[:, part] = total.astype(o_ref.dtype)
+        for toward in (0, 1):
+            o_ref[toward, :, part] = sums_in[toward, reach[toward] - 1, :, part]
 
 
 def kernel_reduce_scatter(partial, axis, other, collective_id, pieces=4):
@@ -152,11 +151,11 @@
     blocks = partial.reshape((count, partial.shape[0] // count) + partial.shape[1:])
     block = blocks.shape[1:]
     reach = count // 2
-    return pl.pallas_call(
+    arrived = pl.pallas_call(
         functools.partial(
             ring_sum_kernel, count=count, axis=axis, other=other, pieces=pieces
         ),
-        out_shape=jax.ShapeDtypeStruct(block, partial.dtype),
+        out_shape=jax.ShapeDtypeStruct((2,) + block, partial.dtype),
         in_specs=[pl.BlockSpec(memory_space=pltpu.VMEM)],
         out_specs=pl.BlockSpec(memory_space=pltpu.VMEM),
         scratch_shapes=[
@@ -166,6 +165,9 @@
         ],
         compiler_params=pltpu.CompilerParams(collective_id=collective_id, has_side_effects=True),
     )(blocks)
+    own = lax.dynamic_index_in_dim(blocks, lax.axis_index(axis), 0, keepdims=False)
+    total = own.astype(jnp.float32) + arrived[0].astype(jnp.float32)
+    return (total + arrived[1].astype(jnp.float32)).astype(partial.dtype)
 
 
 def project_rows(rows, weight):

time: 210 us -> 213 us (1.014)
  other arithmetic: 8.43 us -> 11.6 us
  transfers between devices with their start and end apart: 4 -> 4, of which waited for: 2 -> 2; matrix products, arithmetic and copies ran while one was open for 9% -> 10% of each run, Pallas kernels for 38% -> 38%
where the time goes in v13:
time: 213 us; the launch traced here: 212 us
  Pallas kernels  131 us (62%)
  starting transfers between devices  18.4 us (9%)
  waiting for transfers between devices  16.1 us (8%)
  between operations  13.7 us (6%)
  other arithmetic  11.6 us (5%)
  matrix products  11.4 us (5%)
  local copies, waits for them, and re-layouts  9.88 us (5%)
    pallas_call x1, Pallas kernels, kernel_gather(): pl.pallas_call(functools.partial(ring_gather_kernel, count=count, axis=ax...  80.4 us
    pallas_call x1, Pallas kernels, kernel_reduce_scatter(): pl.pallas_call(functools.partial(ring_sum_kernel, count=count, axis=axis,...  50.6 us
    all_to_all x1, starting transfers between devices, local(): lax.all_to_all(outgoing, 'ctx', split_axis=0, concat_axis=0, tiled=True)  9.29 us
    all_to_all x1, waiting for transfers between devices, local(): lax.all_to_all(outgoing, 'ctx', split_axis=0, concat_axis=0, tiled=True)  8.51 us
    all_to_all x1, starting transfers between devices, local(): lax.all_to_all(jnp.broadcast_to(query_weight[None], (ctx_count,) + query_...  6.99 us
    ppermute x1, waiting for transfers between devices, shifted(): return lax.ppermute(block, axis, route)  6.85 us
  transfers between devices with their start and end apart: 4, of which 2 were waited for; matrix products, arithmetic and copies ran while one was open for 10% of the time, Pallas kernels for 38%

profile of v13, /device:TPU:24, one launch (start us, length us, event | category | flops | bytes accessed | tf_op | source)
XLA Modules:
  0.0 212.0 jit_solution(9571646424098315670)
XLA Ops:
  6.5 0.7 all-gather.2.cloned.1.call-update
  7.3 0.8 copy.15
  8.2 0.9 select_reduce_fusion
  9.7 1.5 gather_fusion
  11.3 0.9 bitcast_multiply_fusion
  12.2 9.3 %all-to-all-start.1 = ((bf16[32,1,8,1024]{3,2,1,0:T(8,128)(2,1)}), bf16[32,1,8,1024]{3,2,1,0:T(8,128)(2,1)S(1)}, u32[]{:S(2)}, u32[]{:S(2)}) async-start(bf16[32,1,8,1024]{3,2,1,0:T(8,128)(2,1)} %bitcast_multiply_fusion), calls=%async_computation.1 | async-start | bytes 1048576 | tf_op jit(solution)/shard_map/all_to_all | solution.py:229
  22.4 8.5 %all-to-all-done.1 = bf16[32,1,8,1024]{3,2,1,0:T(8,128)(2,1)S(1)} async-done(((bf16[32,1,8,1024]{3,2,1,0:T(8,128)(2,1)}), bf16[32,1,8,1024]{3,2,1,0:T(8,128)(2,1)S(1)}, u32[]{:S(2)}, u32[]{:S(2)}) %all-to-all-start.1) | async-done | bytes 524320 | tf_op jit(solution)/shard_map/all_to_all | solution.py:229
  30.9 1.5 broadcast_in_dim.46
  32.5 7.0 %all-to-all-start = ((bf16[32,128,256]{2,1,0:T(8,128)(2,1)}), bf16[32,128,256]{2,1,0:T(8,128)(2,1)}, u32[]{:S(2)}, u32[]{:S(2)}) async-start(bf16[32,128,256]{2,1,0:T(8,128)(2,1)} %broadcast_in_dim.46), calls=%async_computation | async-start | bytes 4194304 | tf_op jit(solution)/shard_map/all_to_all | solution.py:206
  39.5 1.3 gather_fusion.1
  40.7 80.4 %shard_map.100 = bf16[16,16,8,1024]{3,2,1,0:T(8,128)(2,1)} custom-call(bf16[16,8,1024]{2,1,0:T(8,128)(2,1)} %gather_fusion.1), custom_call_target="tpu_custom_call" | custom-call | tf_op jit(solution)/shard_map/pallas_call | solution.py:84
  121.1 2.7 %copy.16 = bf16[16,16,8,1024]{3,2,1,0:T(8,128)(2,1)S(1)} copy(bf16[16,16,8,1024]{3,2,0,1:T(8,128)(2,1)} %bitcast.44) | data formatting | bytes 8388608 | tf_op jit(solution)/shard_map/transpose | solution.py:239
  123.8 1.3 convolution_convert_fusion.2
  125.1 1.3 convolution_convert_fusion.1
  126.5 1.0 copy-done.1
  127.5 2.1 collective-permute-start
  130.4 6.8 %collective-permute-done = bf16[2,2,128,256]{3,2,1,0:T(8,128)(2,1)S(1)} collective-permute-done((bf16[2,2,128,256]{3,2,1,0:T(8,128)(2,1)S(1)}, bf16[2,2,128,256]{3,2,1,0:T(8,128)(2,1)S(1)}, u32[]{:S(2)}, u32[]{:S(2)}) %collective-permute-start) | collective-permute-done | bytes 262176 | tf_op jit(solution)/shard_map/ppermute | solution.py:23
  137.3 1.3 pad_maximum_fusion
  138.6 1.1 pad_maximum_fusion.1
  139.8 3.1 %fusion = f32[512]{0:T(512)S(1)} fusion(bf16[512,4096]{1,0:T(8,128)(2,1)} %all-gather.2.cloned.1.call-done), kind=kLoop, calls=%fused_computation.4 | loop fusion | flops 6290944 | bytes 4196352 | tf_op jit(solution)/shard_map/reduce_sum | solution.py:202
  142.9 4.2 %fusion.10 = bf16[512,256]{1,0:T(8,128)(2,1)S(1)} fusion(bf16[4096,256]{1,0:T(8,128)(2,1)} %bitcast, bf16[512,4096]{1,0:T(8,128)(2,1)} %all-gather.2.cloned.1.call-done, f32[4096]{0:T(1024)S(1)} %copy-done.8, f32[512]{0:T(512)S(1)} %add_rsqrt_fusion), kind=kOutput, calls=%fused_computation.16 | convolution fusion | flops 1082392576 | bytes 6572032 | tf_op jit(solution)/shard_map/dot_general | solution.py:213
  149.4 3.2 %convolution_convert_fusion = bf16[512,4096]{1,0:T(8,128)(2,1)} fusion(bf16[256,4096]{1,0:T(8,128)(2,1)S(1)} %copy-done, bf16[576,256]{1,0:T(8,128)(2,1)S(1)} %bitcast.56, pred[512]{0:T(512)(128)(4,1)S(1)} %fusion.39), kind=kOutput, calls=%fused_computation.7 | convolution fusion | flops 1075970048 | bytes 6554112 | tf_op jit(solution)/shard_map/dot_general | solution.py:292
  152.6 50.6 %shard_map.101 = bf16[2,32,4096]{2,1,0:T(8,128)(2,1)} custom-call(bf16[16,32,4096]{2,1,0:T(8,128)(2,1)} %bitcast.42), custom_call_target="tpu_custom_call" | custom-call | tf_op jit(solution)/shard_map/pallas_call | solution.py:154
  203.3 1.9 fusion.26
  (57 shorter events, 4.8 us)
Async XLA Ops:
  6.5 142.8 %copy-start = (bf16[256,4096]{1,0:T(8,128)(2,1)S(1)}, bf16[256,4096]{1,0:T(8,128)(2,1)}, u32[]{:S(2)}) copy-start(bf16[256,4096]{1,0:T(8,128)(2,1)} %param.15) | copy-start | bytes 6291460
  6.5 14.9 %copy-start.9 = (s32[256]{0:T(256)S(1)}, s32[256]{0:T(256)}, u32[]{:S(2)}) copy-start(s32[256]{0:T(256)} %param.19) | copy-start | bytes 3076
  6.5 24.4 %copy-start.5 = (bf16[128,256]{1,0:T(8,128)(2,1)S(1)}, bf16[128,256]{1,0:T(8,128)(2,1)}, u32[]{:S(2)}) copy-start(bf16[128,256]{1,0:T(8,128)(2,1)} %param.12) | copy-start | bytes 196612
  6.5 133.2 %all-gather.2.cloned.1.call-start = ((), (), s32[]{:S(2)}) async-start(), calls=%async_computation.2 | async-start | bytes 4456448 | tf_op jit(solution)/shard_map/all_gather | solution.py:200
  12.2 18.8 %all-to-all-start.1 = ((bf16[32,1,8,1024]{3,2,1,0:T(8,128)(2,1)}), bf16[32,1,8,1024]{3,2,1,0:T(8,128)(2,1)S(1)}, u32[]{:S(2)}, u32[]{:S(2)}) async-start(bf16[32,1,8,1024]{3,2,1,0:T(8,128)(2,1)} %bitcast_multiply_fusion), calls=%async_computation.1 | async-start | bytes 1048576 | tf_op jit(solution)/shard_map/all_to_all | solution.py:229
  32.5 110.4 %all-to-all-start = ((bf16[32,128,256]{2,1,0:T(8,128)(2,1)}), bf16[32,128,256]{2,1,0:T(8,128)(2,1)}, u32[]{:S(2)}, u32[]{:S(2)}) async-start(bf16[32,128,256]{2,1,0:T(8,128)(2,1)} %broadcast_in_dim.46), calls=%async_computation | async-start | bytes 4194304 | tf_op jit(solution)/shard_map/all_to_all | solution.py:206
  121.1 2.7 %copy-start.6 = (bf16[1024,256]{1,0:T(8,128)(2,1)S(1)}, bf16[1024,256]{1,0:T(8,128)(2,1)}, u32[]{:S(2)}) copy-start(bf16[1024,256]{1,0:T(8,128)(2,1)} %param.13) | copy-start | bytes 1572868
  123.8 1.3 copy-start.7
  125.1 1.3 copy-start.3
  126.4 1.0 copy-start.1
  127.5 9.8 %collective-permute-start = (bf16[2,2,128,256]{3,2,1,0:T(8,128)(2,1)S(1)}, bf16[2,2,128,256]{3,2,1,0:T(8,128)(2,1)S(1)}, u32[]{:S(2)}, u32[]{:S(2)}) collective-permute-start(bf16[2,2,128,256]{3,2,1,0:T(8,128)(2,1)S(1)} %pad_maximum_fusion.3), channel_id=1, source_target_pairs={{0,16},{16,32},{32,48},{48,64},{64,80},{80,96},{96,112},{112,128},... | collective-permute-start | bytes 786440 | tf_op jit(solution)/shard_map/ppermute | solution.py:23
  130.3 8.3 %copy-start.2 = (bf16[2048,256]{1,0:T(8,128)(2,1)S(1)}, bf16[2048,256]{1,0:T(8,128)(2,1)}, u32[]{:S(2)}) copy-start(bf16[2048,256]{1,0:T(8,128)(2,1)} %copy-done.1) | copy-start | bytes 3145732
  139.7 3.1 %copy-start.8 = (f32[4096]{0:T(1024)S(1)}, f32[4096]{0:T(1024)}, u32[]{:S(2)}) copy-start(f32[4096]{0:T(1024)} %param.11) | copy-start | bytes 49156
  147.1 1.4 copy-start.4
Sparse Core Ops, SparseCore 0:
  9.4 123.5 all-gather.1

commit v14 on v12

--- a/solution.py
+++ b/solution.py
@@ -195,9 +195,11 @@
     head_width = query_weight.shape[1]
     head_count = head_width // HS
     slot_cap = -(-rows_dev // ctx_count)
+    local_wide = hidden.astype(jnp.float32)
+    square_parts = lax.all_gather(jnp.sum(local_wide * local_wide, axis=1), "tp", axis=1)
     whole = lax.all_gather(hidden, "tp", axis=1, tiled=True)
     values_wide = whole.astype(jnp.float32)
-    mean_square = jnp.mean(values_wide * values_wide, axis=1, keepdims=True)
+    mean_square = jnp.sum(square_parts, axis=1, keepdims=True) / whole.shape[1]
     normed = (values_wide * lax.rsqrt(mean_square + epsilon) * norm_gain[None, :]).astype(
         jnp.bfloat16
     )

time: 210 us -> 225 us (1.071)
  blocking collectives: 0 us -> 33.6 us
  Pallas kernels: 131 us -> 115 us
  other arithmetic: 8.43 us -> 5.53 us
    all_gather x0 -> x1, blocking collectives: none -> 33.6 us  [local(): lax.all_gather(jnp.sum(local_wide * local_wide, axis=1), 'tp', axis=1)]
    pallas_call x1, Pallas kernels: 80.4 us -> 64.6 us  [kernel_gather(): pl.pallas_call(functools.partial(ring_gather_kernel, count=count, axis=ax...]
    reduce_sum x1 -> x2, other arithmetic: 3.09 us -> 0.19 us  [the longest x1 0.15 us: local(): jnp.sum(local_wide * local_wide, axis=1)]
  transfers between devices with their start and end apart: 4 -> 4, of which waited for: 2 -> 2; matrix products, arithmetic and copies ran while one was open for 9% -> 7% of each run, Pallas kernels for 38% -> 29%
where the time goes in v14:
time: 225 us
  Pallas kernels  115 us (51%)
  blocking collectives  33.6 us (15%)
  starting transfers between devices  18.5 us (8%)
  waiting for transfers between devices  16.6 us (7%)
  between operations  13.7 us (6%)
  matrix products  11.4 us (5%)
  local copies, waits for them, and re-layouts  10.6 us (5%)
  other arithmetic  5.53 us (2%)
    pallas_call x1, Pallas kernels, kernel_gather(): pl.pallas_call(functools.partial(ring_gather_kernel, count=count, axis=ax...  64.6 us
    pallas_call x1, Pallas kernels, kernel_reduce_scatter(): pl.pallas_call(functools.partial(ring_sum_kernel, count=count, axis=axis,...  50.4 us
    all_gather x1, blocking collectives, local(): lax.all_gather(jnp.sum(local_wide * local_wide, axis=1), 'tp', axis=1)  33.6 us
    all_to_all x1, starting transfers between devices, local(): lax.all_to_all(outgoing, 'ctx', split_axis=0, concat_axis=0, tiled=True)  9.29 us
    all_to_all x1, waiting for transfers between devices, local(): lax.all_to_all(outgoing, 'ctx', split_axis=0, concat_axis=0, tiled=True)  9.07 us
    all_to_all x1, starting transfers between devices, local(): lax.all_to_all(jnp.broadcast_to(query_weight[None], (ctx_count,) + query_...  7.13 us
    ppermute x1, waiting for transfers between devices, shifted(): return lax.ppermute(block, axis, route)  6.85 us
  transfers between devices with their start and end apart: 4, of which 2 were waited for; matrix products, arithmetic and copies ran while one was open for 7% of the time, Pallas kernels for 29%

profile of v14, /device:TPU:24, one launch (start us, length us, event | category | flops | bytes accessed | tf_op | source)
XLA Modules:
  0.0 224.9 jit_solution(10615346229189794574)
XLA Ops:
  6.5 0.7 all-gather.3.cloned.1.call-update
  7.3 0.8 copy.15
  8.2 0.9 select_reduce_fusion
  9.7 1.5 gather_fusion
  11.3 0.9 bitcast_multiply_fusion
  12.2 9.3 %all-to-all-start.1 = ((bf16[32,1,8,1024]{3,2,1,0:T(8,128)(2,1)}), bf16[32,1,8,1024]{3,2,1,0:T(8,128)(2,1)S(1)}, u32[]{:S(2)}, u32[]{:S(2)}) async-start(bf16[32,1,8,1024]{3,2,1,0:T(8,128)(2,1)} %bitcast_multiply_fusion), calls=%async_computation.1 | async-start | bytes 1048576 | tf_op jit(solution)/shard_map/all_to_all | solution.py:229
  21.9 9.1 %all-to-all-done.1 = bf16[32,1,8,1024]{3,2,1,0:T(8,128)(2,1)S(1)} async-done(((bf16[32,1,8,1024]{3,2,1,0:T(8,128)(2,1)}), bf16[32,1,8,1024]{3,2,1,0:T(8,128)(2,1)S(1)}, u32[]{:S(2)}, u32[]{:S(2)}) %all-to-all-start.1) | async-done | bytes 524320 | tf_op jit(solution)/shard_map/all_to_all | solution.py:229
  30.9 1.5 broadcast_in_dim.46
  32.5 7.1 %all-to-all-start = ((bf16[32,128,256]{2,1,0:T(8,128)(2,1)}), bf16[32,128,256]{2,1,0:T(8,128)(2,1)}, u32[]{:S(2)}, u32[]{:S(2)}) async-start(bf16[32,128,256]{2,1,0:T(8,128)(2,1)} %broadcast_in_dim.46), calls=%async_computation | async-start | bytes 4194304 | tf_op jit(solution)/shard_map/all_to_all | solution.py:206
  39.6 0.6 dynamic_slice.10
  40.3 33.6 %all-gather = f32[16,1,512]{2,1,0:T(1,128)S(1)} all-gather(f32[1,1,512]{2,1,0:T(1,128)S(1)} %bitcast.57), channel_id=1, replica_groups=mesh['ctx'=32,'tp'=16] {'tp'}, dimensions={0}, use_global_device_ids=true | all-gather | bytes 34816 | tf_op jit(solution)/shard_map/all_gather | solution.py:199
  74.0 1.3 gather_fusion.1
  75.3 64.6 %shard_map.100 = bf16[16,16,8,1024]{3,2,1,0:T(8,128)(2,1)} custom-call(bf16[16,8,1024]{2,1,0:T(8,128)(2,1)} %gather_fusion.1), custom_call_target="tpu_custom_call" | custom-call | tf_op jit(solution)/shard_map/pallas_call | solution.py:84
  139.9 2.7 %copy.16 = bf16[16,16,8,1024]{3,2,1,0:T(8,128)(2,1)S(1)} copy(bf16[16,16,8,1024]{3,2,0,1:T(8,128)(2,1)} %bitcast.42) | data formatting | bytes 8388608 | tf_op jit(solution)/shard_map/transpose | solution.py:239
  142.6 1.3 convolution_convert_fusion.2
  143.9 1.3 convolution_convert_fusion.1
  145.2 2.1 collective-permute-start
  147.3 0.7 pad_add_fusion
  148.2 6.9 %collective-permute-done = bf16[2,2,128,256]{3,2,1,0:T(8,128)(2,1)S(1)} collective-permute-done((bf16[2,2,128,256]{3,2,1,0:T(8,128)(2,1)S(1)}, bf16[2,2,128,256]{3,2,1,0:T(8,128)(2,1)S(1)}, u32[]{:S(2)}, u32[]{:S(2)}) %collective-permute-start) | collective-permute-done | bytes 262176 | tf_op jit(solution)/shard_map/ppermute | solution.py:23
  155.2 1.1 pad_maximum_fusion.1
  156.3 4.2 %fusion.4 = bf16[512,256]{1,0:T(8,128)(2,1)S(1)} fusion(bf16[4096,256]{1,0:T(8,128)(2,1)} %bitcast.1, bf16[512,4096]{1,0:T(8,128)(2,1)} %all-gather.3.cloned.1.call-done, f32[4096]{0:T(1024)S(1)} %copy-done.6, f32[512]{0:T(512)S(1)} %add_rsqrt_fusion), kind=kOutput, calls=%fused_computation.12 | convolution fusion | flops 1082392576 | bytes 6572032 | tf_op jit(solution)/shard_map/dot_general | solution.py:213
  162.8 3.2 %convolution_convert_fusion = bf16[512,4096]{1,0:T(8,128)(2,1)} fusion(bf16[256,4096]{1,0:T(8,128)(2,1)S(1)} %copy-done, bf16[576,256]{1,0:T(8,128)(2,1)S(1)} %bitcast.54, pred[512]{0:T(512)(128)(4,1)S(1)} %fusion.30), kind=kOutput, calls=%fused_computation.3 | convolution fusion | flops 1075970048 | bytes 6554112 | tf_op jit(solution)/shard_map/dot_general | solution.py:292
  166.1 50.4 %shard_map.101 = bf16[32,4096]{1,0:T(8,128)(2,1)} custom-call(bf16[16,32,4096]{2,1,0:T(8,128)(2,1)} %bitcast.41), custom_call_target="tpu_custom_call" | custom-call | tf_op jit(solution)/shard_map/pallas_call | solution.py:155
  216.4 1.7 copy.18
  (55 shorter events, 3.8 us)
Async XLA Ops:
  6.5 156.3 %copy-start = (bf16[256,4096]{1,0:T(8,128)(2,1)S(1)}, bf16[256,4096]{1,0:T(8,128)(2,1)}, u32[]{:S(2)}) copy-start(bf16[256,4096]{1,0:T(8,128)(2,1)} %param.15) | copy-start | bytes 6291460
  6.5 15.2 %copy-start.2 = (bf16[512,256]{1,0:T(8,128)(2,1)S(1)}, bf16[512,256]{1,0:T(8,128)(2,1)}, u32[]{:S(2)}) copy-start(bf16[512,256]{1,0:T(8,128)(2,1)} %param.10) | copy-start | bytes 786436
  6.5 24.4 %copy-start.3 = (bf16[128,256]{1,0:T(8,128)(2,1)S(1)}, bf16[128,256]{1,0:T(8,128)(2,1)}, u32[]{:S(2)}) copy-start(bf16[128,256]{1,0:T(8,128)(2,1)} %param.12) | copy-start | bytes 196612
  6.5 149.8 %all-gather.3.cloned.1.call-start = ((), (), s32[]{:S(2)}) async-start(), calls=%async_computation.2 | async-start | bytes 4456448 | tf_op jit(solution)/shard_map/all_gather | solution.py:200
  12.2 18.8 %all-to-all-start.1 = ((bf16[32,1,8,1024]{3,2,1,0:T(8,128)(2,1)}), bf16[32,1,8,1024]{3,2,1,0:T(8,128)(2,1)S(1)}, u32[]{:S(2)}, u32[]{:S(2)}) async-start(bf16[32,1,8,1024]{3,2,1,0:T(8,128)(2,1)} %bitcast_multiply_fusion), calls=%async_computation.1 | async-start | bytes 1048576 | tf_op jit(solution)/shard_map/all_to_all | solution.py:229
  32.5 7.2 %copy-start.7 = (s32[256]{0:T(256)S(1)}, s32[256]{0:T(256)}, u32[]{:S(2)}) copy-start(s32[256]{0:T(256)} %param.19) | copy-start | bytes 3076
  32.5 123.8 %all-to-all-start = ((bf16[32,128,256]{2,1,0:T(8,128)(2,1)}), bf16[32,128,256]{2,1,0:T(8,128)(2,1)}, u32[]{:S(2)}, u32[]{:S(2)}) async-start(bf16[32,128,256]{2,1,0:T(8,128)(2,1)} %broadcast_in_dim.46), calls=%async_computation | async-start | bytes 4194304 | tf_op jit(solution)/shard_map/all_to_all | solution.py:206
  139.8 2.7 %copy-start.4 = (bf16[1024,256]{1,0:T(8,128)(2,1)S(1)}, bf16[1024,256]{1,0:T(8,128)(2,1)}, u32[]{:S(2)}) copy-start(bf16[1024,256]{1,0:T(8,128)(2,1)} %param.13) | copy-start | bytes 1572868
  142.6 1.3 copy-start.5
  145.2 9.8 %collective-permute-start = (bf16[2,2,128,256]{3,2,1,0:T(8,128)(2,1)S(1)}, bf16[2,2,128,256]{3,2,1,0:T(8,128)(2,1)S(1)}, u32[]{:S(2)}, u32[]{:S(2)}) collective-permute-start(bf16[2,2,128,256]{3,2,1,0:T(8,128)(2,1)S(1)} %pad_maximum_fusion.3), channel_id=1, source_target_pairs={{0,16},{16,32},{32,48},{48,64},{64,80},{80,96},{96,112},{112,128},... | collective-permute-start | bytes 786440 | tf_op jit(solution)/shard_map/ppermute | solution.py:23
  155.1 1.2 copy-start.6
  160.5 1.4 copy-start.1
Sparse Core Ops, SparseCore 0:
  9.4 119.7 all-gather.2

commit v15 on v12

--- a/solution.py
+++ b/solution.py
@@ -234,7 +234,7 @@
     flat_index = own_sources * slot_cap + own_rank
     picked = incoming.reshape(ctx_count * slot_cap, slice_tokens, enc_width)[flat_index]
     row_total = picked.shape[0]
-    full_rows = jnp.swapaxes(kernel_gather(picked, "tp", "ctx", 0), 0, 1).reshape(
+    full_rows = jnp.swapaxes(kernel_gather(picked, "tp", "ctx", 0, pieces=2), 0, 1).reshape(
         picked.shape[0], -1, picked.shape[2]
     )
     keys = project_rows(full_rows, key_weight).reshape(row_total, -1, head_width)

time: 210 us -> 211 us (level)
  no operation moved by 1% of the time
where the time goes in v15:
time: 211 us; the launch traced here: 210 us
  Pallas kernels  132 us (63%)
  starting transfers between devices  18.4 us (9%)
  waiting for transfers between devices  16.1 us (8%)
  between operations  13.7 us (6%)
  matrix products  11.4 us (5%)
  local copies, waits for them, and re-layouts  10.6 us (5%)
  other arithmetic  8.43 us (4%)
    pallas_call x1, Pallas kernels, kernel_gather(): pl.pallas_call(functools.partial(ring_gather_kernel, count=count, axis=ax...  79.9 us
    pallas_call x1, Pallas kernels, kernel_reduce_scatter(): pl.pallas_call(functools.partial(ring_sum_kernel, count=count, axis=axis,...  52 us
    all_to_all x1, starting transfers between devices, local(): lax.all_to_all(outgoing, 'ctx', split_axis=0, concat_axis=0, tiled=True)  9.29 us
    all_to_all x1, waiting for transfers between devices, local(): lax.all_to_all(outgoing, 'ctx', split_axis=0, concat_axis=0, tiled=True)  8.51 us
    all_to_all x1, starting transfers between devices, local(): lax.all_to_all(jnp.broadcast_to(query_weight[None], (ctx_count,) + query_...  6.99 us
    ppermute x1, waiting for transfers between devices, shifted(): return lax.ppermute(block, axis, route)  6.85 us
  transfers between devices with their start and end apart: 4, of which 2 were waited for; matrix products, arithmetic and copies ran while one was open for 9% of the time, Pallas kernels for 38%

profile of v15, /device:TPU:24, one launch (start us, length us, event | category | flops | bytes accessed | tf_op | source)
XLA Modules:
  0.0 210.5 jit_solution(4431101707300154100)
XLA Ops:
  6.5 0.7 all-gather.2.cloned.1.call-update
  7.3 0.8 copy.15
  8.2 0.9 select_reduce_fusion
  9.7 1.5 gather_fusion
  11.3 0.9 bitcast_multiply_fusion
  12.2 9.3 %all-to-all-start.1 = ((bf16[32,1,8,1024]{3,2,1,0:T(8,128)(2,1)}), bf16[32,1,8,1024]{3,2,1,0:T(8,128)(2,1)S(1)}, u32[]{:S(2)}, u32[]{:S(2)}) async-start(bf16[32,1,8,1024]{3,2,1,0:T(8,128)(2,1)} %bitcast_multiply_fusion), calls=%async_computation.1 | async-start | bytes 1048576 | tf_op jit(solution)/shard_map/all_to_all | solution.py:227
  21.5 0.6 dynamic_slice.10
  22.4 8.5 %all-to-all-done.1 = bf16[32,1,8,1024]{3,2,1,0:T(8,128)(2,1)S(1)} async-done(((bf16[32,1,8,1024]{3,2,1,0:T(8,128)(2,1)}), bf16[32,1,8,1024]{3,2,1,0:T(8,128)(2,1)S(1)}, u32[]{:S(2)}, u32[]{:S(2)}) %all-to-all-start.1) | async-done | bytes 524320 | tf_op jit(solution)/shard_map/all_to_all | solution.py:227
  30.9 1.5 broadcast_in_dim.46
  32.5 7.0 %all-to-all-start = ((bf16[32,128,256]{2,1,0:T(8,128)(2,1)}), bf16[32,128,256]{2,1,0:T(8,128)(2,1)}, u32[]{:S(2)}, u32[]{:S(2)}) async-start(bf16[32,128,256]{2,1,0:T(8,128)(2,1)} %broadcast_in_dim.46), calls=%async_computation | async-start | bytes 4194304 | tf_op jit(solution)/shard_map/all_to_all | solution.py:204
  39.5 1.3 gather_fusion.1
  40.7 79.9 %shard_map.100 = bf16[16,16,8,1024]{3,2,1,0:T(8,128)(2,1)} custom-call(bf16[16,8,1024]{2,1,0:T(8,128)(2,1)} %gather_fusion.1), custom_call_target="tpu_custom_call" | custom-call | tf_op jit(solution)/shard_map/pallas_call | solution.py:84
  120.7 2.7 %copy.16 = bf16[16,16,8,1024]{3,2,1,0:T(8,128)(2,1)S(1)} copy(bf16[16,16,8,1024]{3,2,0,1:T(8,128)(2,1)} %bitcast.41) | data formatting | bytes 8388608 | tf_op jit(solution)/shard_map/transpose | solution.py:237
  123.4 1.3 convolution_convert_fusion.2
  124.7 1.3 convolution_convert_fusion.1
  126.0 2.1 collective-permute-start
  128.2 0.7 pad_add_fusion
  129.0 6.9 %collective-permute-done = bf16[2,2,128,256]{3,2,1,0:T(8,128)(2,1)S(1)} collective-permute-done((bf16[2,2,128,256]{3,2,1,0:T(8,128)(2,1)S(1)}, bf16[2,2,128,256]{3,2,1,0:T(8,128)(2,1)S(1)}, u32[]{:S(2)}, u32[]{:S(2)}) %collective-permute-start) | collective-permute-done | bytes 262176 | tf_op jit(solution)/shard_map/ppermute | solution.py:23
  136.0 1.1 pad_maximum_fusion.1
  137.1 3.1 %fusion = f32[512]{0:T(512)S(1)} fusion(bf16[512,4096]{1,0:T(8,128)(2,1)} %all-gather.2.cloned.1.call-done), kind=kLoop, calls=%fused_computation.4 | loop fusion | flops 6290944 | bytes 4196352 | tf_op jit(solution)/shard_map/reduce_sum | solution.py:200
  140.2 4.2 %fusion.10 = bf16[512,256]{1,0:T(8,128)(2,1)S(1)} fusion(bf16[4096,256]{1,0:T(8,128)(2,1)} %bitcast, bf16[512,4096]{1,0:T(8,128)(2,1)} %all-gather.2.cloned.1.call-done, f32[4096]{0:T(1024)S(1)} %copy-done.5, f32[512]{0:T(512)S(1)} %add_rsqrt_fusion), kind=kOutput, calls=%fused_computation.16 | convolution fusion | flops 1082392576 | bytes 6572032 | tf_op jit(solution)/shard_map/dot_general | solution.py:211
  146.7 3.2 %convolution_convert_fusion = bf16[512,4096]{1,0:T(8,128)(2,1)} fusion(bf16[256,4096]{1,0:T(8,128)(2,1)S(1)} %copy-done, bf16[576,256]{1,0:T(8,128)(2,1)S(1)} %bitcast.53, pred[512]{0:T(512)(128)(4,1)S(1)} %fusion.38), kind=kOutput, calls=%fused_computation.7 | convolution fusion | flops 1075970048 | bytes 6554112 | tf_op jit(solution)/shard_map/dot_general | solution.py:290
  150.0 52.0 %shard_map.101 = bf16[32,4096]{1,0:T(8,128)(2,1)} custom-call(bf16[16,32,4096]{2,1,0:T(8,128)(2,1)} %bitcast.40), custom_call_target="tpu_custom_call" | custom-call | tf_op jit(solution)/shard_map/pallas_call | solution.py:155
  202.0 1.7 copy.18
  (51 shorter events, 3.6 us)
Async XLA Ops:
  6.5 140.2 %copy-start = (bf16[256,4096]{1,0:T(8,128)(2,1)S(1)}, bf16[256,4096]{1,0:T(8,128)(2,1)}, u32[]{:S(2)}) copy-start(bf16[256,4096]{1,0:T(8,128)(2,1)} %param.15) | copy-start | bytes 6291460
  6.5 14.9 %copy-start.6 = (s32[256]{0:T(256)S(1)}, s32[256]{0:T(256)}, u32[]{:S(2)}) copy-start(s32[256]{0:T(256)} %param.19) | copy-start | bytes 3076
  6.5 24.4 %copy-start.2 = (bf16[128,256]{1,0:T(8,128)(2,1)S(1)}, bf16[128,256]{1,0:T(8,128)(2,1)}, u32[]{:S(2)}) copy-start(bf16[128,256]{1,0:T(8,128)(2,1)} %param.12) | copy-start | bytes 196612
  6.5 130.6 %all-gather.2.cloned.1.call-start = ((), (), s32[]{:S(2)}) async-start(), calls=%async_computation.2 | async-start | bytes 4456448 | tf_op jit(solution)/shard_map/all_gather | solution.py:198
  12.2 18.8 %all-to-all-start.1 = ((bf16[32,1,8,1024]{3,2,1,0:T(8,128)(2,1)}), bf16[32,1,8,1024]{3,2,1,0:T(8,128)(2,1)S(1)}, u32[]{:S(2)}, u32[]{:S(2)}) async-start(bf16[32,1,8,1024]{3,2,1,0:T(8,128)(2,1)} %bitcast_multiply_fusion), calls=%async_computation.1 | async-start | bytes 1048576 | tf_op jit(solution)/shard_map/all_to_all | solution.py:227
  32.5 107.7 %all-to-all-start = ((bf16[32,128,256]{2,1,0:T(8,128)(2,1)}), bf16[32,128,256]{2,1,0:T(8,128)(2,1)}, u32[]{:S(2)}, u32[]{:S(2)}) async-start(bf16[32,128,256]{2,1,0:T(8,128)(2,1)} %broadcast_in_dim.46), calls=%async_computation | async-start | bytes 4194304 | tf_op jit(solution)/shard_map/all_to_all | solution.py:204
  120.7 2.7 %copy-start.3 = (bf16[1024,256]{1,0:T(8,128)(2,1)S(1)}, bf16[1024,256]{1,0:T(8,128)(2,1)}, u32[]{:S(2)}) copy-start(bf16[1024,256]{1,0:T(8,128)(2,1)} %param.13) | copy-start | bytes 1572868
  123.4 1.3 copy-start.4
  126.0 9.8 %collective-permute-start = (bf16[2,2,128,256]{3,2,1,0:T(8,128)(2,1)S(1)}, bf16[2,2,128,256]{3,2,1,0:T(8,128)(2,1)S(1)}, u32[]{:S(2)}, u32[]{:S(2)}) collective-permute-start(bf16[2,2,128,256]{3,2,1,0:T(8,128)(2,1)S(1)} %pad_maximum_fusion.3), channel_id=1, source_target_pairs={{0,16},{16,32},{32,48},{48,64},{64,80},{80,96},{96,112},{112,128},... | collective-permute-start | bytes 786440 | tf_op jit(solution)/shard_map/ppermute | solution.py:23
  137.1 3.1 %copy-start.5 = (f32[4096]{0:T(1024)S(1)}, f32[4096]{0:T(1024)}, u32[]{:S(2)}) copy-start(f32[4096]{0:T(1024)} %param.11) | copy-start | bytes 49156
  144.4 1.4 copy-start.1
Sparse Core Ops, SparseCore 0:
  9.4 122.7 all-gather.1

commit v16 on v12

--- a/solution.py
+++ b/solution.py
@@ -290,7 +290,7 @@
     mixed_part = jnp.dot(attended, out_weight, preferred_element_type=jnp.float32).astype(
         jnp.bfloat16
     )
-    return kernel_reduce_scatter(mixed_part, "tp", "ctx", 1)
+    return kernel_reduce_scatter(mixed_part, "tp", "ctx", 1, pieces=8)
 
 
 def solution(mesh):

time: 210 us -> 211 us (level)
  no operation moved by 1% of the time
where the time goes in v16:
time: 211 us; the launch traced here: 210 us
  Pallas kernels  132 us (63%)
  starting transfers between devices  18.4 us (9%)
  waiting for transfers between devices  16.1 us (8%)
  between operations  13.7 us (6%)
  matrix products  11.4 us (5%)
  local copies, waits for them, and re-layouts  10.6 us (5%)
  other arithmetic  8.43 us (4%)
    pallas_call x1, Pallas kernels, kernel_gather(): pl.pallas_call(functools.partial(ring_gather_kernel, count=count, axis=ax...  80.4 us
    pallas_call x1, Pallas kernels, kernel_reduce_scatter(): pl.pallas_call(functools.partial(ring_sum_kernel, count=count, axis=axis,...  51.5 us
    all_to_all x1, starting transfers between devices, local(): lax.all_to_all(outgoing, 'ctx', split_axis=0, concat_axis=0, tiled=True)  9.29 us
    all_to_all x1, waiting for transfers between devices, local(): lax.all_to_all(outgoing, 'ctx', split_axis=0, concat_axis=0, tiled=True)  8.51 us
    all_to_all x1, starting transfers between devices, local(): lax.all_to_all(jnp.broadcast_to(query_weight[None], (ctx_count,) + query_...  6.99 us
    ppermute x1, waiting for transfers between devices, shifted(): return lax.ppermute(block, axis, route)  6.85 us
  transfers between devices with their start and end apart: 4, of which 2 were waited for; matrix products, arithmetic and copies ran while one was open for 9% of the time, Pallas kernels for 38%

profile of v16, /device:TPU:24, one launch (start us, length us, event | category | flops | bytes accessed | tf_op | source)
XLA Modules:
  0.0 210.4 jit_solution(13672138183708136032)
XLA Ops:
  6.5 0.7 all-gather.2.cloned.1.call-update
  7.3 0.8 copy.15
  8.2 0.9 select_reduce_fusion
  9.7 1.5 gather_fusion
  11.3 0.9 bitcast_multiply_fusion
  12.2 9.3 %all-to-all-start.1 = ((bf16[32,1,8,1024]{3,2,1,0:T(8,128)(2,1)}), bf16[32,1,8,1024]{3,2,1,0:T(8,128)(2,1)S(1)}, u32[]{:S(2)}, u32[]{:S(2)}) async-start(bf16[32,1,8,1024]{3,2,1,0:T(8,128)(2,1)} %bitcast_multiply_fusion), calls=%async_computation.1 | async-start | bytes 1048576 | tf_op jit(solution)/shard_map/all_to_all | solution.py:227
  21.5 0.6 dynamic_slice.10
  22.4 8.5 %all-to-all-done.1 = bf16[32,1,8,1024]{3,2,1,0:T(8,128)(2,1)S(1)} async-done(((bf16[32,1,8,1024]{3,2,1,0:T(8,128)(2,1)}), bf16[32,1,8,1024]{3,2,1,0:T(8,128)(2,1)S(1)}, u32[]{:S(2)}, u32[]{:S(2)}) %all-to-all-start.1) | async-done | bytes 524320 | tf_op jit(solution)/shard_map/all_to_all | solution.py:227
  30.9 1.5 broadcast_in_dim.46
  32.5 7.0 %all-to-all-start = ((bf16[32,128,256]{2,1,0:T(8,128)(2,1)}), bf16[32,128,256]{2,1,0:T(8,128)(2,1)}, u32[]{:S(2)}, u32[]{:S(2)}) async-start(bf16[32,128,256]{2,1,0:T(8,128)(2,1)} %broadcast_in_dim.46), calls=%async_computation | async-start | bytes 4194304 | tf_op jit(solution)/shard_map/all_to_all | solution.py:204
  39.5 1.3 gather_fusion.1
  40.7 80.4 %shard_map.100 = bf16[16,16,8,1024]{3,2,1,0:T(8,128)(2,1)} custom-call(bf16[16,8,1024]{2,1,0:T(8,128)(2,1)} %gather_fusion.1), custom_call_target="tpu_custom_call" | custom-call | tf_op jit(solution)/shard_map/pallas_call | solution.py:84
  121.1 2.7 %copy.16 = bf16[16,16,8,1024]{3,2,1,0:T(8,128)(2,1)S(1)} copy(bf16[16,16,8,1024]{3,2,0,1:T(8,128)(2,1)} %bitcast.41) | data formatting | bytes 8388608 | tf_op jit(solution)/shard_map/transpose | solution.py:237
  123.8 1.3 convolution_convert_fusion.2
  125.1 1.3 convolution_convert_fusion.1
  126.5 2.1 collective-permute-start
  128.6 0.7 pad_add_fusion
  129.4 6.9 %collective-permute-done = bf16[2,2,128,256]{3,2,1,0:T(8,128)(2,1)S(1)} collective-permute-done((bf16[2,2,128,256]{3,2,1,0:T(8,128)(2,1)S(1)}, bf16[2,2,128,256]{3,2,1,0:T(8,128)(2,1)S(1)}, u32[]{:S(2)}, u32[]{:S(2)}) %collective-permute-start) | collective-permute-done | bytes 262176 | tf_op jit(solution)/shard_map/ppermute | solution.py:23
  136.4 1.1 pad_maximum_fusion.1
  137.5 3.1 %fusion = f32[512]{0:T(512)S(1)} fusion(bf16[512,4096]{1,0:T(8,128)(2,1)} %all-gather.2.cloned.1.call-done), kind=kLoop, calls=%fused_computation.4 | loop fusion | flops 6290944 | bytes 4196352 | tf_op jit(solution)/shard_map/reduce_sum | solution.py:200
  140.7 4.2 %fusion.10 = bf16[512,256]{1,0:T(8,128)(2,1)S(1)} fusion(bf16[4096,256]{1,0:T(8,128)(2,1)} %bitcast, bf16[512,4096]{1,0:T(8,128)(2,1)} %all-gather.2.cloned.1.call-done, f32[4096]{0:T(1024)S(1)} %copy-done.5, f32[512]{0:T(512)S(1)} %add_rsqrt_fusion), kind=kOutput, calls=%fused_computation.16 | convolution fusion | flops 1082392576 | bytes 6572032 | tf_op jit(solution)/shard_map/dot_general | solution.py:211
  147.2 3.2 %convolution_convert_fusion = bf16[512,4096]{1,0:T(8,128)(2,1)} fusion(bf16[256,4096]{1,0:T(8,128)(2,1)S(1)} %copy-done, bf16[576,256]{1,0:T(8,128)(2,1)S(1)} %bitcast.53, pred[512]{0:T(512)(128)(4,1)S(1)} %fusion.38), kind=kOutput, calls=%fused_computation.7 | convolution fusion | flops 1075970048 | bytes 6554112 | tf_op jit(solution)/shard_map/dot_general | solution.py:290
  150.4 51.5 %shard_map.101 = bf16[32,4096]{1,0:T(8,128)(2,1)} custom-call(bf16[16,32,4096]{2,1,0:T(8,128)(2,1)} %bitcast.40), custom_call_target="tpu_custom_call" | custom-call | tf_op jit(solution)/shard_map/pallas_call | solution.py:155
  201.9 1.7 copy.18
  (51 shorter events, 3.6 us)
Async XLA Ops:
  6.5 140.6 %copy-start = (bf16[256,4096]{1,0:T(8,128)(2,1)S(1)}, bf16[256,4096]{1,0:T(8,128)(2,1)}, u32[]{:S(2)}) copy-start(bf16[256,4096]{1,0:T(8,128)(2,1)} %param.15) | copy-start | bytes 6291460
  6.5 14.9 %copy-start.6 = (s32[256]{0:T(256)S(1)}, s32[256]{0:T(256)}, u32[]{:S(2)}) copy-start(s32[256]{0:T(256)} %param.19) | copy-start | bytes 3076
  6.5 24.4 %copy-start.2 = (bf16[128,256]{1,0:T(8,128)(2,1)S(1)}, bf16[128,256]{1,0:T(8,128)(2,1)}, u32[]{:S(2)}) copy-start(bf16[128,256]{1,0:T(8,128)(2,1)} %param.12) | copy-start | bytes 196612
  6.5 131.0 %all-gather.2.cloned.1.call-start = ((), (), s32[]{:S(2)}) async-start(), calls=%async_computation.2 | async-start | bytes 4456448 | tf_op jit(solution)/shard_map/all_gather | solution.py:198
  12.2 18.8 %all-to-all-start.1 = ((bf16[32,1,8,1024]{3,2,1,0:T(8,128)(2,1)}), bf16[32,1,8,1024]{3,2,1,0:T(8,128)(2,1)S(1)}, u32[]{:S(2)}, u32[]{:S(2)}) async-start(bf16[32,1,8,1024]{3,2,1,0:T(8,128)(2,1)} %bitcast_multiply_fusion), calls=%async_computation.1 | async-start | bytes 1048576 | tf_op jit(solution)/shard_map/all_to_all | solution.py:227
  32.5 108.2 %all-to-all-start = ((bf16[32,128,256]{2,1,0:T(8,128)(2,1)}), bf16[32,128,256]{2,1,0:T(8,128)(2,1)}, u32[]{:S(2)}, u32[]{:S(2)}) async-start(bf16[32,128,256]{2,1,0:T(8,128)(2,1)} %broadcast_in_dim.46), calls=%async_computation | async-start | bytes 4194304 | tf_op jit(solution)/shard_map/all_to_all | solution.py:204
  121.1 2.7 %copy-start.3 = (bf16[1024,256]{1,0:T(8,128)(2,1)S(1)}, bf16[1024,256]{1,0:T(8,128)(2,1)}, u32[]{:S(2)}) copy-start(bf16[1024,256]{1,0:T(8,128)(2,1)} %param.13) | copy-start | bytes 1572868
  123.8 1.3 copy-start.4
  126.5 9.8 %collective-permute-start = (bf16[2,2,128,256]{3,2,1,0:T(8,128)(2,1)S(1)}, bf16[2,2,128,256]{3,2,1,0:T(8,128)(2,1)S(1)}, u32[]{:S(2)}, u32[]{:S(2)}) collective-permute-start(bf16[2,2,128,256]{3,2,1,0:T(8,128)(2,1)S(1)} %pad_maximum_fusion.3), channel_id=1, source_target_pairs={{0,16},{16,32},{32,48},{48,64},{64,80},{80,96},{96,112},{112,128},... | collective-permute-start | bytes 786440 | tf_op jit(solution)/shard_map/ppermute | solution.py:23
  137.5 3.1 %copy-start.5 = (f32[4096]{0:T(1024)S(1)}, f32[4096]{0:T(1024)}, u32[]{:S(2)}) copy-start(f32[4096]{0:T(1024)} %param.11) | copy-start | bytes 49156
  144.8 1.4 copy-start.1
Sparse Core Ops, SparseCore 0:
  9.4 123.5 all-gather.1

commit v17 on v12

--- a/solution.py
+++ b/solution.py
@@ -201,15 +201,6 @@
     normed = (values_wide * lax.rsqrt(mean_square + epsilon) * norm_gain[None, :]).astype(
         jnp.bfloat16
     )
-    query_full = lax.all_to_all(
-        jnp.broadcast_to(query_weight[None], (ctx_count,) + query_weight.shape),
-        "ctx",
-        split_axis=0,
-        concat_axis=0,
-        tiled=True,
-    ).reshape(-1, query_weight.shape[1])
-    query_sum = jnp.dot(normed, query_full, preferred_element_type=jnp.float32)
-    queries = (query_sum * HS ** (-0.5)).astype(jnp.bfloat16)
     matches = neighbour_ids.reshape(-1)[:, None] == jnp.arange(row_place.shape[0])[None, :]
     storage = jnp.sum(jnp.where(matches, row_place[None, :], 0), axis=1).reshape(
         ctx_count, rows_dev
@@ -237,6 +228,16 @@
     full_rows = jnp.swapaxes(kernel_gather(picked, "tp", "ctx", 0), 0, 1).reshape(
         picked.shape[0], -1, picked.shape[2]
     )
+    query_source, full_rows = lax.optimization_barrier((query_weight, full_rows))
+    query_full = lax.all_to_all(
+        jnp.broadcast_to(query_source[None], (ctx_count,) + query_weight.shape),
+        "ctx",
+        split_axis=0,
+        concat_axis=0,
+        tiled=True,
+    ).reshape(-1, query_weight.shape[1])
+    query_sum = jnp.dot(normed, query_full, preferred_element_type=jnp.float32)
+    queries = (query_sum * HS ** (-0.5)).astype(jnp.bfloat16)
     keys = project_rows(full_rows, key_weight).reshape(row_total, -1, head_width)
     values = project_rows(full_rows, value_weight).reshape(row_total, -1, head_width)
     neighbour_len = keys.shape[1]

time: 210 us -> 229 us (1.090)
  waiting for transfers between devices: 16.1 us -> 29.1 us
  local copies, waits for them, and re-layouts: 10.6 us -> 14.1 us
  matrix products: 11.4 us -> 13.8 us
    ppermute x1, waiting for transfers between devices: 6.85 us -> 21.2 us  [shifted(): return lax.ppermute(block, axis, route)]
    reshape x0 -> x1, local copies, waits for them, and re-layouts: none -> 4.83 us  [local(): jnp.swapaxes(kernel_gather(picked, 'tp', 'ctx', 0), 0, 1)]
    transpose x1 -> x0, local copies, waits for them, and re-layouts: 2.69 us -> none  [local(): jnp.swapaxes(kernel_gather(picked, 'tp', 'ctx', 0), 0, 1)]
    dot_general x2, matrix products: 2.57 us -> 4.88 us  [project_rows(): jnp.dot(flat, weight, preferred_element_type=jnp.float32)]
  transfers between devices with their start and end apart: 4 -> 4, of which waited for: 2 -> 2; matrix products, arithmetic and copies ran while one was open for 9% -> 11% of each run, Pallas kernels for 38% -> 35%
where the time goes in v17:
time: 229 us; the launch traced here: 228 us
  Pallas kernels  131 us (57%)
  waiting for transfers between devices  29.1 us (13%)
  starting transfers between devices  18.2 us (8%)
  local copies, waits for them, and re-layouts  14.1 us (6%)
  matrix products  13.8 us (6%)
  between operations  13.7 us (6%)
  other arithmetic  8.42 us (4%)
    pallas_call x1, Pallas kernels, kernel_gather(): pl.pallas_call(functools.partial(ring_gather_kernel, count=count, axis=ax...  79.9 us
    pallas_call x1, Pallas kernels, kernel_reduce_scatter(): pl.pallas_call(functools.partial(ring_sum_kernel, count=count, axis=axis,...  50.9 us
    ppermute x1, waiting for transfers between devices, shifted(): return lax.ppermute(block, axis, route)  21.2 us
    all_to_all x1, starting transfers between devices, local(): lax.all_to_all(outgoing, 'ctx', split_axis=0, concat_axis=0, tiled=True)  9.29 us
    all_to_all x1, waiting for transfers between devices, local(): lax.all_to_all(outgoing, 'ctx', split_axis=0, concat_axis=0, tiled=True)  7.16 us
    all_to_all x1, starting transfers between devices, local(): lax.all_to_all(jnp.broadcast_to(query_source[None], (ctx_count,) + query_...  6.63 us
    dot_general x2, matrix products, project_rows(): jnp.dot(flat, weight, preferred_element_type=jnp.float32)  4.88 us
    reshape x1, local copies, waits for them, and re-layouts, local(): jnp.swapaxes(kernel_gather(picked, 'tp', 'ctx', 0), 0, 1)  4.83 us
  transfers between devices with their start and end apart: 4, of which 2 were waited for; matrix products, arithmetic and copies ran while one was open for 11% of the time, Pallas kernels for 35%

profile of v17, /device:TPU:24, one launch (start us, length us, event | category | flops | bytes accessed | tf_op | source)
XLA Modules:
  0.0 228.0 jit_solution(9537081519287085230)
XLA Ops:
  6.5 0.7 all-gather.2.cloned.1.call-update
  7.3 0.8 copy.15
  8.2 0.9 select_reduce_fusion
  9.7 1.5 gather_fusion
  11.3 0.9 bitcast_multiply_fusion
  12.2 9.3 %all-to-all-start = ((bf16[32,1,8,1024]{3,2,1,0:T(8,128)(2,1)}), bf16[32,1,8,1024]{3,2,1,0:T(8,128)(2,1)S(1)}, u32[]{:S(2)}, u32[]{:S(2)}) async-start(bf16[32,1,8,1024]{3,2,1,0:T(8,128)(2,1)} %bitcast_multiply_fusion), calls=%async_computation | async-start | bytes 1048576 | tf_op jit(solution)/shard_map/all_to_all | solution.py:218
  21.5 0.8 dynamic_slice.11
  22.2 1.3 dynamic_slice.10
  23.8 7.2 %all-to-all-done = bf16[32,1,8,1024]{3,2,1,0:T(8,128)(2,1)S(1)} async-done(((bf16[32,1,8,1024]{3,2,1,0:T(8,128)(2,1)}), bf16[32,1,8,1024]{3,2,1,0:T(8,128)(2,1)S(1)}, u32[]{:S(2)}, u32[]{:S(2)}) %all-to-all-start) | async-done | bytes 524320 | tf_op jit(solution)/shard_map/all_to_all | solution.py:218
  30.9 1.3 gather_fusion.1
  32.2 79.9 %shard_map.100 = bf16[16,16,8,1024]{3,2,1,0:T(8,128)(2,1)} custom-call(bf16[16,8,1024]{2,1,0:T(8,128)(2,1)} %gather_fusion.1), custom_call_target="tpu_custom_call" | custom-call | tf_op jit(solution)/shard_map/pallas_call | solution.py:84
  112.1 4.8 %copy_bitcast_fusion = bf16[16,128,1024]{2,1,0:T(8,128)(2,1)} fusion(bf16[16,16,8,1024]{3,2,1,0:T(8,128)(2,1)} %shard_map.100), kind=kLoop, calls=%fused_computation.9 | loop fusion | bytes 8388608 | tf_op jit(solution)/shard_map/reshape | solution.py:228
  116.9 1.5 broadcast_in_dim.77
  118.5 6.6 %all-to-all-start.1 = ((bf16[32,128,256]{2,1,0:T(8,128)(2,1)}), bf16[32,128,256]{2,1,0:T(8,128)(2,1)}, u32[]{:S(2)}, u32[]{:S(2)}) async-start(bf16[32,128,256]{2,1,0:T(8,128)(2,1)} %broadcast_in_dim.77), calls=%async_computation.1 | async-start | bytes 4194304 | tf_op jit(solution)/shard_map/all_to_all | solution.py:232
  125.1 3.6 %convolution_convert_fusion.1 = bf16[2048,256]{1,0:T(8,128)(2,1)S(1)} fusion(bf16[2048,1024]{1,0:T(8,128)(2,1)} %bitcast.47, bf16[1024,256]{1,0:T(8,128)(2,1)S(1)} %copy-done.4), kind=kOutput, calls=%fused_computation.12 | convolution fusion | flops 1074266112 | bytes 5767168 | tf_op jit(solution)/shard_map/dot_general | solution.py:173
  128.8 1.3 convolution_convert_fusion.2
  130.1 2.2 collective-permute-start
  133.2 21.2 %collective-permute-done = bf16[2,2,128,256]{3,2,1,0:T(8,128)(2,1)S(1)} collective-permute-done((bf16[2,2,128,256]{3,2,1,0:T(8,128)(2,1)S(1)}, bf16[2,2,128,256]{3,2,1,0:T(8,128)(2,1)S(1)}, u32[]{:S(2)}, u32[]{:S(2)}) %collective-permute-start) | collective-permute-done | bytes 262176 | tf_op jit(solution)/shard_map/ppermute | solution.py:23
  154.4 1.1 pad_maximum_fusion.1
  155.7 3.1 %fusion = f32[512]{0:T(512)S(1)} fusion(bf16[512,4096]{1,0:T(8,128)(2,1)} %all-gather.2.cloned.1.call-done), kind=kLoop, calls=%fused_computation.4 | loop fusion | flops 6290944 | bytes 4196352 | tf_op jit(solution)/shard_map/reduce_sum | solution.py:200
  158.8 4.3 %fusion.10 = bf16[512,256]{1,0:T(8,128)(2,1)S(1)} fusion(bf16[4096,256]{1,0:T(8,128)(2,1)} %bitcast.10, bf16[512,4096]{1,0:T(8,128)(2,1)} %all-gather.2.cloned.1.call-done, f32[4096]{0:T(1024)S(1)} %copy-done.6, f32[512]{0:T(512)S(1)} %add_rsqrt_fusion), kind=kOutput, calls=%fused_computation.17 | convolution fusion | flops 1082392576 | bytes 6572032 | tf_op jit(solution)/shard_map/dot_general | solution.py:239
  165.4 3.2 %convolution_convert_fusion = bf16[512,4096]{1,0:T(8,128)(2,1)} fusion(bf16[256,4096]{1,0:T(8,128)(2,1)S(1)} %copy-done, bf16[576,256]{1,0:T(8,128)(2,1)S(1)} %bitcast.56, pred[512]{0:T(512)(128)(4,1)S(1)} %fusion.38), kind=kOutput, calls=%fused_computation.7 | convolution fusion | flops 1075970048 | bytes 6554112 | tf_op jit(solution)/shard_map/dot_general | solution.py:291
  168.6 50.9 %shard_map.101 = bf16[32,4096]{1,0:T(8,128)(2,1)} custom-call(bf16[16,32,4096]{2,1,0:T(8,128)(2,1)} %bitcast.44), custom_call_target="tpu_custom_call" | custom-call | tf_op jit(solution)/shard_map/pallas_call | solution.py:155
  219.5 1.7 copy.19
  (51 shorter events, 4.3 us)
Async XLA Ops:
  6.5 158.8 %copy-start = (bf16[256,4096]{1,0:T(8,128)(2,1)S(1)}, bf16[256,4096]{1,0:T(8,128)(2,1)}, u32[]{:S(2)}) copy-start(bf16[256,4096]{1,0:T(8,128)(2,1)} %param.15) | copy-start | bytes 6291460
  6.5 149.1 %all-gather.2.cloned.1.call-start = ((), (), s32[]{:S(2)}) async-start(), calls=%async_computation.2 | async-start | bytes 4456448 | tf_op jit(solution)/shard_map/all_gather | solution.py:198
  12.2 18.8 %all-to-all-start = ((bf16[32,1,8,1024]{3,2,1,0:T(8,128)(2,1)}), bf16[32,1,8,1024]{3,2,1,0:T(8,128)(2,1)S(1)}, u32[]{:S(2)}, u32[]{:S(2)}) async-start(bf16[32,1,8,1024]{3,2,1,0:T(8,128)(2,1)} %bitcast_multiply_fusion), calls=%async_computation | async-start | bytes 1048576 | tf_op jit(solution)/shard_map/all_to_all | solution.py:218
  112.1 4.8 %copy-start.3 = (bf16[128,256]{1,0:T(8,128)(2,1)S(1)}, bf16[128,256]{1,0:T(8,128)(2,1)}, u32[]{:S(2)}) copy-start(bf16[128,256]{1,0:T(8,128)(2,1)} %param.12) | copy-start | bytes 196612
  116.9 8.2 %copy-start.4 = (bf16[1024,256]{1,0:T(8,128)(2,1)S(1)}, bf16[1024,256]{1,0:T(8,128)(2,1)}, u32[]{:S(2)}) copy-start(bf16[1024,256]{1,0:T(8,128)(2,1)} %param.14) | copy-start | bytes 1572868
  118.5 40.3 %all-to-all-start.1 = ((bf16[32,128,256]{2,1,0:T(8,128)(2,1)}), bf16[32,128,256]{2,1,0:T(8,128)(2,1)}, u32[]{:S(2)}, u32[]{:S(2)}) async-start(bf16[32,128,256]{2,1,0:T(8,128)(2,1)} %broadcast_in_dim.77), calls=%async_computation.1 | async-start | bytes 4194304 | tf_op jit(solution)/shard_map/all_to_all | solution.py:232
  125.1 3.7 %copy-start.1 = (bf16[16,128,1024]{2,1,0:T(8,128)(2,1)S(1)}, bf16[16,128,1024]{2,1,0:T(8,128)(2,1)}, u32[]{:S(2)}) copy-start(bf16[16,128,1024]{2,1,0:T(8,128)(2,1)} %copy_bitcast_fusion) | copy-start | bytes 12582916
  125.1 3.7 %copy-start.5 = (bf16[1024,256]{1,0:T(8,128)(2,1)S(1)}, bf16[1024,256]{1,0:T(8,128)(2,1)}, u32[]{:S(2)}) copy-start(bf16[1024,256]{1,0:T(8,128)(2,1)} %param.13) | copy-start | bytes 1572868
  130.1 24.3 %collective-permute-start = (bf16[2,2,128,256]{3,2,1,0:T(8,128)(2,1)S(1)}, bf16[2,2,128,256]{3,2,1,0:T(8,128)(2,1)S(1)}, u32[]{:S(2)}, u32[]{:S(2)}) collective-permute-start(bf16[2,2,128,256]{3,2,1,0:T(8,128)(2,1)S(1)} %pad_maximum_fusion.3), channel_id=1, source_target_pairs={{0,16},{16,32},{32,48},{48,64},{64,80},{80,96},{96,112},{112,128},... | collective-permute-start | bytes 786440 | tf_op jit(solution)/shard_map/ppermute | solution.py:23
  154.4 4.4 %copy-start.6 = (f32[4096]{0:T(1024)S(1)}, f32[4096]{0:T(1024)}, u32[]{:S(2)}) copy-start(f32[4096]{0:T(1024)} %param.11) | copy-start | bytes 49156
  158.8 5.6 %copy-start.2 = (bf16[18,128,256]{2,1,0:T(8,128)(2,1)S(1)}, bf16[18,128,256]{2,1,0:T(8,128)(2,1)}, u32[]{:S(2)}) copy-start(bf16[18,128,256]{2,1,0:T(8,128)(2,1)} %pad_maximum_fusion.1) | copy-start | bytes 3538948
Sparse Core Ops, SparseCore 0:
  9.4 124.2 all-gather.1

commit v18 on v15

--- a/solution.py
+++ b/solution.py
@@ -234,7 +234,7 @@
     flat_index = own_sources * slot_cap + own_rank
     picked = incoming.reshape(ctx_count * slot_cap, slice_tokens, enc_width)[flat_index]
     row_total = picked.shape[0]
-    full_rows = jnp.swapaxes(kernel_gather(picked, "tp", "ctx", 0, pieces=2), 0, 1).reshape(
+    full_rows = jnp.swapaxes(kernel_gather(picked, "tp", "ctx", 0, pieces=8), 0, 1).reshape(
         picked.shape[0], -1, picked.shape[2]
     )
     keys = project_rows(full_rows, key_weight).reshape(row_total, -1, head_width)

time: 211 us -> 211 us (level)
  transfers between devices with their start and end apart: 4 -> 4, of which waited for: 2 -> 2; matrix products, arithmetic and copies ran while one was open for 9% -> 9% of each run, Pallas kernels for 38% -> 39%
where the time goes in v18:
time: 211 us
  Pallas kernels  132 us (63%)
  starting transfers between devices  18.4 us (9%)
  waiting for transfers between devices  16.1 us (8%)
  between operations  13.7 us (6%)
  matrix products  11.4 us (5%)
  local copies, waits for them, and re-layouts  10.6 us (5%)
  other arithmetic  8.43 us (4%)
    pallas_call x1, Pallas kernels, kernel_gather(): pl.pallas_call(functools.partial(ring_gather_kernel, count=count, axis=ax...  81.6 us
    pallas_call x1, Pallas kernels, kernel_reduce_scatter(): pl.pallas_call(functools.partial(ring_sum_kernel, count=count, axis=axis,...  50.6 us
    all_to_all x1, starting transfers between devices, local(): lax.all_to_all(outgoing, 'ctx', split_axis=0, concat_axis=0, tiled=True)  9.29 us
    all_to_all x1, waiting for transfers between devices, local(): lax.all_to_all(outgoing, 'ctx', split_axis=0, concat_axis=0, tiled=True)  8.51 us
    all_to_all x1, starting transfers between devices, local(): lax.all_to_all(jnp.broadcast_to(query_weight[None], (ctx_count,) + query_...  6.99 us
    ppermute x1, waiting for transfers between devices, shifted(): return lax.ppermute(block, axis, route)  6.85 us
  transfers between devices with their start and end apart: 4, of which 2 were waited for; matrix products, arithmetic and copies ran while one was open for 9% of the time, Pallas kernels for 39%

profile of v18, /device:TPU:24, one launch (start us, length us, event | category | flops | bytes accessed | tf_op | source)
XLA Modules:
  0.0 210.8 jit_solution(12984520005892497157)
XLA Ops:
  6.5 0.7 all-gather.2.cloned.1.call-update
  7.3 0.8 copy.15
  8.2 0.9 select_reduce_fusion
  9.7 1.5 gather_fusion
  11.3 0.9 bitcast_multiply_fusion
  12.2 9.3 %all-to-all-start.1 = ((bf16[32,1,8,1024]{3,2,1,0:T(8,128)(2,1)}), bf16[32,1,8,1024]{3,2,1,0:T(8,128)(2,1)S(1)}, u32[]{:S(2)}, u32[]{:S(2)}) async-start(bf16[32,1,8,1024]{3,2,1,0:T(8,128)(2,1)} %bitcast_multiply_fusion), calls=%async_computation.1 | async-start | bytes 1048576 | tf_op jit(solution)/shard_map/all_to_all | solution.py:227
  21.5 0.6 dynamic_slice.10
  22.4 8.5 %all-to-all-done.1 = bf16[32,1,8,1024]{3,2,1,0:T(8,128)(2,1)S(1)} async-done(((bf16[32,1,8,1024]{3,2,1,0:T(8,128)(2,1)}), bf16[32,1,8,1024]{3,2,1,0:T(8,128)(2,1)S(1)}, u32[]{:S(2)}, u32[]{:S(2)}) %all-to-all-start.1) | async-done | bytes 524320 | tf_op jit(solution)/shard_map/all_to_all | solution.py:227
  30.9 1.5 broadcast_in_dim.46
  32.5 7.0 %all-to-all-start = ((bf16[32,128,256]{2,1,0:T(8,128)(2,1)}), bf16[32,128,256]{2,1,0:T(8,128)(2,1)}, u32[]{:S(2)}, u32[]{:S(2)}) async-start(bf16[32,128,256]{2,1,0:T(8,128)(2,1)} %broadcast_in_dim.46), calls=%async_computation | async-start | bytes 4194304 | tf_op jit(solution)/shard_map/all_to_all | solution.py:204
  39.5 1.3 gather_fusion.1
  40.7 81.6 %shard_map.100 = bf16[16,16,8,1024]{3,2,1,0:T(8,128)(2,1)} custom-call(bf16[16,8,1024]{2,1,0:T(8,128)(2,1)} %gather_fusion.1), custom_call_target="tpu_custom_call" | custom-call | tf_op jit(solution)/shard_map/pallas_call | solution.py:84
  122.4 2.7 %copy.16 = bf16[16,16,8,1024]{3,2,1,0:T(8,128)(2,1)S(1)} copy(bf16[16,16,8,1024]{3,2,0,1:T(8,128)(2,1)} %bitcast.41) | data formatting | bytes 8388608 | tf_op jit(solution)/shard_map/transpose | solution.py:237
  125.1 1.3 convolution_convert_fusion.2
  126.4 1.3 convolution_convert_fusion.1
  127.8 2.1 collective-permute-start
  129.9 0.7 pad_add_fusion
  130.7 6.9 %collective-permute-done = bf16[2,2,128,256]{3,2,1,0:T(8,128)(2,1)S(1)} collective-permute-done((bf16[2,2,128,256]{3,2,1,0:T(8,128)(2,1)S(1)}, bf16[2,2,128,256]{3,2,1,0:T(8,128)(2,1)S(1)}, u32[]{:S(2)}, u32[]{:S(2)}) %collective-permute-start) | collective-permute-done | bytes 262176 | tf_op jit(solution)/shard_map/ppermute | solution.py:23
  137.7 1.1 pad_maximum_fusion.1
  138.8 3.1 %fusion = f32[512]{0:T(512)S(1)} fusion(bf16[512,4096]{1,0:T(8,128)(2,1)} %all-gather.2.cloned.1.call-done), kind=kLoop, calls=%fused_computation.4 | loop fusion | flops 6290944 | bytes 4196352 | tf_op jit(solution)/shard_map/reduce_sum | solution.py:200
  141.9 4.2 %fusion.10 = bf16[512,256]{1,0:T(8,128)(2,1)S(1)} fusion(bf16[4096,256]{1,0:T(8,128)(2,1)} %bitcast, bf16[512,4096]{1,0:T(8,128)(2,1)} %all-gather.2.cloned.1.call-done, f32[4096]{0:T(1024)S(1)} %copy-done.5, f32[512]{0:T(512)S(1)} %add_rsqrt_fusion), kind=kOutput, calls=%fused_computation.16 | convolution fusion | flops 1082392576 | bytes 6572032 | tf_op jit(solution)/shard_map/dot_general | solution.py:211
  148.4 3.2 %convolution_convert_fusion = bf16[512,4096]{1,0:T(8,128)(2,1)} fusion(bf16[256,4096]{1,0:T(8,128)(2,1)S(1)} %copy-done, bf16[576,256]{1,0:T(8,128)(2,1)S(1)} %bitcast.53, pred[512]{0:T(512)(128)(4,1)S(1)} %fusion.38), kind=kOutput, calls=%fused_computation.7 | convolution fusion | flops 1075970048 | bytes 6554112 | tf_op jit(solution)/shard_map/dot_general | solution.py:290
  151.7 50.6 %shard_map.101 = bf16[32,4096]{1,0:T(8,128)(2,1)} custom-call(bf16[16,32,4096]{2,1,0:T(8,128)(2,1)} %bitcast.40), custom_call_target="tpu_custom_call" | custom-call | tf_op jit(solution)/shard_map/pallas_call | solution.py:155
  202.3 1.7 copy.18
  (51 shorter events, 3.6 us)
Async XLA Ops:
  6.5 141.9 %copy-start = (bf16[256,4096]{1,0:T(8,128)(2,1)S(1)}, bf16[256,4096]{1,0:T(8,128)(2,1)}, u32[]{:S(2)}) copy-start(bf16[256,4096]{1,0:T(8,128)(2,1)} %param.15) | copy-start | bytes 6291460
  6.5 14.9 %copy-start.6 = (s32[256]{0:T(256)S(1)}, s32[256]{0:T(256)}, u32[]{:S(2)}) copy-start(s32[256]{0:T(256)} %param.19) | copy-start | bytes 3076
  6.5 24.4 %copy-start.2 = (bf16[128,256]{1,0:T(8,128)(2,1)S(1)}, bf16[128,256]{1,0:T(8,128)(2,1)}, u32[]{:S(2)}) copy-start(bf16[128,256]{1,0:T(8,128)(2,1)} %param.12) | copy-start | bytes 196612
  6.5 132.3 %all-gather.2.cloned.1.call-start = ((), (), s32[]{:S(2)}) async-start(), calls=%async_computation.2 | async-start | bytes 4456448 | tf_op jit(solution)/shard_map/all_gather | solution.py:198
  12.2 18.8 %all-to-all-start.1 = ((bf16[32,1,8,1024]{3,2,1,0:T(8,128)(2,1)}), bf16[32,1,8,1024]{3,2,1,0:T(8,128)(2,1)S(1)}, u32[]{:S(2)}, u32[]{:S(2)}) async-start(bf16[32,1,8,1024]{3,2,1,0:T(8,128)(2,1)} %bitcast_multiply_fusion), calls=%async_computation.1 | async-start | bytes 1048576 | tf_op jit(solution)/shard_map/all_to_all | solution.py:227
  32.5 109.4 %all-to-all-start = ((bf16[32,128,256]{2,1,0:T(8,128)(2,1)}), bf16[32,128,256]{2,1,0:T(8,128)(2,1)}, u32[]{:S(2)}, u32[]{:S(2)}) async-start(bf16[32,128,256]{2,1,0:T(8,128)(2,1)} %broadcast_in_dim.46), calls=%async_computation | async-start | bytes 4194304 | tf_op jit(solution)/shard_map/all_to_all | solution.py:204
  122.3 2.7 %copy-start.3 = (bf16[1024,256]{1,0:T(8,128)(2,1)S(1)}, bf16[1024,256]{1,0:T(8,128)(2,1)}, u32[]{:S(2)}) copy-start(bf16[1024,256]{1,0:T(8,128)(2,1)} %param.13) | copy-start | bytes 1572868
  125.1 1.3 copy-start.4
  127.8 9.8 %collective-permute-start = (bf16[2,2,128,256]{3,2,1,0:T(8,128)(2,1)S(1)}, bf16[2,2,128,256]{3,2,1,0:T(8,128)(2,1)S(1)}, u32[]{:S(2)}, u32[]{:S(2)}) collective-permute-start(bf16[2,2,128,256]{3,2,1,0:T(8,128)(2,1)S(1)} %pad_maximum_fusion.3), channel_id=1, source_target_pairs={{0,16},{16,32},{32,48},{48,64},{64,80},{80,96},{96,112},{112,128},... | collective-permute-start | bytes 786440 | tf_op jit(solution)/shard_map/ppermute | solution.py:23
  138.8 3.1 %copy-start.5 = (f32[4096]{0:T(1024)S(1)}, f32[4096]{0:T(1024)}, u32[]{:S(2)}) copy-start(f32[4096]{0:T(1024)} %param.11) | copy-start | bytes 49156
  146.1 1.4 copy-start.1
Sparse Core Ops, SparseCore 0:
  9.4 124.1 all-gather.1

commit v19 on v16

--- a/solution.py
+++ b/solution.py
@@ -290,7 +290,7 @@
     mixed_part = jnp.dot(attended, out_weight, preferred_element_type=jnp.float32).astype(
         jnp.bfloat16
     )
-    return kernel_reduce_scatter(mixed_part, "tp", "ctx", 1, pieces=8)
+    return kernel_reduce_scatter(mixed_part, "tp", "ctx", 1, pieces=2)
 
 
 def solution(mesh):

time: 211 us -> 211 us (level)
  no operation moved by 1% of the time
where the time goes in v19:
time: 211 us; the launch traced here: 210 us
  Pallas kernels  132 us (63%)
  starting transfers between devices  18.4 us (9%)
  waiting for transfers between devices  16.1 us (8%)
  between operations  13.7 us (6%)
  matrix products  11.4 us (5%)
  local copies, waits for them, and re-layouts  10.6 us (5%)
  other arithmetic  8.43 us (4%)
    pallas_call x1, Pallas kernels, kernel_gather(): pl.pallas_call(functools.partial(ring_gather_kernel, count=count, axis=ax...  80.4 us
    pallas_call x1, Pallas kernels, kernel_reduce_scatter(): pl.pallas_call(functools.partial(ring_sum_kernel, count=count, axis=axis,...  51.5 us
    all_to_all x1, starting transfers between devices, local(): lax.all_to_all(outgoing, 'ctx', split_axis=0, concat_axis=0, tiled=True)  9.29 us
    all_to_all x1, waiting for transfers between devices, local(): lax.all_to_all(outgoing, 'ctx', split_axis=0, concat_axis=0, tiled=True)  8.51 us
    all_to_all x1, starting transfers between devices, local(): lax.all_to_all(jnp.broadcast_to(query_weight[None], (ctx_count,) + query_...  6.99 us
    ppermute x1, waiting for transfers between devices, shifted(): return lax.ppermute(block, axis, route)  6.85 us
  transfers between devices with their start and end apart: 4, of which 2 were waited for; matrix products, arithmetic and copies ran while one was open for 9% of the time, Pallas kernels for 38%

profile of v19, /device:TPU:24, one launch (start us, length us, event | category | flops | bytes accessed | tf_op | source)
XLA Modules:
  0.0 210.5 jit_solution(17201125693115823821)
XLA Ops:
  6.5 0.7 all-gather.2.cloned.1.call-update
  7.3 0.8 copy.15
  8.2 0.9 select_reduce_fusion
  9.7 1.5 gather_fusion
  11.3 0.9 bitcast_multiply_fusion
  12.2 9.3 %all-to-all-start.1 = ((bf16[32,1,8,1024]{3,2,1,0:T(8,128)(2,1)}), bf16[32,1,8,1024]{3,2,1,0:T(8,128)(2,1)S(1)}, u32[]{:S(2)}, u32[]{:S(2)}) async-start(bf16[32,1,8,1024]{3,2,1,0:T(8,128)(2,1)} %bitcast_multiply_fusion), calls=%async_computation.1 | async-start | bytes 1048576 | tf_op jit(solution)/shard_map/all_to_all | solution.py:227
  21.5 0.6 dynamic_slice.10
  22.4 8.5 %all-to-all-done.1 = bf16[32,1,8,1024]{3,2,1,0:T(8,128)(2,1)S(1)} async-done(((bf16[32,1,8,1024]{3,2,1,0:T(8,128)(2,1)}), bf16[32,1,8,1024]{3,2,1,0:T(8,128)(2,1)S(1)}, u32[]{:S(2)}, u32[]{:S(2)}) %all-to-all-start.1) | async-done | bytes 524320 | tf_op jit(solution)/shard_map/all_to_all | solution.py:227
  30.9 1.5 broadcast_in_dim.46
  32.5 7.0 %all-to-all-start = ((bf16[32,128,256]{2,1,0:T(8,128)(2,1)}), bf16[32,128,256]{2,1,0:T(8,128)(2,1)}, u32[]{:S(2)}, u32[]{:S(2)}) async-start(bf16[32,128,256]{2,1,0:T(8,128)(2,1)} %broadcast_in_dim.46), calls=%async_computation | async-start | bytes 4194304 | tf_op jit(solution)/shard_map/all_to_all | solution.py:204
  39.5 1.3 gather_fusion.1
  40.7 80.4 %shard_map.100 = bf16[16,16,8,1024]{3,2,1,0:T(8,128)(2,1)} custom-call(bf16[16,8,1024]{2,1,0:T(8,128)(2,1)} %gather_fusion.1), custom_call_target="tpu_custom_call" | custom-call | tf_op jit(solution)/shard_map/pallas_call | solution.py:84
  121.1 2.7 %copy.16 = bf16[16,16,8,1024]{3,2,1,0:T(8,128)(2,1)S(1)} copy(bf16[16,16,8,1024]{3,2,0,1:T(8,128)(2,1)} %bitcast.41) | data formatting | bytes 8388608 | tf_op jit(solution)/shard_map/transpose | solution.py:237
  123.8 1.3 convolution_convert_fusion.2
  125.1 1.3 convolution_convert_fusion.1
  126.5 2.1 collective-permute-start
  128.6 0.7 pad_add_fusion
  129.4 6.9 %collective-permute-done = bf16[2,2,128,256]{3,2,1,0:T(8,128)(2,1)S(1)} collective-permute-done((bf16[2,2,128,256]{3,2,1,0:T(8,128)(2,1)S(1)}, bf16[2,2,128,256]{3,2,1,0:T(8,128)(2,1)S(1)}, u32[]{:S(2)}, u32[]{:S(2)}) %collective-permute-start) | collective-permute-done | bytes 262176 | tf_op jit(solution)/shard_map/ppermute | solution.py:23
  136.4 1.1 pad_maximum_fusion.1
  137.5 3.1 %fusion = f32[512]{0:T(512)S(1)} fusion(bf16[512,4096]{1,0:T(8,128)(2,1)} %all-gather.2.cloned.1.call-done), kind=kLoop, calls=%fused_computation.4 | loop fusion | flops 6290944 | bytes 4196352 | tf_op jit(solution)/shard_map/reduce_sum | solution.py:200
  140.7 4.2 %fusion.10 = bf16[512,256]{1,0:T(8,128)(2,1)S(1)} fusion(bf16[4096,256]{1,0:T(8,128)(2,1)} %bitcast, bf16[512,4096]{1,0:T(8,128)(2,1)} %all-gather.2.cloned.1.call-done, f32[4096]{0:T(1024)S(1)} %copy-done.5, f32[512]{0:T(512)S(1)} %add_rsqrt_fusion), kind=kOutput, calls=%fused_computation.16 | convolution fusion | flops 1082392576 | bytes 6572032 | tf_op jit(solution)/shard_map/dot_general | solution.py:211
  147.2 3.2 %convolution_convert_fusion = bf16[512,4096]{1,0:T(8,128)(2,1)} fusion(bf16[256,4096]{1,0:T(8,128)(2,1)S(1)} %copy-done, bf16[576,256]{1,0:T(8,128)(2,1)S(1)} %bitcast.53, pred[512]{0:T(512)(128)(4,1)S(1)} %fusion.38), kind=kOutput, calls=%fused_computation.7 | convolution fusion | flops 1075970048 | bytes 6554112 | tf_op jit(solution)/shard_map/dot_general | solution.py:290
  150.4 51.5 %shard_map.101 = bf16[32,4096]{1,0:T(8,128)(2,1)} custom-call(bf16[16,32,4096]{2,1,0:T(8,128)(2,1)} %bitcast.40), custom_call_target="tpu_custom_call" | custom-call | tf_op jit(solution)/shard_map/pallas_call | solution.py:155
  201.9 1.7 copy.18
  (51 shorter events, 3.6 us)
Async XLA Ops:
  6.5 140.6 %copy-start = (bf16[256,4096]{1,0:T(8,128)(2,1)S(1)}, bf16[256,4096]{1,0:T(8,128)(2,1)}, u32[]{:S(2)}) copy-start(bf16[256,4096]{1,0:T(8,128)(2,1)} %param.15) | copy-start | bytes 6291460
  6.5 14.9 %copy-start.6 = (s32[256]{0:T(256)S(1)}, s32[256]{0:T(256)}, u32[]{:S(2)}) copy-start(s32[256]{0:T(256)} %param.19) | copy-start | bytes 3076
  6.5 24.4 %copy-start.2 = (bf16[128,256]{1,0:T(8,128)(2,1)S(1)}, bf16[128,256]{1,0:T(8,128)(2,1)}, u32[]{:S(2)}) copy-start(bf16[128,256]{1,0:T(8,128)(2,1)} %param.12) | copy-start | bytes 196612
  6.5 131.0 %all-gather.2.cloned.1.call-start = ((), (), s32[]{:S(2)}) async-start(), calls=%async_computation.2 | async-start | bytes 4456448 | tf_op jit(solution)/shard_map/all_gather | solution.py:198
  12.2 18.8 %all-to-all-start.1 = ((bf16[32,1,8,1024]{3,2,1,0:T(8,128)(2,1)}), bf16[32,1,8,1024]{3,2,1,0:T(8,128)(2,1)S(1)}, u32[]{:S(2)}, u32[]{:S(2)}) async-start(bf16[32,1,8,1024]{3,2,1,0:T(8,128)(2,1)} %bitcast_multiply_fusion), calls=%async_computation.1 | async-start | bytes 1048576 | tf_op jit(solution)/shard_map/all_to_all | solution.py:227
  32.5 108.2 %all-to-all-start = ((bf16[32,128,256]{2,1,0:T(8,128)(2,1)}), bf16[32,128,256]{2,1,0:T(8,128)(2,1)}, u32[]{:S(2)}, u32[]{:S(2)}) async-start(bf16[32,128,256]{2,1,0:T(8,128)(2,1)} %broadcast_in_dim.46), calls=%async_computation | async-start | bytes 4194304 | tf_op jit(solution)/shard_map/all_to_all | solution.py:204
  121.1 2.7 %copy-start.3 = (bf16[1024,256]{1,0:T(8,128)(2,1)S(1)}, bf16[1024,256]{1,0:T(8,128)(2,1)}, u32[]{:S(2)}) copy-start(bf16[1024,256]{1,0:T(8,128)(2,1)} %param.13) | copy-start | bytes 1572868
  123.8 1.3 copy-start.4
  126.5 9.8 %collective-permute-start = (bf16[2,2,128,256]{3,2,1,0:T(8,128)(2,1)S(1)}, bf16[2,2,128,256]{3,2,1,0:T(8,128)(2,1)S(1)}, u32[]{:S(2)}, u32[]{:S(2)}) collective-permute-start(bf16[2,2,128,256]{3,2,1,0:T(8,128)(2,1)S(1)} %pad_maximum_fusion.3), channel_id=1, source_target_pairs={{0,16},{16,32},{32,48},{48,64},{64,80},{80,96},{96,112},{112,128},... | collective-permute-start | bytes 786440 | tf_op jit(solution)/shard_map/ppermute | solution.py:23
  137.5 3.1 %copy-start.5 = (f32[4096]{0:T(1024)S(1)}, f32[4096]{0:T(1024)}, u32[]{:S(2)}) copy-start(f32[4096]{0:T(1024)} %param.11) | copy-start | bytes 49156
  144.8 1.4 copy-start.1
Sparse Core Ops, SparseCore 0:
  9.4 123.5 all-gather.1

commit v20 on v12

--- a/solution.py
+++ b/solution.py
@@ -220,10 +220,8 @@
     rank_position = jnp.cumsum(from_here.astype(jnp.int32), axis=1) - 1
     picked_rows = from_here & (rank_position == 0)
     pick_list = [jnp.sum(jnp.where(picked_rows, local_rows, 0), axis=1)]
-    fill_list = [jnp.any(picked_rows, axis=1)]
     pick_index = jnp.stack(pick_list, axis=1)
-    fill_mask = jnp.stack(fill_list, axis=1)
-    outgoing = encodings[pick_index] * fill_mask[:, :, None, None].astype(jnp.bfloat16)
+    outgoing = encodings[pick_index]
     incoming = lax.all_to_all(outgoing, "ctx", split_axis=0, concat_axis=0, tiled=True)
     own_sources = lax.dynamic_index_in_dim(sources, ctx_index, 0, keepdims=False)
     slot_order = jnp.arange(rows_dev)

time: 210 us -> 210 us (level)
  transfers between devices with their start and end apart: 4 -> 4, of which waited for: 2 -> 2; matrix products, arithmetic and copies ran while one was open for 9% -> 9% of each run, Pallas kernels for 38% -> 39%
where the time goes in v20:
time: 210 us; the launch traced here: 209 us
  Pallas kernels  131 us (62%)
  starting transfers between devices  18.4 us (9%)
  waiting for transfers between devices  16.1 us (8%)
  between operations  13.7 us (7%)
  local copies, waits for them, and re-layouts  11.4 us (5%)
  matrix products  11.4 us (5%)
  other arithmetic  7.4 us (4%)
    pallas_call x1, Pallas kernels, kernel_gather(): pl.pallas_call(functools.partial(ring_gather_kernel, count=count, axis=ax...  80.6 us
    pallas_call x1, Pallas kernels, kernel_reduce_scatter(): pl.pallas_call(functools.partial(ring_sum_kernel, count=count, axis=axis,...  50.2 us
    all_to_all x1, starting transfers between devices, local(): lax.all_to_all(outgoing, 'ctx', split_axis=0, concat_axis=0, tiled=True)  9.3 us
    all_to_all x1, waiting for transfers between devices, local(): lax.all_to_all(outgoing, 'ctx', split_axis=0, concat_axis=0, tiled=True)  8.51 us
    all_to_all x1, starting transfers between devices, local(): lax.all_to_all(jnp.broadcast_to(query_weight[None], (ctx_count,) + query_...  7 us
    ppermute x1, waiting for transfers between devices, shifted(): return lax.ppermute(block, axis, route)  6.85 us
  transfers between devices with their start and end apart: 4, of which 2 were waited for; matrix products, arithmetic and copies ran while one was open for 9% of the time, Pallas kernels for 39%

profile of v20, /device:TPU:24, one launch (start us, length us, event | category | flops | bytes accessed | tf_op | source)
XLA Modules:
  0.0 209.1 jit_solution(10878932258030259812)
XLA Ops:
  6.5 0.7 all-gather.2.cloned.1.call-update
  7.3 0.8 copy.15
  8.2 0.9 select_reduce_fusion
  9.6 2.3 %gather_fusion = bf16[32,8,1024]{2,1,0:T(8,128)(2,1)} fusion(bf16[16,8,1024]{2,1,0:T(8,128)(2,1)} %param.16, s32[1024]{0:T(1024)S(1)} %pad_clamp_fusion.1), kind=kCustom, calls=%fused_computation | custom fusion | bytes 1048704 | tf_op jit(solution)/shard_map/gather | solution.py:224
  11.9 9.3 %all-to-all-start.1 = ((bf16[32,1,8,1024]{3,2,1,0:T(8,128)(2,1)}), bf16[32,1,8,1024]{3,2,1,0:T(8,128)(2,1)S(1)}, u32[]{:S(2)}, u32[]{:S(2)}) async-start(bf16[32,1,8,1024]{3,2,1,0:T(8,128)(2,1)} %bitcast.4), calls=%async_computation.1 | async-start | bytes 1048576 | tf_op jit(solution)/shard_map/all_to_all | solution.py:225
  21.2 0.6 dynamic_slice.10
  22.2 8.5 %all-to-all-done.1 = bf16[32,1,8,1024]{3,2,1,0:T(8,128)(2,1)S(1)} async-done(((bf16[32,1,8,1024]{3,2,1,0:T(8,128)(2,1)}), bf16[32,1,8,1024]{3,2,1,0:T(8,128)(2,1)S(1)}, u32[]{:S(2)}, u32[]{:S(2)}) %all-to-all-start.1) | async-done | bytes 524320 | tf_op jit(solution)/shard_map/all_to_all | solution.py:225
  30.7 1.5 broadcast_in_dim.46
  32.2 7.0 %all-to-all-start = ((bf16[32,128,256]{2,1,0:T(8,128)(2,1)}), bf16[32,128,256]{2,1,0:T(8,128)(2,1)}, u32[]{:S(2)}, u32[]{:S(2)}) async-start(bf16[32,128,256]{2,1,0:T(8,128)(2,1)} %broadcast_in_dim.46), calls=%async_computation | async-start | bytes 4194304 | tf_op jit(solution)/shard_map/all_to_all | solution.py:204
  39.2 1.3 gather_fusion.1
  40.5 80.6 %shard_map.100 = bf16[16,16,8,1024]{3,2,1,0:T(8,128)(2,1)} custom-call(bf16[16,8,1024]{2,1,0:T(8,128)(2,1)} %gather_fusion.1), custom_call_target="tpu_custom_call" | custom-call | tf_op jit(solution)/shard_map/pallas_call | solution.py:84
  121.1 2.7 %copy.16 = bf16[16,16,8,1024]{3,2,1,0:T(8,128)(2,1)S(1)} copy(bf16[16,16,8,1024]{3,2,0,1:T(8,128)(2,1)} %bitcast.40) | data formatting | bytes 8388608 | tf_op jit(solution)/shard_map/transpose | solution.py:235
  123.8 1.3 convolution_convert_fusion.2
  125.1 1.3 convolution_convert_fusion.1
  126.5 2.1 %collective-permute-start = (bf16[2,2,128,256]{3,2,1,0:T(8,128)(2,1)S(1)}, bf16[2,2,128,256]{3,2,1,0:T(8,128)(2,1)S(1)}, u32[]{:S(2)}, u32[]{:S(2)}) collective-permute-start(bf16[2,2,128,256]{3,2,1,0:T(8,128)(2,1)S(1)} %pad_maximum_fusion.3), channel_id=1, source_target_pairs={{0,16},{16,32},{32,48},{48,64},{64,80},{80,96},{96,112},{112,128},... | collective-permute-start | bytes 786440 | tf_op jit(solution)/shard_map/ppermute | solution.py:23
  128.6 0.7 pad_add_fusion
  129.4 6.9 %collective-permute-done = bf16[2,2,128,256]{3,2,1,0:T(8,128)(2,1)S(1)} collective-permute-done((bf16[2,2,128,256]{3,2,1,0:T(8,128)(2,1)S(1)}, bf16[2,2,128,256]{3,2,1,0:T(8,128)(2,1)S(1)}, u32[]{:S(2)}, u32[]{:S(2)}) %collective-permute-start) | collective-permute-done | bytes 262176 | tf_op jit(solution)/shard_map/ppermute | solution.py:23
  136.4 1.1 pad_maximum_fusion.1
  137.5 3.1 %fusion = f32[512]{0:T(512)S(1)} fusion(bf16[512,4096]{1,0:T(8,128)(2,1)} %all-gather.2.cloned.1.call-done), kind=kLoop, calls=%fused_computation.4 | loop fusion | flops 6290944 | bytes 4196352 | tf_op jit(solution)/shard_map/reduce_sum | solution.py:200
  140.7 4.2 %fusion.10 = bf16[512,256]{1,0:T(8,128)(2,1)S(1)} fusion(bf16[4096,256]{1,0:T(8,128)(2,1)} %bitcast, bf16[512,4096]{1,0:T(8,128)(2,1)} %all-gather.2.cloned.1.call-done, f32[4096]{0:T(1024)S(1)} %copy-done.5, f32[512]{0:T(512)S(1)} %add_rsqrt_fusion), kind=kOutput, calls=%fused_computation.16 | convolution fusion | flops 1082392576 | bytes 6572032 | tf_op jit(solution)/shard_map/dot_general | solution.py:211
  145.5 0.4 fusion.45
  147.2 3.2 %convolution_convert_fusion = bf16[512,4096]{1,0:T(8,128)(2,1)} fusion(bf16[256,4096]{1,0:T(8,128)(2,1)S(1)} %copy-done, bf16[576,256]{1,0:T(8,128)(2,1)S(1)} %bitcast.52, pred[512]{0:T(512)(128)(4,1)S(1)} %fusion.38), kind=kOutput, calls=%fused_computation.7 | convolution fusion | flops 1075970048 | bytes 6554112 | tf_op jit(solution)/shard_map/dot_general | solution.py:288
  150.4 50.2 %shard_map.101 = bf16[32,4096]{1,0:T(8,128)(2,1)} custom-call(bf16[16,32,4096]{2,1,0:T(8,128)(2,1)} %bitcast.39), custom_call_target="tpu_custom_call" | custom-call | tf_op jit(solution)/shard_map/pallas_call | solution.py:155
  200.6 1.7 copy.18
  (48 shorter events, 3.1 us)
Async XLA Ops:
  6.5 140.6 %copy-start = (bf16[256,4096]{1,0:T(8,128)(2,1)S(1)}, bf16[256,4096]{1,0:T(8,128)(2,1)}, u32[]{:S(2)}) copy-start(bf16[256,4096]{1,0:T(8,128)(2,1)} %param.15) | copy-start | bytes 6291460
  6.5 14.7 %copy-start.6 = (s32[256]{0:T(256)S(1)}, s32[256]{0:T(256)}, u32[]{:S(2)}) copy-start(s32[256]{0:T(256)} %param.19) | copy-start | bytes 3076
  6.5 24.2 %copy-start.2 = (bf16[128,256]{1,0:T(8,128)(2,1)S(1)}, bf16[128,256]{1,0:T(8,128)(2,1)}, u32[]{:S(2)}) copy-start(bf16[128,256]{1,0:T(8,128)(2,1)} %param.12) | copy-start | bytes 196612
  6.5 131.0 %all-gather.2.cloned.1.call-start = ((), (), s32[]{:S(2)}) async-start(), calls=%async_computation.2 | async-start | bytes 4456448 | tf_op jit(solution)/shard_map/all_gather | solution.py:198
  11.9 18.8 %all-to-all-start.1 = ((bf16[32,1,8,1024]{3,2,1,0:T(8,128)(2,1)}), bf16[32,1,8,1024]{3,2,1,0:T(8,128)(2,1)S(1)}, u32[]{:S(2)}, u32[]{:S(2)}) async-start(bf16[32,1,8,1024]{3,2,1,0:T(8,128)(2,1)} %bitcast.4), calls=%async_computation.1 | async-start | bytes 1048576 | tf_op jit(solution)/shard_map/all_to_all | solution.py:225
  32.2 108.4 %all-to-all-start = ((bf16[32,128,256]{2,1,0:T(8,128)(2,1)}), bf16[32,128,256]{2,1,0:T(8,128)(2,1)}, u32[]{:S(2)}, u32[]{:S(2)}) async-start(bf16[32,128,256]{2,1,0:T(8,128)(2,1)} %broadcast_in_dim.46), calls=%async_computation | async-start | bytes 4194304 | tf_op jit(solution)/shard_map/all_to_all | solution.py:204
  121.1 2.7 %copy-start.3 = (bf16[1024,256]{1,0:T(8,128)(2,1)S(1)}, bf16[1024,256]{1,0:T(8,128)(2,1)}, u32[]{:S(2)}) copy-start(bf16[1024,256]{1,0:T(8,128)(2,1)} %param.13) | copy-start | bytes 1572868
  123.8 1.3 copy-start.4
  126.5 9.8 %collective-permute-start = (bf16[2,2,128,256]{3,2,1,0:T(8,128)(2,1)S(1)}, bf16[2,2,128,256]{3,2,1,0:T(8,128)(2,1)S(1)}, u32[]{:S(2)}, u32[]{:S(2)}) collective-permute-start(bf16[2,2,128,256]{3,2,1,0:T(8,128)(2,1)S(1)} %pad_maximum_fusion.3), channel_id=1, source_target_pairs={{0,16},{16,32},{32,48},{48,64},{64,80},{80,96},{96,112},{112,128},... | collective-permute-start | bytes 786440 | tf_op jit(solution)/shard_map/ppermute | solution.py:23
  137.5 3.1 %copy-start.5 = (f32[4096]{0:T(1024)S(1)}, f32[4096]{0:T(1024)}, u32[]{:S(2)}) copy-start(f32[4096]{0:T(1024)} %param.11) | copy-start | bytes 49156
  144.8 1.4 copy-start.1
Sparse Core Ops, SparseCore 0:
  9.4 123.5 all-gather.1
